TPU v7x, 512 devices: a whole 4x8x8 slice. The times are simulated.
512 devices in a mesh: dp: 64 (over z, y_hi, core), mp: 8 (over y_lo, x).
Axes of the slice: x: 4, y: 8 (y_hi: 4, y_lo: 2; y = y_hi * 2 + y_lo), z: 8, core: 2. Of those that a mesh axis runs over, the one named last changes fastest.
Arguments:
- views: bfloat16 [32768, 256], P('dp'), may hold values from -1 to 1
- partner: int32 [32768], P('dp'), may hold values from 0 to 32767, as said below
- weight: float32 [32768], P('dp'), may hold values from 0.25 to 4
Outputs:
- loss: float32 [32768], P('dp')
- grad: float32 [32768, 256], P('dp')
Inputs may be any that keep to these rules, and one draw needn't show every extreme that they name: partner pairs the views: partner[partner[i]] = i and partner[i] != i.
All inputs are finite; a program needn't handle non-finite values.
Results may differ from a plain program's by a relative error of at most 0.0056.
Values may be sent and summed in bfloat16 or wider, within the bound.
No kernel may reach another device: no remote copies, remote signals or barrier semaphores. Data moves between devices by JAX's collectives and lax.ppermute only.
A program may use at most 64 MiB of HBM per device.

v0:
```python
import jax
import jax.numpy as jnp
from jax import lax
from jax.sharding import Mesh
from jax.sharding import PartitionSpec as P

DP = ("dp_0", "dp_1", "dp_2")


INV_TAU = 10.0
EPS = 1e-06


def sent_to_all(shard, axis):
    count = lax.axis_size(axis)
    return lax.all_to_all(
        jnp.broadcast_to(shard[None], (count, *shard.shape)), axis, 0, 0, tiled=True
    )


def joined_along(parts, dim):
    parts = jnp.moveaxis(parts, 0, dim)
    shape = parts.shape
    return parts.reshape(*shape[:dim], shape[dim] * shape[dim + 1], *shape[dim + 2 :])


def gathered_by_axis(shard, axes, dim):
    far, near = axes
    leading = sent_to_all(shard, far)
    parts = jnp.swapaxes(sent_to_all(leading, near), 0, 1)
    return joined_along(parts.reshape(-1, *shard.shape), dim)


def of_everyone(shard, axis):
    everything = sent_to_all(shard, axis)
    return jnp.sum(everything, axis=0)


def together(arrays, axis):
    vector, at, finished = (jnp.concatenate([a.reshape(-1) for a in arrays]), 0, [])
    subtotal = of_everyone(vector, axis)
    for a in arrays:
        finished.append(subtotal[at : at + a.size].reshape(a.shape))
        at += a.size
    return tuple(finished)


def turned_gather(arrays, axis, dims):
    turned = [jnp.moveaxis(a, dim, 0) for a, dim in zip(arrays, dims)]
    widths = [t[0].size for t in turned]
    both = jnp.concatenate([t.reshape(-1, w) for t, w in zip(turned, widths)], axis=1)
    whole = lax.all_gather(both, axis, axis=0, tiled=True)
    parts = jnp.split(whole, [sum(widths[:k]) for k in range(1, len(widths))], axis=1)
    return tuple(
        (
            jnp.moveaxis(b.reshape(-1, *t.shape[1:]), 0, dim)
            for b, t, dim in zip(parts, turned, dims)
        )
    )


def cut_along(shard, dim, count):
    shape = shard.shape
    parts = shard.reshape(*shape[:dim], count, shape[dim] // count, *shape[dim + 1 :])
    return jnp.moveaxis(parts, dim, 0)


def sent_and_summed(shard, axis, dim):
    parts = cut_along(shard, dim, lax.axis_size(axis))
    arrived = lax.all_to_all(parts, axis, split_axis=0, concat_axis=0, tiled=True)
    return arrived.sum(axis=0)


def gather_directly(shard, axis, dim):
    parts = sent_to_all(shard, axis)
    return joined_along(parts, dim)


def shards(views, partner, weight):
    rows_dev = views.shape[0]
    width = views.shape[1]
    parts = lax.axis_size("mp")
    slot = lax.axis_index("mp")
    block_index = lax.axis_index(DP)
    piece = rows_dev // parts
    floats = views.astype(jnp.float32)
    length = jnp.sqrt(jnp.sum(floats * floats, axis=1) + EPS)
    unit = floats / length[:, None]
    normal = unit.astype(jnp.bfloat16)
    offset = slot * piece
    mine = lax.dynamic_slice_in_dim(normal, offset, piece, 0)
    columns = gathered_by_axis(mine, (("dp_0", "dp_1"), "dp_2"), 0)
    width_cols = columns.shape[0]
    step_cols = min(512, width_cols)
    count = width_cols // step_cols
    position = jnp.arange(width_cols, dtype=jnp.int32)
    col_ids = position // piece * rows_dev + offset + position % piece
    row_ids = block_index * rows_dev + jnp.arange(rows_dev, dtype=jnp.int32)
    id_blocks = col_ids.reshape(count, step_cols)

    def tile(cols_block, ids_block):
        s = (
            lax.dot_general(
                normal, cols_block, (((1,), (1,)), ((), ())), preferred_element_type=jnp.float32
            )
            * INV_TAU
        )
        off = row_ids[:, None] != ids_block[None, :]
        match = partner[:, None] == ids_block[None, :]
        return (s, off, match)

    def forward(carry, inputs):
        cols_block, ids_block = inputs
        s, off, match = tile(cols_block, ids_block)
        total = carry[0] + jnp.sum(jnp.where(off, jnp.exp(s), jnp.float32(0.0)), axis=1)
        positive = carry[1] + jnp.sum(jnp.where(match, s, jnp.float32(0.0)), axis=1)
        return ((total, positive), None)

    zeros_rows = jnp.zeros((rows_dev,), jnp.float32)
    col_blocks = columns.reshape(count, step_cols, width)
    (total, positive), _ = lax.scan(forward, (zeros_rows, zeros_rows), (col_blocks, id_blocks))
    total, positive = together((total, positive), "mp")
    lse = jnp.log(total)
    loss = lse - positive
    lse_mine = lax.dynamic_slice_in_dim(lse, offset, piece, 0)
    weight_mine = lax.dynamic_slice_in_dim(weight, offset, piece, 0)
    col_lse, col_weight = turned_gather((lse_mine, weight_mine), DP, (0, 0))

    def backward(acc, inputs):
        cols_block, ids_block, lse_block, weight_block = inputs
        s, off, match = tile(cols_block, ids_block)
        prow = jnp.exp(s - lse[:, None])
        pcol = jnp.exp(s - lse_block[None, :])
        coef = jnp.where(
            off, weight[:, None] * prow + weight_block[None, :] * pcol, jnp.float32(0.0)
        )
        coef = coef - jnp.where(match, weight[:, None] + weight_block[None, :], jnp.float32(0.0))
        coef = coef.astype(jnp.bfloat16)
        return (acc + jnp.dot(coef, cols_block, preferred_element_type=jnp.float32), None)

    start_acc = jnp.zeros((rows_dev, width), jnp.float32)
    partial_grad, _ = lax.scan(
        backward,
        start_acc,
        (
            col_blocks,
            id_blocks,
            col_lse.reshape(count, step_cols),
            col_weight.reshape(count, step_cols),
        ),
    )
    share = sent_and_summed(partial_grad, "mp", 0) * INV_TAU
    unit_share = lax.dynamic_slice_in_dim(unit, offset, piece, 0)
    length_share = lax.dynamic_slice_in_dim(length, offset, piece, 0)
    finished = (
        share - unit_share * jnp.sum(unit_share * share, axis=1, keepdims=True)
    ) / length_share[:, None]
    grad = gather_directly(finished, "mp", 0)
    return (loss, grad)


def solution(mesh):
    finer = Mesh(mesh.devices.reshape(8, 4, 2, mesh.shape["mp"]), ("dp_0", "dp_1", "dp_2", "mp"))
    placed = (P(DP, None), P(DP), P(DP))
    return jax.shard_map(
        shards, mesh=finer, in_specs=placed, out_specs=(P(DP), P(DP, None)), check_vma=False
    )
```

profile of v0, /device:TPU:1, one launch (start us, length us, event | category | flops | bytes accessed | tf_op | source)
XLA Modules:
  0.0 204.9 jit_solution(12894335910544377624)
XLA Ops:
  0.6 1.1 fusion.31
  1.7 1.1 convert_divide_fusion
  2.9 1.1 broadcast_in_dim.26
  4.0 16.5 %all-to-all-start = ((bf16[32,64,256]{2,1,0:T(8,128)(2,1)}), bf16[32,64,256]{2,1,0:T(8,128)(2,1)S(1)}, u32[]{:S(2)}, u32[]{:S(2)}) async-start(bf16[32,64,256]{2,1,0:T(8,128)(2,1)} %broadcast_in_dim.26), calls=%async_computation | async-start | bytes 2097152 | tf_op jit(solution)/shard_map/all_to_all | solution.py:16
  20.6 31.4 %all-to-all-done = bf16[32,64,256]{2,1,0:T(8,128)(2,1)S(1)} async-done(((bf16[32,64,256]{2,1,0:T(8,128)(2,1)}), bf16[32,64,256]{2,1,0:T(8,128)(2,1)S(1)}, u32[]{:S(2)}, u32[]{:S(2)}) %all-to-all-start) | async-done | bytes 1048608 | tf_op jit(solution)/shard_map/all_to_all | solution.py:16
  52.2 8.1 %all_to_all.26 = bf16[2,32,64,256]{3,2,1,0:T(8,128)(2,1)S(1)} all-to-all(bf16[2,32,64,256]{3,2,1,0:T(8,128)(2,1)S(1)} %broadcast_in_dim.27), channel_id=1, replica_groups=mesh['dp_0'=8,'dp_1'=4,'dp_2'=2,'mp'=8] {'dp_2'}, dimensions={0} | all-to-all | bytes 4194304 | tf_op jit(solution)/shard_map/all_to_all | solution.py:16
  60.4 0.5 copy-done
  61.0 4.7 %while.24 = (s32[]{:T(128)}, f32[512]{0:T(512)S(1)}, f32[512]{0:T(512)S(1)}, s32[8,512]{1,0:T(8,128)S(1)}, bf16[8,512,256]{2,1,0:T(8,128)(2,1)S(1)}, /*index=5*/...) while((s32[]{:T(128)}, f32[512]{0:T(512)S(1)}, ...), condition=%wide.region_4.5_spmd.clone, body=%wide.region_1.4_spmd.clone.sunk | while | flops 136054272 | bytes 553083 | solution.py:121
  61.0 0.5 select_reduce_fusion.3
  61.6 0.5 select_reduce_fusion.3
  62.2 0.5 select_reduce_fusion.3
  62.8 0.5 select_reduce_fusion.3
  63.3 0.5 select_reduce_fusion.3
  64.5 0.5 select_reduce_fusion.3
  65.7 0.6 broadcast_in_dim.28
  66.3 4.0 %all-to-all-start.2 = ((f32[8,1,1024]{2,1,0:T(1,128)}), f32[8,1,1024]{2,1,0:T(1,128)S(1)}, u32[]{:S(2)}, u32[]{:S(2)}) async-start(f32[8,1,1024]{2,1,0:T(1,128)} %broadcast_in_dim.28), calls=%async_computation.2 | async-start | bytes 65536 | tf_op jit(solution)/shard_map/all_to_all | solution.py:16
  70.4 5.0 %all-to-all-done.2 = f32[8,1,1024]{2,1,0:T(1,128)S(1)} async-done(((f32[8,1,1024]{2,1,0:T(1,128)}), f32[8,1,1024]{2,1,0:T(1,128)S(1)}, u32[]{:S(2)}, u32[]{:S(2)}) %all-to-all-start.2) | async-done | bytes 32800 | tf_op jit(solution)/shard_map/all_to_all | solution.py:16
  75.5 0.6 slice_log_fusion
  76.1 80.5 %all-gather = f32[64,64,2]{1,2,0:T(2,128)S(1)} all-gather(f32[1,64,2]{1,2,0:T(2,128)S(1)} %maximum_bitcast_fusion), channel_id=1, replica_groups=mesh['dp_0'=8,'dp_1'=4,'dp_2'=2,'mp'=8] {'dp_0','dp_1','dp_2'}, dimensions={0}, use_global_device_ids=true | all-gather | bytes 33280 | tf_op jit(solution)/shard_map/all_gather | solution.py:52
  156.9 22.0 %while.25 = (s32[]{:T(128)}, f32[512,256]{1,0:T(8,128)}, s32[8,512]{1,0:T(8,128)S(1)}, f32[512]{0:T(512)S(1)}, bf16[8,512,256]{2,1,0:T(8,128)(2,1)S(1)}, /*index...) while((s32[]{:T(128)}, f32[512,256]{1,0:T(8,128)}, ...), condition=%wide.region_7.8_spmd.clone, body=%wide.region_6.7_spmd.clone.sunk | while | flops 272105984 | bytes 1868947 | solution.py:142
  156.9 1.8 convolution_add_fusion.2
  158.8 2.8 %convolution_add_fusion.2 = f32[512,256]{1,0:T(8,128)} fusion(bf16[512,256]{1,0:T(8,128)(2,1)S(1)} %get-tuple-element.413, f32[512,256]{1,0:T(8,128)} %get-tuple-element.396, f32[512]{0:T(512)S(1)} %bitcast.61, f32[512]{0:T(512)S(1)} %get-tuple-element.411, s32[512]{0:T(512)S(1)} %get-tuple-element.417, f32[512]{0:T(512)S(1)} %bitcast.60, ...), kind=kOutput, calls=%fused_computation.14.clone.1 | convolution fusion | flops 272105472 | bytes 1854465 | tf_op jit(solution)/shard_map/while/body/eval_jaxpr/dot_general | solution.py:139
  161.7 2.8 %convolution_add_fusion.2 = f32[512,256]{1,0:T(8,128)} fusion(bf16[512,256]{1,0:T(8,128)(2,1)S(1)} %get-tuple-element.413, f32[512,256]{1,0:T(8,128)} %get-tuple-element.396, f32[512]{0:T(512)S(1)} %bitcast.61, f32[512]{0:T(512)S(1)} %get-tuple-element.411, s32[512]{0:T(512)S(1)} %get-tuple-element.417, f32[512]{0:T(512)S(1)} %bitcast.60, ...), kind=kOutput, calls=%fused_computation.14.clone.1 | convolution fusion | flops 272105472 | bytes 1854465 | tf_op jit(solution)/shard_map/while/body/eval_jaxpr/dot_general | solution.py:139
  164.5 2.8 %convolution_add_fusion.2 = f32[512,256]{1,0:T(8,128)} fusion(bf16[512,256]{1,0:T(8,128)(2,1)S(1)} %get-tuple-element.413, f32[512,256]{1,0:T(8,128)} %get-tuple-element.396, f32[512]{0:T(512)S(1)} %bitcast.61, f32[512]{0:T(512)S(1)} %get-tuple-element.411, s32[512]{0:T(512)S(1)} %get-tuple-element.417, f32[512]{0:T(512)S(1)} %bitcast.60, ...), kind=kOutput, calls=%fused_computation.14.clone.1 | convolution fusion | flops 272105472 | bytes 1854465 | tf_op jit(solution)/shard_map/while/body/eval_jaxpr/dot_general | solution.py:139
  167.4 2.8 %convolution_add_fusion.2 = f32[512,256]{1,0:T(8,128)} fusion(bf16[512,256]{1,0:T(8,128)(2,1)S(1)} %get-tuple-element.413, f32[512,256]{1,0:T(8,128)} %get-tuple-element.396, f32[512]{0:T(512)S(1)} %bitcast.61, f32[512]{0:T(512)S(1)} %get-tuple-element.411, s32[512]{0:T(512)S(1)} %get-tuple-element.417, f32[512]{0:T(512)S(1)} %bitcast.60, ...), kind=kOutput, calls=%fused_computation.14.clone.1 | convolution fusion | flops 272105472 | bytes 1854465 | tf_op jit(solution)/shard_map/while/body/eval_jaxpr/dot_general | solution.py:139
  170.3 2.8 %convolution_add_fusion.2 = f32[512,256]{1,0:T(8,128)} fusion(bf16[512,256]{1,0:T(8,128)(2,1)S(1)} %get-tuple-element.413, f32[512,256]{1,0:T(8,128)} %get-tuple-element.396, f32[512]{0:T(512)S(1)} %bitcast.61, f32[512]{0:T(512)S(1)} %get-tuple-element.411, s32[512]{0:T(512)S(1)} %get-tuple-element.417, f32[512]{0:T(512)S(1)} %bitcast.60, ...), kind=kOutput, calls=%fused_computation.14.clone.1 | convolution fusion | flops 272105472 | bytes 1854465 | tf_op jit(solution)/shard_map/while/body/eval_jaxpr/dot_general | solution.py:139
  173.2 2.8 %convolution_add_fusion.2 = f32[512,256]{1,0:T(8,128)} fusion(bf16[512,256]{1,0:T(8,128)(2,1)S(1)} %get-tuple-element.413, f32[512,256]{1,0:T(8,128)} %get-tuple-element.396, f32[512]{0:T(512)S(1)} %bitcast.61, f32[512]{0:T(512)S(1)} %get-tuple-element.411, s32[512]{0:T(512)S(1)} %get-tuple-element.417, f32[512]{0:T(512)S(1)} %bitcast.60, ...), kind=kOutput, calls=%fused_computation.14.clone.1 | convolution fusion | flops 272105472 | bytes 1854465 | tf_op jit(solution)/shard_map/while/body/eval_jaxpr/dot_general | solution.py:139
  176.0 2.8 %convolution_add_fusion.2 = f32[512,256]{1,0:T(8,128)} fusion(bf16[512,256]{1,0:T(8,128)(2,1)S(1)} %get-tuple-element.413, f32[512,256]{1,0:T(8,128)} %get-tuple-element.396, f32[512]{0:T(512)S(1)} %bitcast.61, f32[512]{0:T(512)S(1)} %get-tuple-element.411, s32[512]{0:T(512)S(1)} %get-tuple-element.417, f32[512]{0:T(512)S(1)} %bitcast.60, ...), kind=kOutput, calls=%fused_computation.14.clone.1 | convolution fusion | flops 272105472 | bytes 1854465 | tf_op jit(solution)/shard_map/while/body/eval_jaxpr/dot_general | solution.py:139
  178.9 3.5 %all-to-all-start.3 = ((f32[8,64,256]{2,1,0:T(8,128)}), f32[8,64,256]{2,1,0:T(8,128)S(1)}, u32[]{:S(2)}, u32[]{:S(2)}) async-start(f32[8,64,256]{2,1,0:T(8,128)} %bitcast.6), calls=%async_computation.3 | async-start | bytes 1048576 | tf_op jit(solution)/shard_map/all_to_all | solution.py:70
  182.4 8.5 %all-to-all-done.3 = f32[8,64,256]{2,1,0:T(8,128)S(1)} async-done(((f32[8,64,256]{2,1,0:T(8,128)}), f32[8,64,256]{2,1,0:T(8,128)S(1)}, u32[]{:S(2)}, u32[]{:S(2)}) %all-to-all-start.3) | async-done | bytes 524320 | tf_op jit(solution)/shard_map/all_to_all | solution.py:70
  191.3 12.9 %all_to_all.27 = f32[8,64,256]{2,1,0:T(8,128)S(1)} all-to-all(f32[8,64,256]{2,1,0:T(8,128)S(1)} %broadcast_in_dim.30), channel_id=1, replica_groups=mesh['dp_0'=8,'dp_1'=4,'dp_2'=2,'mp'=8] {'mp'}, dimensions={0} | all-to-all | bytes 1048576 | tf_op jit(solution)/shard_map/all_to_all | solution.py:16
  204.1 0.8 copy.33
  (76 shorter events, 2.7 us)
Async XLA Ops:
  4.0 48.0 %all-to-all-start = ((bf16[32,64,256]{2,1,0:T(8,128)(2,1)}), bf16[32,64,256]{2,1,0:T(8,128)(2,1)S(1)}, u32[]{:S(2)}, u32[]{:S(2)}) async-start(bf16[32,64,256]{2,1,0:T(8,128)(2,1)} %broadcast_in_dim.26), calls=%async_computation | async-start | bytes 2097152 | tf_op jit(solution)/shard_map/all_to_all | solution.py:16
  60.3 0.7 copy-start
  61.0 9.4 %copy-start.1 = (f32[512]{0:T(512)S(1)}, f32[512]{0:T(512)}, u32[]{:S(2)}) copy-start(f32[512]{0:T(512)} %param.9) | copy-start | bytes 6148
  66.3 9.1 %all-to-all-start.2 = ((f32[8,1,1024]{2,1,0:T(1,128)}), f32[8,1,1024]{2,1,0:T(1,128)S(1)}, u32[]{:S(2)}, u32[]{:S(2)}) async-start(f32[8,1,1024]{2,1,0:T(1,128)} %broadcast_in_dim.28), calls=%async_computation.2 | async-start | bytes 65536 | tf_op jit(solution)/shard_map/all_to_all | solution.py:16
  178.9 12.1 %all-to-all-start.3 = ((f32[8,64,256]{2,1,0:T(8,128)}), f32[8,64,256]{2,1,0:T(8,128)S(1)}, u32[]{:S(2)}, u32[]{:S(2)}) async-start(f32[8,64,256]{2,1,0:T(8,128)} %bitcast.6), calls=%async_computation.3 | async-start | bytes 1048576 | tf_op jit(solution)/shard_map/all_to_all | solution.py:70
where the time goes:
time: 206 us; the launch traced here: 205 us
  blocking collectives  101 us (49%)
  waiting for transfers between devices  44.9 us (22%)
  matrix products  25.8 us (13%)
  starting transfers between devices  24 us (12%)
  local copies, waits for them, and re-layouts  4.12 us (2%)
  other arithmetic  3.33 us (2%)
    all_gather x1, blocking collectives, turned_gather(): whole = lax.all_gather(both, axis, axis=0, tiled=True)  80.5 us
    all_to_all x2, waiting for transfers between devices, sent_to_all(): lax.all_to_all(jnp.broadcast_to(shard[None], (count, *shard.shape)), axis...  36.4 us
    dot_general x8, matrix products, backward(): jnp.dot(coef, cols_block, preferred_element_type=jnp.float32)  21.6 us
    all_to_all x2, blocking collectives, sent_to_all(): lax.all_to_all(jnp.broadcast_to(shard[None], (count, *shard.shape)), axis...  21 us
    all_to_all x2, starting transfers between devices, sent_to_all(): lax.all_to_all(jnp.broadcast_to(shard[None], (count, *shard.shape)), axis...  20.5 us
    all_to_all x1, waiting for transfers between devices, sent_and_summed(): lax.all_to_all(parts, axis, split_axis=0, concat_axis=0, tiled=True)  8.51 us
    dot_general x8, matrix products, tile(): lax.dot_general(normal, cols_block, (((1,), (1,)), ((), ())), preferred_e...  4.18 us
  transfers between devices with their start and end apart: 3, of which 3 were waited for; matrix products, arithmetic and copies ran while one was open for 0% of the time, Pallas kernels for 0%

commit v1 on v0

v1 whole, which is shorter than its diff:
```python
import functools

import jax
import jax.numpy as jnp
from jax import lax
from jax.experimental import pallas as pl
from jax.experimental.pallas import tpu as pltpu
from jax.sharding import Mesh
from jax.sharding import PartitionSpec as P

INV_TAU = 10.0
EPS = 1e-06
LOG2E = 1.4426950408889634

DP = ("zh", "zl", "yh", "core")
MP = ("yl", "x")
FAR = ("yh", "zh")
TEAM = ("zl", "yl", "x")
OWNERS = ("core", "yh", "zh")

NT = (((1,), (1,)), ((), ()))


def swap(x, axis):
    return lax.ppermute(x, axis, [(0, 1), (1, 0)])


def exchange(x, axes):
    return lax.all_to_all(x, axes, 0, 0, tiled=True)


def scaled(x):
    floats = x.astype(jnp.float32)
    length = jnp.sqrt(jnp.sum(floats * floats, axis=1, keepdims=True) + EPS)
    return floats, length, 1.0 / length


def chunk_scalars(place, k, far_count, piece, sizes):
    zh, zl, yh, core, slot = (place[n] for n in range(5))
    q = k % far_count
    near = k >= far_count
    its_core = 1 - core if near else core
    its_yh, its_zh = q // sizes["zh"], q % sizes["zh"]
    group = ((its_zh * sizes["zl"] + zl) * sizes["yh"] + its_yh) * sizes["core"] + its_core
    base = (group * sizes["mp"] + slot) * piece
    if near:
        return base, None
    mine = jnp.logical_and(yh == its_yh, zh == its_zh)
    return base, jnp.where(mine, slot * piece, -(1 << 20))


def partner_ids(part_ref, oth_ref, rows):
    hi = oth_ref[pl.ds(rows, 8), :].astype(jnp.float32)
    ids = (hi[0:2] * 256.0 + hi[2:4]).astype(jnp.int32)
    other = jnp.concatenate([ids[n : n + 1] for n in range(ids.shape[0])], axis=1)
    return jnp.concatenate([part_ref[...], other], axis=1)


def forward_kernel(
    sizes, place, own, oth, far, near, part, weight, msg, ncol, nrow, s_buf
):
    rows, width = own.shape
    far_count, piece = far.shape[0], far.shape[1]
    half = far_count * piece
    block = 256
    for ref, source in ((0, own[...]), (rows, oth[0:rows, :])):
        floats, _, inverse = scaled(source)
        nrow[pl.ds(ref, rows), :] = (floats * inverse).astype(jnp.bfloat16)
    for at, ref in ((0, far), (half, near)):
        for q in range(far_count):
            floats, _, inverse = scaled(ref[q])
            ncol[pl.ds(at + q * piece, piece), :] = (floats * inverse).astype(jnp.bfloat16)

    both = 2 * rows
    step = 8
    ids = partner_ids(part, oth, rows)
    sub = lax.broadcasted_iota(jnp.int32, (step, both), 0)
    lane = lax.broadcasted_iota(jnp.int32, (step, rows), 1)
    mates = jnp.broadcast_to(ids, (step, both)) - sub
    diag = lane - sub[:, :rows]
    total = jnp.zeros((step, both), jnp.float32)
    positive = jnp.zeros((step, both), jnp.float32)
    right = nrow[...]
    for b in range(2 * half // block):
        s_buf[b % 2] = lax.dot_general(
            ncol[pl.ds(b * block, block), :], right, NT, preferred_element_type=jnp.float32
        )
        for c in range(block // piece):
            base, mine = chunk_scalars(place, b * (block // piece) + c, far_count, piece, sizes)
            for r in range(0, piece, step):
                s = s_buf[b % 2, pl.ds(c * piece + r, step), :]
                e = jnp.exp2(s * (INV_TAU * LOG2E))
                if mine is not None:
                    first = jnp.where(diag == mine + r, 0.0, e[:, :rows])
                    e = jnp.concatenate([first, e[:, rows:]], axis=1)
                total = total + e
                positive = jnp.where(mates == base + r, s, positive)
    total = jnp.sum(total, axis=0, keepdims=True)
    positive = jnp.sum(positive, axis=0, keepdims=True) * INV_TAU
    zl = place[1]
    same = [total[:, :rows], total[:, rows:], positive[:, :rows], weight[...]]
    turned = [total[:, rows:], total[:, :rows], positive[:, rows:], weight[...]]
    half_row = rows // 2

    def stacked(parts):
        return jnp.concatenate(
            [p[:, n * half_row : (n + 1) * half_row] for p in parts for n in range(2)], axis=0
        )

    same, turned = stacked(same), stacked(turned)
    members = sizes["mp"]
    for n in range(members):
        msg[zl * members + n] = same
        msg[(1 - zl) * members + n] = turned


def totals_kernel(sizes, place, got, weight, info, loss, cw):
    zl, slot = place[1], place[4]
    members = sizes["mp"]
    summed = got[0]
    for n in range(1, got.shape[0]):
        summed = summed + got[n]
    other_weight = got[(1 - zl) * members, 6:8, :]

    def joined(pair):
        return jnp.concatenate([pair[0:1], pair[1:2]], axis=1)

    total, total_other = joined(summed[0:2]), joined(summed[2:4])
    positive = joined(summed[4:6])
    other_weight = joined(other_weight)
    own_weight = weight[...]
    share = own_weight / total
    share_other = other_weight / total_other
    loss[...] = jnp.log(total) - positive
    info[...] = jnp.concatenate([share, share_other, own_weight, other_weight], axis=0)
    piece = own_weight.shape[1] // members
    out = jnp.zeros((1, 2 * piece), jnp.float32)
    for n in range(members):
        at = slice(n * piece, (n + 1) * piece)
        out = jnp.where(slot == n, jnp.concatenate([share[:, at], own_weight[:, at]], axis=1), out)
    for n in range(cw.shape[0]):
        cw[n] = out


def backward_kernel(
    sizes, place, own, oth, part, ncol, nrow, info, cw, msg, s_buf, coef, acc
):
    rows, width = own.shape
    owners = cw.shape[0]
    far_count = owners // 2
    half = ncol.shape[0] // 2
    piece = half // far_count
    block = 256
    both = 2 * rows
    step = 16
    core = place[3]
    shares = []
    for at in (core, 1 - core):
        flat = cw[pl.ds(at * far_count, far_count)].reshape(far_count, 2 * piece)
        shares.append(flat.T)
    ids = partner_ids(part, oth, rows)
    sub = lax.broadcasted_iota(jnp.int32, (step, both), 0)
    lane = lax.broadcasted_iota(jnp.int32, (step, rows), 1)
    mates = jnp.broadcast_to(ids, (step, both)) - sub
    diag = lane - sub[:, :rows]
    row_share = jnp.concatenate([info[0:1, :], info[1:2, :]], axis=1)
    row_weight = jnp.concatenate([info[2:3, :], info[3:4, :]], axis=1)
    row_share = jnp.broadcast_to(row_share, (step, both))
    row_weight = jnp.broadcast_to(row_weight, (step, both))
    right = nrow[...]
    for b in range(2 * half // block):
        s_buf[b % 2] = lax.dot_general(
            ncol[pl.ds(b * block, block), :], right, NT, preferred_element_type=jnp.float32
        )
        for c in range(block // piece):
            k = b * (block // piece) + c
            base, mine = chunk_scalars(place, k, far_count, piece, sizes)
            column = shares[k // far_count][:, k % far_count : k % far_count + 1]
            for r in range(0, piece, step):
                s = s_buf[b % 2, pl.ds(c * piece + r, step), :]
                e = jnp.exp2(s * (INV_TAU * LOG2E))
                if mine is not None:
                    first = jnp.where(diag == mine + r, 0.0, e[:, :rows])
                    e = jnp.concatenate([first, e[:, rows:]], axis=1)
                value = e * (row_share + column[r : r + step])
                pull = row_weight + column[piece + r : piece + r + step]
                value = jnp.where(mates == base + r, value - pull, value)
                coef[b % 2, pl.ds(c * piece + r, step), :] = value.astype(jnp.bfloat16)
        left = ncol[pl.ds(b * block, block), :].T
        product = jnp.dot(left, coef[b % 2], preferred_element_type=jnp.float32)
        if b == 0:
            acc[...] = product
        else:
            acc[...] += product
    zl = place[1]
    members = sizes["mp"]
    for at, first, source in ((zl, 0, own[...]), (1 - zl, rows, oth[0:rows, :])):
        floats, _, inverse = scaled(source)
        g = acc[:, first : first + rows].T * INV_TAU
        unit = floats * inverse
        out = (g - unit * jnp.sum(unit * g, axis=1, keepdims=True)) * inverse
        msg[pl.ds(at * members, members)] = out.astype(jnp.bfloat16).reshape(members, -1, width)


def shards(sizes, views, partner, weight):
    rows, width = views.shape
    members = sizes["mp"]
    piece = rows // members
    slot = lax.axis_index(MP)
    place = jnp.stack([lax.axis_index(a) for a in ("zh", "zl", "yh", "core")] + [slot])
    place = place.astype(jnp.int32)

    mine = lax.dynamic_slice_in_dim(views, slot * piece, piece, 0)
    packed = jnp.concatenate([partner >> 8, partner & 255]).astype(jnp.bfloat16)
    packed = packed.reshape(-1, width)
    packed = jnp.pad(packed, ((0, 16 - packed.shape[0]), (0, 0)))
    oth = swap(jnp.concatenate([views, packed], axis=0), "zl")
    far_count = sizes["zh"] * sizes["yh"]
    far = exchange(jnp.broadcast_to(mine[None], (far_count, piece, width)), FAR)
    near = swap(far, "core")

    part = partner.reshape(1, rows)
    heft = weight.reshape(1, rows)
    columns = 2 * far_count * piece
    smem = pl.BlockSpec(memory_space=pltpu.SMEM)
    vmem = pl.BlockSpec(memory_space=pltpu.VMEM)
    team = 2 * members
    f32, bf16 = jnp.float32, jnp.bfloat16
    params = pltpu.CompilerParams(vmem_limit_bytes=40 << 20)
    shape = jax.ShapeDtypeStruct
    flops = 2 * columns * 2 * rows * width
    msg, ncol, nrow = pl.pallas_call(
        functools.partial(forward_kernel, sizes),
        name="forward",
        in_specs=[smem] + [vmem] * 6,
        out_specs=[vmem] * 3,
        out_shape=[
            shape((team, 8, rows // 2), f32),
            shape((columns, width), bf16),
            shape((2 * rows, width), bf16),
        ],
        scratch_shapes=[pltpu.VMEM((2, 256, 2 * rows), f32)],
        compiler_params=params,
        cost_estimate=pl.CostEstimate(flops=flops, bytes_accessed=4 << 20, transcendentals=0),
    )(place, views, oth, far, near, part, heft)
    got = exchange(msg, TEAM)
    info, loss, cw = pl.pallas_call(
        functools.partial(totals_kernel, sizes),
        name="totals",
        in_specs=[smem] + [vmem] * 2,
        out_specs=[vmem] * 3,
        out_shape=[
            shape((4, rows), f32),
            shape((1, rows), f32),
            shape((2 * far_count, 1, 2 * piece), f32),
        ],
    )(place, got, heft)
    cw = exchange(cw, OWNERS)
    grads = pl.pallas_call(
        functools.partial(backward_kernel, sizes),
        name="backward",
        in_specs=[smem] + [vmem] * 7,
        out_specs=vmem,
        out_shape=shape((team, piece, width), bf16),
        scratch_shapes=[
            pltpu.VMEM((2, 256, 2 * rows), f32),
            pltpu.VMEM((2, 256, 2 * rows), bf16),
            pltpu.VMEM((width, 2 * rows), f32),
        ],
        compiler_params=params,
        cost_estimate=pl.CostEstimate(flops=2 * flops, bytes_accessed=4 << 20, transcendentals=0),
    )(place, views, oth, part, ncol, nrow, info, cw)
    shares = exchange(grads, TEAM)
    share = jnp.sum(shares.astype(f32), axis=0).astype(bf16)
    grad = exchange(jnp.broadcast_to(share[None], (members, piece, width)), MP)
    return loss.reshape(rows), grad.astype(f32).reshape(rows, width)


def solution(mesh):
    dims = {"zh": 4, "zl": 2, "yh": 4, "core": 2, "yl": 2, "x": 4}
    finer = Mesh(mesh.devices.reshape(tuple(dims.values())), tuple(dims))
    sizes = {**dims, "mp": dims["yl"] * dims["x"]}
    placed = (P(DP, None), P(DP), P(DP))
    return jax.shard_map(
        functools.partial(shards, sizes),
        mesh=finer,
        in_specs=placed,
        out_specs=(P(DP), P(DP, None)),
        check_vma=False,
    )
```

time: 206 us -> 116 us (0.56)
  waiting for transfers between devices: 44.9 us -> 7.46 us
  matrix products: 25.8 us -> 0 us
  starting transfers between devices: 24 us -> 6.02 us
  blocking collectives: 101 us -> 88 us
  Pallas kernels: 0 us -> 10.9 us
  local copies, waits for them, and re-layouts: 4.12 us -> 1.54 us
  other arithmetic: 3.33 us -> 0.96 us
    all_gather x1 -> x0, blocking collectives: 80.5 us -> none  [turned_gather(): whole = lax.all_gather(both, axis, axis=0, tiled=True)]
    all_to_all x2 -> x5, blocking collectives: 21 us -> 88 us  [exchange(): return lax.all_to_all(x, axes, 0, 0, tiled=True)]
    all_to_all x3 -> x0, waiting for transfers between devices: 44.9 us -> none  [the longest x2 36.4 us: sent_to_all(): lax.all_to_all(jnp.broadcast_to(shard[None], (count, *shard.shape)), axis...]
    dot_general x16 -> x0, matrix products: 25.8 us -> none  [the longest x8 21.6 us: backward(): jnp.dot(coef, cols_block, preferred_element_type=jnp.float32)]
    all_to_all x3 -> x0, starting transfers between devices: 24 us -> none  [the longest x2 20.5 us: sent_to_all(): lax.all_to_all(jnp.broadcast_to(shard[None], (count, *shard.shape)), axis...]
    pallas_call x0 -> x3, Pallas kernels: none -> 10.9 us  [the longest x1 5.73 us: shards(): pl.pallas_call(functools.partial(backward_kernel, sizes), name='backward'...]
    ppermute x0 -> x2, waiting for transfers between devices: none -> 7.46 us  [swap(): return lax.ppermute(x, axis, [(0, 1), (1, 0)])]
    ppermute x0 -> x2, starting transfers between devices: none -> 6.02 us  [swap(): return lax.ppermute(x, axis, [(0, 1), (1, 0)])]
  transfers between devices with their start and end apart: 3 -> 2, of which waited for: 3 -> 1; matrix products, arithmetic and copies ran while one was open for 0% -> 0% of each run, Pallas kernels for 0% -> 0%
where the time goes in v1:
time: 116 us
  blocking collectives  88 us (76%)
  Pallas kernels  10.9 us (9%)
  waiting for transfers between devices  7.46 us (6%)
  starting transfers between devices  6.02 us (5%)
  local copies, waits for them, and re-layouts  1.54 us (1%)
    all_to_all x5, blocking collectives, exchange(): return lax.all_to_all(x, axes, 0, 0, tiled=True)  88 us
    ppermute x2, waiting for transfers between devices, swap(): return lax.ppermute(x, axis, [(0, 1), (1, 0)])  7.46 us
    ppermute x2, starting transfers between devices, swap(): return lax.ppermute(x, axis, [(0, 1), (1, 0)])  6.02 us
    pallas_call x1, Pallas kernels, shards(): pl.pallas_call(functools.partial(backward_kernel, sizes), name='backward'...  5.73 us
    pallas_call x1, Pallas kernels, shards(): pl.pallas_call(functools.partial(forward_kernel, sizes), name='forward',...  3.54 us
  transfers between devices with their start and end apart: 2, of which 1 were waited for; matrix products, arithmetic and copies ran while one was open for 0% of the time, Pallas kernels for 0%

profile of v1, /device:TPU:1, one launch (start us, length us, event | category | flops | bytes accessed | tf_op | source)
XLA Modules:
  0.0 115.7 jit_solution(8029766421611743360)
XLA Ops:
  0.6 0.8 constant_dynamic-slice_fusion
  1.5 0.0 copy-start.4
  1.5 0.0 copy-start
  1.5 36.6 %all_to_all.25.far = bf16[16,64,256]{2,1,0:T(8,128)(2,1)S(1)} all-to-all(bf16[16,64,256]{2,1,0:T(8,128)(2,1)S(1)} %broadcast_in_dim.4), channel_id=1, replica_groups=mesh['zh'=4,'zl'=2,'yh'=4,'core'=2,'yl'=2,'x'=4] {'yh','zh'}, dimensions={0} | all-to-all | bytes 1048576 | tf_op jit(solution)/shard_map/all_to_all | solution.py:29
  38.1 3.7 %collective-permute-start.1 = (bf16[16,64,256]{2,1,0:T(8,128)(2,1)S(1)}, bf16[16,64,256]{2,1,0:T(8,128)(2,1)S(1)}, u32[]{:S(2)}, u32[]{:S(2)}) collective-permute-start(bf16[16,64,256]{2,1,0:T(8,128)(2,1)S(1)} %all_to_all.25.far), channel_id=1, source_target_pairs={{0,8},{8,0},{1,9},{9,1},{2,10},{10,2},{3,11},{11,3},{4,12},{12,4},... | collective-permute-start | bytes 1572872 | tf_op jit(solution)/shard_map/ppermute | solution.py:25
  41.8 0.0 copy-done.4
  41.9 0.0 copy-done
  41.9 2.4 %collective-permute-start = (bf16[528,256]{1,0:T(8,128)(2,1)S(1)}, bf16[528,256]{1,0:T(8,128)(2,1)S(1)}, u32[]{:S(2)}, u32[]{:S(2)}) collective-permute-start(bf16[528,256]{1,0:T(8,128)(2,1)S(1)} %pad_maximum_fusion), channel_id=1, source_target_pairs={{0,64},{64,0},{1,65},{65,1},{2,66},{66,2},{3,67},{67,3},{4,68},{68... | collective-permute-start | bytes 811016 | tf_op jit(solution)/shard_map/ppermute | solution.py:25
  44.3 0.1 stack.23.place
  44.4 0.0 copy-start.2
  44.4 0.0 copy-start.1
  44.4 7.5 %collective-permute-done.oth = bf16[528,256]{1,0:T(8,128)(2,1)S(1)} collective-permute-done((bf16[528,256]{1,0:T(8,128)(2,1)S(1)}, bf16[528,256]{1,0:T(8,128)(2,1)S(1)}, u32[]{:S(2)}, u32[]{:S(2)}) %collective-permute-start) | collective-permute-done | bytes 270368 | tf_op jit(solution)/shard_map/ppermute | solution.py:25
  51.8 0.0 collective-permute-done.1.near
  51.8 0.0 copy-done.2
  51.8 0.0 copy-done.1
  51.8 3.5 %forward.1 = (f32[16,8,256]{2,1,0:T(8,128)S(1)}, bf16[2048,256]{1,0:T(8,128)(2,1)S(1)}, bf16[1024,256]{1,0:T(8,128)(2,1)S(1)}) custom-call(s32[5]{0:T(128)S(1)} %stack.23.place, bf16[512,256]{1,0:T(8,128)(2,1)S(1)} %copy-done, bf16[528,256]{1,0:T(8,128)(2,1)S(1)} %collective-permute-done.oth, bf16[16,64,256]{2,1,0:T(8,128)(2,1)S(1)} %all_to_all.25.far, ...), custom_call_target="tpu_custom_call" | custom-call | flops 1073741824 | bytes 4194304 | tf_op jit(solution)/shard_map/forward/pallas_call | solution.py:232
  55.4 10.8 %all_to_all.26.got = f32[16,8,256]{2,1,0:T(8,128)} all-to-all(f32[16,8,256]{2,1,0:T(8,128)S(1)} %get-tuple-element.8), channel_id=1, replica_groups=mesh['zh'=4,'zl'=2,'yh'=4,'core'=2,'yl'=2,'x'=4] {'zl','yl','x'}, dimensions={0} | all-to-all | bytes 262144 | tf_op jit(solution)/shard_map/all_to_all | solution.py:29
  66.2 1.6 %totals.1 = (f32[4,512]{1,0:T(4,128)}, f32[1,512]{1,0:T(1,128)}, f32[32,1,128]{2,1,0:T(1,128)}) custom-call(s32[5]{0:T(128)} %copy-done.2, f32[16,8,256]{2,1,0:T(8,128)} %all_to_all.26.got, f32[1,512]{1,0:T(1,128)} %bitcast.11), custom_call_target="tpu_custom_call" | custom-call | tf_op jit(solution)/shard_map/totals/pallas_call | solution.py:247
  67.8 0.0 copy-start.5
  67.8 18.8 %all_to_all.27.cw = f32[32,1,128]{2,1,0:T(1,128)S(1)} all-to-all(f32[32,1,128]{2,1,0:T(1,128)} %get-tuple-element.13), channel_id=1, replica_groups=mesh['zh'=4,'zl'=2,'yh'=4,'core'=2,'yl'=2,'x'=4] {'core','yh','zh'}, dimensions={0} | all-to-all | bytes 32768 | tf_op jit(solution)/shard_map/all_to_all | solution.py:29
  86.6 0.0 copy-start.3
  86.6 0.0 copy-done.5
  86.6 0.6 copy-done.3
  87.2 5.7 %backward.1 = bf16[16,64,256]{2,1,0:T(8,128)(2,1)S(1)} custom-call(s32[5]{0:T(128)S(1)} %copy-done.3, bf16[512,256]{1,0:T(8,128)(2,1)S(1)} %copy-done, bf16[528,256]{1,0:T(8,128)(2,1)S(1)} %collective-permute-done.oth, s32[1,512]{1,0:T(1,128)S(1)} %bitcast.14, bf16[2048,256]{1,0:T(8,128)(2,1)S(1)} %get-tuple-element.10.ncol, ...), custom_call_target="tpu_custom_call" | custom-call | flops 2147483648 | bytes 4194304 | tf_op jit(solution)/shard_map/backward/pallas_call | solution.py:259
  93.0 13.2 %all_to_all.28 = bf16[16,64,256]{2,1,0:T(8,128)(2,1)S(1)} all-to-all(bf16[16,64,256]{2,1,0:T(8,128)(2,1)S(1)} %backward.1), channel_id=1, replica_groups=mesh['zh'=4,'zl'=2,'yh'=4,'core'=2,'yl'=2,'x'=4] {'zl','yl','x'}, dimensions={0} | all-to-all | bytes 1048576 | tf_op jit(solution)/shard_map/all_to_all | solution.py:29
  106.2 0.1 reduce_sum.12
  106.3 8.5 %all_to_all.29 = bf16[8,64,256]{2,1,0:T(8,128)(2,1)S(1)} all-to-all(bf16[8,64,256]{2,1,0:T(8,128)(2,1)S(1)} %broadcast_in_dim.5), channel_id=1, replica_groups=mesh['zh'=4,'zl'=2,'yh'=4,'core'=2,'yl'=2,'x'=4] {'yl','x'}, dimensions={0} | all-to-all | bytes 524288 | tf_op jit(solution)/shard_map/all_to_all | solution.py:29
  114.8 0.8 bitcast_convert_fusion
  (7 shorter events, 0.1 us)
Async XLA Ops:
  1.5 40.3 %copy-start.4 = (s32[512]{0:T(512)S(1)}, s32[512]{0:T(512)}, u32[]{:S(2)}) copy-start(s32[512]{0:T(512)} %param.4) | copy-start | bytes 6148
  1.5 40.4 %copy-start = (bf16[512,256]{1,0:T(8,128)(2,1)S(1)}, bf16[512,256]{1,0:T(8,128)(2,1)}, u32[]{:S(2)}) copy-start(bf16[512,256]{1,0:T(8,128)(2,1)} %own.3) | copy-start | bytes 786436
  38.1 13.7 %collective-permute-start.1 = (bf16[16,64,256]{2,1,0:T(8,128)(2,1)S(1)}, bf16[16,64,256]{2,1,0:T(8,128)(2,1)S(1)}, u32[]{:S(2)}, u32[]{:S(2)}) collective-permute-start(bf16[16,64,256]{2,1,0:T(8,128)(2,1)S(1)} %all_to_all.25.far), channel_id=1, source_target_pairs={{0,8},{8,0},{1,9},{9,1},{2,10},{10,2},{3,11},{11,3},{4,12},{12,4},... | collective-permute-start | bytes 1572872 | tf_op jit(solution)/shard_map/ppermute | solution.py:25
  41.9 9.9 %collective-permute-start = (bf16[528,256]{1,0:T(8,128)(2,1)S(1)}, bf16[528,256]{1,0:T(8,128)(2,1)S(1)}, u32[]{:S(2)}, u32[]{:S(2)}) collective-permute-start(bf16[528,256]{1,0:T(8,128)(2,1)S(1)} %pad_maximum_fusion), channel_id=1, source_target_pairs={{0,64},{64,0},{1,65},{65,1},{2,66},{66,2},{3,67},{67,3},{4,68},{68... | collective-permute-start | bytes 811016 | tf_op jit(solution)/shard_map/ppermute | solution.py:25
  44.4 7.5 %copy-start.2 = (s32[5]{0:T(128)}, s32[5]{0:T(128)S(1)}, u32[]{:S(2)}) copy-start(s32[5]{0:T(128)S(1)} %stack.23.place) | copy-start | bytes 64
  44.4 7.5 %copy-start.1 = (f32[512]{0:T(512)S(1)}, f32[512]{0:T(512)}, u32[]{:S(2)}) copy-start(f32[512]{0:T(512)} %param.5) | copy-start | bytes 6148
  67.8 18.8 %copy-start.5 = (f32[4,512]{1,0:T(4,128)S(1)}, f32[4,512]{1,0:T(4,128)}, u32[]{:S(2)}) copy-start(f32[4,512]{1,0:T(4,128)} %get-tuple-element.12.info) | copy-start | bytes 24580
  86.6 0.6 copy-start.3

commit v2 on v1

v2 whole, which is shorter than its diff:
```python
import functools

import jax
import jax.numpy as jnp
from jax import lax
from jax.experimental import pallas as pl
from jax.experimental.pallas import tpu as pltpu
from jax.sharding import Mesh
from jax.sharding import PartitionSpec as P


INV_TAU = 10.0
EPS = 1e-06
LOG2E = 1.4426950408889634

DP = ("zh", "zl", "yh", "core")
MP = ("yl", "x")
FAR = ("yh", "zh")
TEAM = ("zl", "yl", "x")
OWNERS = ("core", "yh", "zh")

BLOCK = 256
NT = (((1,), (1,)), ((), ()))


def swap(x, axis):
    return lax.ppermute(x, axis, [(0, 1), (1, 0)])


def exchange(x, axes):
    return lax.all_to_all(x, axes, 0, 0, tiled=True)


def scaled(x):
    floats = x.astype(jnp.float32)
    length = jnp.sqrt(jnp.sum(floats * floats, axis=1, keepdims=True) + EPS)
    return floats, length, 1.0 / length


def place():
    zh, zl, yh, core = (lax.axis_index(a) for a in DP)
    return zh, zl, yh, core, lax.axis_index(MP)


def chunk_scalars(at, q, near, piece, sizes):
    zh, zl, yh, core, slot = at
    its_core = 1 - core if near else core
    its_yh, its_zh = q // sizes["zh"], q % sizes["zh"]
    group = ((its_zh * sizes["zl"] + zl) * sizes["yh"] + its_yh) * sizes["core"] + its_core
    base = (group * sizes["mp"] + slot) * piece
    if near:
        return base, None
    mine = jnp.logical_and(yh == its_yh, zh == its_zh)
    return base, jnp.where(mine, slot * piece, -(1 << 20))


def partner_ids(own_ref, oth_ref, rows):
    ids = []
    for ref in (own_ref, oth_ref):
        pair = ref[pl.ds(rows, 8), :].astype(jnp.float32)
        pair = (pair[0:2] * 256.0 + pair[2:4]).astype(jnp.int32)
        ids += [pair[n : n + 1] for n in range(pair.shape[0])]
    return jnp.concatenate(ids, axis=1)


def forward_half(sizes, at, near, source, ids, nrow, ncol, e_out, s_buf, total, positive):
    chunks, piece = source.shape[0], source.shape[1]
    both = nrow.shape[0]
    rows = both // 2
    for q in range(chunks):
        floats, _, inverse = scaled(source[q])
        ncol[pl.ds(q * piece, piece), :] = (floats * inverse).astype(jnp.bfloat16)
    step = 8
    sub = lax.broadcasted_iota(jnp.int32, (step, both), 0)
    mates = jnp.broadcast_to(ids, (step, both)) - sub
    if not near:
        diag = lax.broadcasted_iota(jnp.int32, (step, rows), 1) - sub[:, :rows]
    right = nrow[...]
    for b in range(chunks * piece // BLOCK):
        s_buf[b % 2] = lax.dot_general(
            ncol[pl.ds(b * BLOCK, BLOCK), :], right, NT, preferred_element_type=jnp.float32
        )
        for c in range(BLOCK // piece):
            base, mine = chunk_scalars(at, b * (BLOCK // piece) + c, near, piece, sizes)
            for r in range(0, piece, step):
                s = s_buf[b % 2, pl.ds(c * piece + r, step), :]
                e = jnp.exp2(s * (INV_TAU * LOG2E))
                if mine is not None:
                    first = jnp.where(diag == mine + r, 0.0, e[:, :rows])
                    e = jnp.concatenate([first, e[:, rows:]], axis=1)
                e_out[pl.ds(b * BLOCK + c * piece + r, step), :] = e
                total = total + e
                positive = jnp.where(mates == base + r, s, positive)
    return total, positive


def far_kernel(sizes, own, oth, far, sums, ncol, nrow, e_out, s_buf):
    rows = nrow.shape[0] // 2
    for at, source in ((0, own[0:rows, :]), (rows, oth[0:rows, :])):
        floats, _, inverse = scaled(source)
        nrow[pl.ds(at, rows), :] = (floats * inverse).astype(jnp.bfloat16)
    ids = partner_ids(own, oth, rows)
    zero = jnp.zeros((8, 2 * rows), jnp.float32)
    total, positive = forward_half(
        sizes, place(), False, far, ids, nrow, ncol, e_out, s_buf, zero, zero
    )
    sums[0] = total
    sums[1] = positive


def near_kernel(sizes, own, oth, near, weight, sums, nrow, msg, ncol, e_out, s_buf):
    rows = nrow.shape[0] // 2
    at = place()
    ids = partner_ids(own, oth, rows)
    total, positive = forward_half(
        sizes, at, True, near, ids, nrow, ncol, e_out, s_buf, sums[0], sums[1]
    )
    total = jnp.sum(total, axis=0, keepdims=True)
    positive = jnp.sum(positive, axis=0, keepdims=True) * INV_TAU
    zl = at[1]
    same = [total[:, :rows], total[:, rows:], positive[:, :rows], weight[...]]
    turned = [total[:, rows:], total[:, :rows], positive[:, rows:], weight[...]]
    half_row = rows // 2

    def stacked(parts):
        return jnp.concatenate(
            [p[:, n * half_row : (n + 1) * half_row] for p in parts for n in range(2)], axis=0
        )

    same, turned = stacked(same), stacked(turned)
    members = sizes["mp"]
    for n in range(members):
        msg[zl * members + n] = same
        msg[(1 - zl) * members + n] = turned


def totals_kernel(sizes, got, weight, info, loss, cw):
    _, zl, _, _, slot = place()
    members = sizes["mp"]
    summed = got[0]
    for n in range(1, got.shape[0]):
        summed = summed + got[n]
    other_weight = got[(1 - zl) * members, 6:8, :]

    def joined(pair):
        return jnp.concatenate([pair[0:1], pair[1:2]], axis=1)

    total, total_other = joined(summed[0:2]), joined(summed[2:4])
    positive = joined(summed[4:6])
    other_weight = joined(other_weight)
    own_weight = weight[...]
    share = own_weight / total
    share_other = other_weight / total_other
    loss[...] = jnp.log(total) - positive
    info[...] = jnp.concatenate([share, share_other, own_weight, other_weight], axis=0)
    piece = own_weight.shape[1] // members
    out = jnp.zeros((1, 2 * piece), jnp.float32)
    for n in range(members):
        at = slice(n * piece, (n + 1) * piece)
        out = jnp.where(slot == n, jnp.concatenate([share[:, at], own_weight[:, at]], axis=1), out)
    for n in range(cw.shape[0]):
        cw[n] = out


def backward_kernel(
    sizes, own, oth, ncol_far, ncol_near, e_far, e_near, info, cw, msg, coef, acc
):
    both, width = acc.shape[1], acc.shape[0]
    rows = both // 2
    chunks = cw.shape[0] // 2
    half = ncol_far.shape[0]
    piece = half // chunks
    step = 16
    at = place()
    ids = partner_ids(own, oth, rows)
    mates = jnp.broadcast_to(ids, (step, both)) - lax.broadcasted_iota(jnp.int32, (step, both), 0)
    row_share = jnp.concatenate([info[0:1, :], info[1:2, :]], axis=1)
    row_weight = jnp.concatenate([info[2:3, :], info[3:4, :]], axis=1)
    row_share = jnp.broadcast_to(row_share, (step, both))
    row_weight = jnp.broadcast_to(row_weight, (step, both))
    turn = 0
    for near, ncol, e_ref in ((False, ncol_far, e_far), (True, ncol_near, e_near)):
        core = 1 - at[3] if near else at[3]
        columns = cw[pl.ds(core * chunks, chunks)].reshape(chunks, 2 * piece).T
        for b in range(half // BLOCK):
            for c in range(BLOCK // piece):
                q = b * (BLOCK // piece) + c
                base, _ = chunk_scalars(at, q, near, piece, sizes)
                column = columns[:, q : q + 1]
                for r in range(0, piece, step):
                    e = e_ref[pl.ds(b * BLOCK + c * piece + r, step), :]
                    value = e * (row_share + column[r : r + step])
                    pull = row_weight + column[piece + r : piece + r + step]
                    value = jnp.where(mates == base + r, value - pull, value)
                    coef[turn % 2, pl.ds(c * piece + r, step), :] = value.astype(jnp.bfloat16)
            left = ncol[pl.ds(b * BLOCK, BLOCK), :].T
            product = jnp.dot(left, coef[turn % 2], preferred_element_type=jnp.float32)
            if turn == 0:
                acc[...] = product
            else:
                acc[...] += product
            turn += 1
    zl = at[1]
    members = sizes["mp"]
    for to, first, source in ((zl, 0, own[0:rows, :]), (1 - zl, rows, oth[0:rows, :])):
        floats, _, inverse = scaled(source)
        g = acc[:, first : first + rows].T * INV_TAU
        unit = floats * inverse
        out = (g - unit * jnp.sum(unit * g, axis=1, keepdims=True)) * inverse
        msg[pl.ds(to * members, members)] = out.astype(jnp.bfloat16).reshape(members, -1, width)


def call(kernel, outs, args, scratch=(), mib=4, flops=0):
    vmem = pl.BlockSpec(memory_space=pltpu.VMEM)
    return pl.pallas_call(
        kernel,
        in_specs=[vmem] * len(args),
        out_specs=[vmem] * len(outs),
        out_shape=[jax.ShapeDtypeStruct(*o) for o in outs],
        scratch_shapes=list(scratch),
        compiler_params=pltpu.CompilerParams(vmem_limit_bytes=mib << 20),
        cost_estimate=pl.CostEstimate(flops=flops, bytes_accessed=1 << 20, transcendentals=0),
    )(*args)


def shards(sizes, views, partner, weight):
    return body(sizes, views, partner, weight)


def body(sizes, views, partner, weight):
    rows, width = views.shape
    members = sizes["mp"]
    piece = rows // members
    slot = lax.axis_index(MP)
    f32, bf16 = jnp.float32, jnp.bfloat16

    packed = jnp.concatenate([partner >> 8, partner & 255]).astype(bf16).reshape(-1, width)
    packed = jnp.pad(packed, ((0, 16 - packed.shape[0]), (0, 0)))
    own = lax.optimization_barrier(jnp.concatenate([views, packed], axis=0))
    oth = swap(own, "zl")
    mine = lax.dynamic_slice_in_dim(own, slot * piece, piece, 0)
    chunks = sizes["zh"] * sizes["yh"]
    far = exchange(jnp.broadcast_to(mine[None], (chunks, piece, width)), FAR)
    near = swap(far, "core")

    heft = weight.reshape(1, rows)
    half, both, team = chunks * piece, 2 * rows, 2 * members
    flops = 2 * half * both * width
    score = pltpu.VMEM((2, BLOCK, both), f32)
    sums, ncol_far, nrow, e_far = call(
        functools.partial(far_kernel, sizes),
        [((2, 8, both), f32), ((half, width), bf16), ((both, width), bf16), ((half, both), f32)],
        (own, oth, far),
        [score],
        16,
        flops,
    )
    msg, ncol_near, e_near = call(
        functools.partial(near_kernel, sizes),
        [((team, 8, rows // 2), f32), ((half, width), bf16), ((half, both), f32)],
        (own, oth, near, heft, sums, nrow),
        [score],
        16,
        flops,
    )
    got = exchange(msg, TEAM)
    info, loss, cw = call(
        functools.partial(totals_kernel, sizes),
        [((4, rows), f32), ((1, rows), f32), ((2 * chunks, 1, 2 * piece), f32)],
        (got, heft),
    )
    cw = exchange(cw, OWNERS)
    (grads,) = call(
        functools.partial(backward_kernel, sizes),
        [((team, piece, width), bf16)],
        (own, oth, ncol_far, ncol_near, e_far, e_near, info, cw),
        [pltpu.VMEM((2, BLOCK, both), bf16), pltpu.VMEM((width, both), f32)],
        16,
        2 * flops,
    )
    shares = exchange(grads, TEAM)
    share = jnp.sum(shares.astype(f32), axis=0).astype(bf16)
    grad = exchange(jnp.broadcast_to(share[None], (members, piece, width)), MP)
    return loss.reshape(rows), grad.astype(f32).reshape(rows, width)


def solution(mesh):
    dims = {"zh": 4, "zl": 2, "yh": 4, "core": 2, "yl": 2, "x": 4}
    finer = Mesh(mesh.devices.reshape(tuple(dims.values())), tuple(dims))
    sizes = {**dims, "mp": dims["yl"] * dims["x"]}
    placed = (P(DP, None), P(DP), P(DP))
    return jax.shard_map(
        functools.partial(shards, sizes),
        mesh=finer,
        in_specs=placed,
        out_specs=(P(DP), P(DP, None)),
        check_vma=False,
    )
```

time: 116 us -> 112 us (0.966)
  Pallas kernels: 10.9 us -> 7.14 us
  other arithmetic: 0.96 us -> 2.59 us
  local copies, waits for them, and re-layouts: 1.54 us -> 0.11 us
    pallas_call x3 -> x4, Pallas kernels: 10.9 us -> 7.14 us  [call(): pl.pallas_call(kernel, in_specs=[vmem] * len(args), out_specs=[vmem] * le...]
  transfers between devices with their start and end apart: 2 -> 2, of which waited for: 1 -> 1; matrix products, arithmetic and copies ran while one was open for 0% -> 0% of each run, Pallas kernels for 0% -> 2%
where the time goes in v2:
time: 112 us
  blocking collectives  87.5 us (78%)
  waiting for transfers between devices  7.56 us (7%)
  Pallas kernels  7.14 us (6%)
  starting transfers between devices  6.02 us (5%)
  other arithmetic  2.59 us (2%)
    all_to_all x5, blocking collectives, exchange(): return lax.all_to_all(x, axes, 0, 0, tiled=True)  87.5 us
    ppermute x2, waiting for transfers between devices, swap(): return lax.ppermute(x, axis, [(0, 1), (1, 0)])  7.56 us
    pallas_call x4, Pallas kernels, call(): pl.pallas_call(kernel, in_specs=[vmem] * len(args), out_specs=[vmem] * le...  7.14 us
    ppermute x2, starting transfers between devices, swap(): return lax.ppermute(x, axis, [(0, 1), (1, 0)])  6.02 us
  transfers between devices with their start and end apart: 2, of which 1 were waited for; matrix products, arithmetic and copies ran while one was open for 0% of the time, Pallas kernels for 2%

profile of v2, /device:TPU:1, one launch (start us, length us, event | category | flops | bytes accessed | tf_op | source)
XLA Modules:
  0.0 111.7 jit_solution(12561154707511389051)
XLA Ops:
  0.6 0.0 copy-start
  0.6 0.7 shift-right-arithmetic_convert_fusion
  1.4 1.0 pad_maximum_fusion.own
  2.4 36.5 %all_to_all.25.far = bf16[16,64,256]{2,1,0:T(8,128)(2,1)S(1)} all-to-all(bf16[16,64,256]{2,1,0:T(8,128)(2,1)S(1)} %broadcast_in_dim.4), channel_id=1, replica_groups=mesh['zh'=4,'zl'=2,'yh'=4,'core'=2,'yl'=2,'x'=4] {'yh','zh'}, dimensions={0} | all-to-all | bytes 1048576 | tf_op jit(solution)/shard_map/all_to_all | solution.py:31
  38.9 3.7 %collective-permute-start.1 = (bf16[16,64,256]{2,1,0:T(8,128)(2,1)S(1)}, bf16[16,64,256]{2,1,0:T(8,128)(2,1)S(1)}, u32[]{:S(2)}, u32[]{:S(2)}) collective-permute-start(bf16[16,64,256]{2,1,0:T(8,128)(2,1)S(1)} %all_to_all.25.far), channel_id=1, source_target_pairs={{0,8},{8,0},{1,9},{9,1},{2,10},{10,2},{3,11},{11,3},{4,12},{12,4},... | collective-permute-start | bytes 1572872 | tf_op jit(solution)/shard_map/ppermute | solution.py:27
  42.6 2.4 %collective-permute-start = (bf16[528,256]{1,0:T(8,128)(2,1)S(1)}, bf16[528,256]{1,0:T(8,128)(2,1)S(1)}, u32[]{:S(2)}, u32[]{:S(2)}) collective-permute-start(bf16[528,256]{1,0:T(8,128)(2,1)S(1)} %pad_maximum_fusion.own), channel_id=1, source_target_pairs={{0,64},{64,0},{1,65},{65,1},{2,66},{66,2},{3,67},{67,3},{4,68},{68... | collective-permute-start | bytes 811016 | tf_op jit(solution)/shard_map/ppermute | solution.py:27
  45.0 7.6 %collective-permute-done.oth = bf16[528,256]{1,0:T(8,128)(2,1)S(1)} collective-permute-done((bf16[528,256]{1,0:T(8,128)(2,1)S(1)}, bf16[528,256]{1,0:T(8,128)(2,1)S(1)}, u32[]{:S(2)}, u32[]{:S(2)}) %collective-permute-start) | collective-permute-done | bytes 270368 | tf_op jit(solution)/shard_map/ppermute | solution.py:27
  52.5 1.8 %shard_map.50 = (f32[2,8,1024]{2,1,0:T(8,128)S(1)}, bf16[1024,256]{1,0:T(8,128)(2,1)S(1)}, bf16[1024,256]{1,0:T(8,128)(2,1)S(1)}, f32[1024,1024]{1,0:T(8,128)S(1)}) custom-call(bf16[528,256]{1,0:T(8,128)(2,1)S(1)} %pad_maximum_fusion.own, bf16[528,256]{1,0:T(8,128)(2,1)S(1)} %collective-permute-done.oth, bf16[16,64,256]{2,1,0:T(8,128)(2,1)S(1)} %all_to_all.25.far), custom_call_target="tpu_custom_call" | custom-call | flops 536870912 | bytes 1048576 | tf_op jit(solution)/shard_map/pallas_call | solution.py:215
  54.3 0.0 collective-permute-done.1.near
  54.3 0.0 copy-done
  54.3 1.4 %shard_map.51 = (f32[16,8,256]{2,1,0:T(8,128)S(1)}, bf16[1024,256]{1,0:T(8,128)(2,1)S(1)}, f32[1024,1024]{1,0:T(8,128)S(1)}) custom-call(bf16[528,256]{1,0:T(8,128)(2,1)S(1)} %pad_maximum_fusion.own, bf16[528,256]{1,0:T(8,128)(2,1)S(1)} %collective-permute-done.oth, bf16[16,64,256]{2,1,0:T(8,128)(2,1)S(1)} %collective-permute-done.1.near, ...), custom_call_target="tpu_custom_call" | custom-call | flops 536870912 | bytes 1048576 | tf_op jit(solution)/shard_map/pallas_call | solution.py:215
  55.7 10.7 %all_to_all.26.got = f32[16,8,256]{2,1,0:T(8,128)S(1)} all-to-all(f32[16,8,256]{2,1,0:T(8,128)S(1)} %get-tuple-element.14), channel_id=1, replica_groups=mesh['zh'=4,'zl'=2,'yh'=4,'core'=2,'yl'=2,'x'=4] {'zl','yl','x'}, dimensions={0} | all-to-all | bytes 262144 | tf_op jit(solution)/shard_map/all_to_all | solution.py:31
  66.4 0.6 shard_map.52
  67.0 18.6 %all_to_all.27.cw = f32[32,1,128]{2,1,0:T(1,128)S(1)} all-to-all(f32[32,1,128]{2,1,0:T(1,128)S(1)} %get-tuple-element.21), channel_id=1, replica_groups=mesh['zh'=4,'zl'=2,'yh'=4,'core'=2,'yl'=2,'x'=4] {'core','yh','zh'}, dimensions={0} | all-to-all | bytes 32768 | tf_op jit(solution)/shard_map/all_to_all | solution.py:31
  85.6 3.4 %shard_map.53 = bf16[16,64,256]{2,1,0:T(8,128)(2,1)S(1)} custom-call(bf16[528,256]{1,0:T(8,128)(2,1)S(1)} %pad_maximum_fusion.own, bf16[528,256]{1,0:T(8,128)(2,1)S(1)} %collective-permute-done.oth, bf16[1024,256]{1,0:T(8,128)(2,1)S(1)} %get-tuple-element.16.ncol_far, bf16[1024,256]{1,0:T(8,128)(2,1)S(1)} %get-tuple-element.17.ncol_near, ...), custom_call_target="tpu_custom_call" | custom-call | flops 1073741824 | bytes 1048576 | tf_op jit(solution)/shard_map/pallas_call | solution.py:215
  89.0 13.2 %all_to_all.28 = bf16[16,64,256]{2,1,0:T(8,128)(2,1)S(1)} all-to-all(bf16[16,64,256]{2,1,0:T(8,128)(2,1)S(1)} %shard_map.53), channel_id=1, replica_groups=mesh['zh'=4,'zl'=2,'yh'=4,'core'=2,'yl'=2,'x'=4] {'zl','yl','x'}, dimensions={0} | all-to-all | bytes 1048576 | tf_op jit(solution)/shard_map/all_to_all | solution.py:31
  102.2 0.1 reduce_sum.12
  102.3 8.5 %all_to_all.29 = bf16[8,64,256]{2,1,0:T(8,128)(2,1)S(1)} all-to-all(bf16[8,64,256]{2,1,0:T(8,128)(2,1)S(1)} %broadcast_in_dim.5), channel_id=1, replica_groups=mesh['zh'=4,'zl'=2,'yh'=4,'core'=2,'yl'=2,'x'=4] {'yl','x'}, dimensions={0} | all-to-all | bytes 524288 | tf_op jit(solution)/shard_map/all_to_all | solution.py:31
  110.8 0.8 bitcast_convert_fusion
  (6 shorter events, 0.1 us)
Async XLA Ops:
  0.6 53.7 %copy-start = (f32[512]{0:T(512)S(1)}, f32[512]{0:T(512)}, u32[]{:S(2)}) copy-start(f32[512]{0:T(512)} %param.5) | copy-start | bytes 6148
  38.9 15.4 %collective-permute-start.1 = (bf16[16,64,256]{2,1,0:T(8,128)(2,1)S(1)}, bf16[16,64,256]{2,1,0:T(8,128)(2,1)S(1)}, u32[]{:S(2)}, u32[]{:S(2)}) collective-permute-start(bf16[16,64,256]{2,1,0:T(8,128)(2,1)S(1)} %all_to_all.25.far), channel_id=1, source_target_pairs={{0,8},{8,0},{1,9},{9,1},{2,10},{10,2},{3,11},{11,3},{4,12},{12,4},... | collective-permute-start | bytes 1572872 | tf_op jit(solution)/shard_map/ppermute | solution.py:27
  42.6 9.9 %collective-permute-start = (bf16[528,256]{1,0:T(8,128)(2,1)S(1)}, bf16[528,256]{1,0:T(8,128)(2,1)S(1)}, u32[]{:S(2)}, u32[]{:S(2)}) collective-permute-start(bf16[528,256]{1,0:T(8,128)(2,1)S(1)} %pad_maximum_fusion.own), channel_id=1, source_target_pairs={{0,64},{64,0},{1,65},{65,1},{2,66},{66,2},{3,67},{67,3},{4,68},{68... | collective-permute-start | bytes 811016 | tf_op jit(solution)/shard_map/ppermute | solution.py:27

commit v3 on v2

--- a/solution.py
+++ b/solution.py
@@ -94,26 +94,28 @@
     return total, positive
 
 
-def far_kernel(sizes, own, oth, far, sums, ncol, nrow, e_out, s_buf):
+def rows_kernel(own, oth, nrow, ids):
     rows = nrow.shape[0] // 2
     for at, source in ((0, own[0:rows, :]), (rows, oth[0:rows, :])):
         floats, _, inverse = scaled(source)
         nrow[pl.ds(at, rows), :] = (floats * inverse).astype(jnp.bfloat16)
-    ids = partner_ids(own, oth, rows)
-    zero = jnp.zeros((8, 2 * rows), jnp.float32)
+    ids[...] = partner_ids(own, oth, rows)
+
+
+def far_kernel(sizes, far, ids, nrow, sums, ncol, e_out, s_buf):
+    zero = jnp.zeros((8, nrow.shape[0]), jnp.float32)
     total, positive = forward_half(
-        sizes, place(), False, far, ids, nrow, ncol, e_out, s_buf, zero, zero
+        sizes, place(), False, far, ids[...], nrow, ncol, e_out, s_buf, zero, zero
     )
     sums[0] = total
     sums[1] = positive
 
 
-def near_kernel(sizes, own, oth, near, weight, sums, nrow, msg, ncol, e_out, s_buf):
+def near_kernel(sizes, near, ids, weight, sums, nrow, msg, ncol, e_out, s_buf):
     rows = nrow.shape[0] // 2
     at = place()
-    ids = partner_ids(own, oth, rows)
     total, positive = forward_half(
-        sizes, at, True, near, ids, nrow, ncol, e_out, s_buf, sums[0], sums[1]
+        sizes, at, True, near, ids[...], nrow, ncol, e_out, s_buf, sums[0], sums[1]
     )
     total = jnp.sum(total, axis=0, keepdims=True)
     positive = jnp.sum(positive, axis=0, keepdims=True) * INV_TAU
@@ -163,7 +165,7 @@
 
 
 def backward_kernel(
-    sizes, own, oth, ncol_far, ncol_near, e_far, e_near, info, cw, msg, coef, acc
+    sizes, own, oth, ids, ncol_far, ncol_near, e_far, e_near, info, cw, msg, coef, acc
 ):
     both, width = acc.shape[1], acc.shape[0]
     rows = both // 2
@@ -172,8 +174,7 @@
     piece = half // chunks
     step = 16
     at = place()
-    ids = partner_ids(own, oth, rows)
-    mates = jnp.broadcast_to(ids, (step, both)) - lax.broadcasted_iota(jnp.int32, (step, both), 0)
+    mates = jnp.broadcast_to(ids[...], (step, both)) - lax.broadcasted_iota(jnp.int32, (step, both), 0)
     row_share = jnp.concatenate([info[0:1, :], info[1:2, :]], axis=1)
     row_weight = jnp.concatenate([info[2:3, :], info[3:4, :]], axis=1)
     row_share = jnp.broadcast_to(row_share, (step, both))
@@ -234,23 +235,25 @@
     slot = lax.axis_index(MP)
     f32, bf16 = jnp.float32, jnp.bfloat16
 
+    mine = lax.dynamic_slice_in_dim(views, slot * piece, piece, 0)
+    chunks = sizes["zh"] * sizes["yh"]
+    far = exchange(jnp.broadcast_to(mine[None], (chunks, piece, width)), FAR)
     packed = jnp.concatenate([partner >> 8, partner & 255]).astype(bf16).reshape(-1, width)
     packed = jnp.pad(packed, ((0, 16 - packed.shape[0]), (0, 0)))
     own = lax.optimization_barrier(jnp.concatenate([views, packed], axis=0))
     oth = swap(own, "zl")
-    mine = lax.dynamic_slice_in_dim(own, slot * piece, piece, 0)
-    chunks = sizes["zh"] * sizes["yh"]
-    far = exchange(jnp.broadcast_to(mine[None], (chunks, piece, width)), FAR)
+    both = 2 * rows
+    nrow, ids = call(rows_kernel, [((both, width), bf16), ((1, both), jnp.int32)], (own, oth))
     near = swap(far, "core")
 
     heft = weight.reshape(1, rows)
-    half, both, team = chunks * piece, 2 * rows, 2 * members
+    half, team = chunks * piece, 2 * members
     flops = 2 * half * both * width
     score = pltpu.VMEM((2, BLOCK, both), f32)
-    sums, ncol_far, nrow, e_far = call(
+    sums, ncol_far, e_far = call(
         functools.partial(far_kernel, sizes),
-        [((2, 8, both), f32), ((half, width), bf16), ((both, width), bf16), ((half, both), f32)],
-        (own, oth, far),
+        [((2, 8, both), f32), ((half, width), bf16), ((half, both), f32)],
+        (far, ids, nrow),
         [score],
         16,
         flops,
@@ -258,7 +261,7 @@
     msg, ncol_near, e_near = call(
         functools.partial(near_kernel, sizes),
         [((team, 8, rows // 2), f32), ((half, width), bf16), ((half, both), f32)],
-        (own, oth, near, heft, sums, nrow),
+        (near, ids, heft, sums, nrow),
         [score],
         16,
         flops,
@@ -273,7 +276,7 @@
     (grads,) = call(
         functools.partial(backward_kernel, sizes),
         [((team, piece, width), bf16)],
-        (own, oth, ncol_far, ncol_near, e_far, e_near, info, cw),
+        (own, oth, ids, ncol_far, ncol_near, e_far, e_near, info, cw),
         [pltpu.VMEM((2, BLOCK, both), bf16), pltpu.VMEM((width, both), f32)],
         16,
         2 * flops,

time: 112 us -> 113 us (level)
  blocking collectives: 87.5 us -> 51 us
  waiting for transfers between devices: 7.56 us -> 27.3 us
  starting transfers between devices: 6.02 us -> 22.2 us
  local copies, waits for them, and re-layouts: 0.11 us -> 1.67 us
    all_to_all x5 -> x4, blocking collectives: 87.5 us -> 51 us  [exchange(): return lax.all_to_all(x, axes, 0, 0, tiled=True)]
    all_to_all x0 -> x1, waiting for transfers between devices: none -> 19.8 us  [exchange(): return lax.all_to_all(x, axes, 0, 0, tiled=True)]
    all_to_all x0 -> x1, starting transfers between devices: none -> 16.2 us  [exchange(): return lax.all_to_all(x, axes, 0, 0, tiled=True)]
    pallas_call x4 -> x5, Pallas kernels: 7.14 us -> 7.17 us  [call(): pl.pallas_call(kernel, in_specs=[vmem] * len(args), out_specs=[vmem] * le...]
  transfers between devices with their start and end apart: 2 -> 3, of which waited for: 1 -> 2; matrix products, arithmetic and copies ran while one was open for 0% -> 2% of each run, Pallas kernels for 2% -> 2%
where the time goes in v3:
time: 113 us
  blocking collectives  51 us (45%)
  waiting for transfers between devices  27.3 us (24%)
  starting transfers between devices  22.2 us (20%)
  Pallas kernels  7.17 us (6%)
  other arithmetic  2.59 us (2%)
  local copies, waits for them, and re-layouts  1.67 us (1%)
    all_to_all x4, blocking collectives, exchange(): return lax.all_to_all(x, axes, 0, 0, tiled=True)  51 us
    all_to_all x1, waiting for transfers between devices, exchange(): return lax.all_to_all(x, axes, 0, 0, tiled=True)  19.8 us
    all_to_all x1, starting transfers between devices, exchange(): return lax.all_to_all(x, axes, 0, 0, tiled=True)  16.2 us
    ppermute x2, waiting for transfers between devices, swap(): return lax.ppermute(x, axis, [(0, 1), (1, 0)])  7.56 us
    pallas_call x5, Pallas kernels, call(): pl.pallas_call(kernel, in_specs=[vmem] * len(args), out_specs=[vmem] * le...  7.17 us
    ppermute x2, starting transfers between devices, swap(): return lax.ppermute(x, axis, [(0, 1), (1, 0)])  6.02 us
  transfers between devices with their start and end apart: 3, of which 2 were waited for; matrix products, arithmetic and copies ran while one was open for 2% of the time, Pallas kernels for 2%

profile of v3, /device:TPU:1, one launch (start us, length us, event | category | flops | bytes accessed | tf_op | source)
XLA Modules:
  0.0 112.7 jit_solution(3182054927146478345)
XLA Ops:
  0.6 0.0 copy-start
  0.6 0.8 constant_dynamic-slice_fusion
  1.4 0.8 broadcast_in_dim.4
  2.3 16.2 %all-to-all-start = ((bf16[16,64,256]{2,1,0:T(8,128)(2,1)}), bf16[16,64,256]{2,1,0:T(8,128)(2,1)S(1)}, u32[]{:S(2)}, u32[]{:S(2)}) async-start(bf16[16,64,256]{2,1,0:T(8,128)(2,1)} %broadcast_in_dim.4), calls=%async_computation | async-start | bytes 1048576 | tf_op jit(solution)/shard_map/all_to_all | solution.py:31
  18.5 0.7 shift-right-arithmetic_convert_fusion
  19.2 19.8 %all-to-all-done.far = bf16[16,64,256]{2,1,0:T(8,128)(2,1)S(1)} async-done(((bf16[16,64,256]{2,1,0:T(8,128)(2,1)}), bf16[16,64,256]{2,1,0:T(8,128)(2,1)S(1)}, u32[]{:S(2)}, u32[]{:S(2)}) %all-to-all-start) | async-done | bytes 524320 | tf_op jit(solution)/shard_map/all_to_all | solution.py:31
  39.0 3.7 %collective-permute-start = (bf16[16,64,256]{2,1,0:T(8,128)(2,1)S(1)}, bf16[16,64,256]{2,1,0:T(8,128)(2,1)S(1)}, u32[]{:S(2)}, u32[]{:S(2)}) collective-permute-start(bf16[16,64,256]{2,1,0:T(8,128)(2,1)S(1)} %all-to-all-done.far), channel_id=1, source_target_pairs={{0,8},{8,0},{1,9},{9,1},{2,10},{10,2},{3,11},{11,3},{4,12},{12,4},... | collective-permute-start | bytes 1572872 | tf_op jit(solution)/shard_map/ppermute | solution.py:27
  42.7 1.0 pad_maximum_fusion.own
  43.6 2.4 %collective-permute-start.1 = (bf16[528,256]{1,0:T(8,128)(2,1)S(1)}, bf16[528,256]{1,0:T(8,128)(2,1)S(1)}, u32[]{:S(2)}, u32[]{:S(2)}) collective-permute-start(bf16[528,256]{1,0:T(8,128)(2,1)S(1)} %pad_maximum_fusion.own), channel_id=1, source_target_pairs={{0,64},{64,0},{1,65},{65,1},{2,66},{66,2},{3,67},{67,3},{4,68},{68... | collective-permute-start | bytes 811016 | tf_op jit(solution)/shard_map/ppermute | solution.py:27
  46.0 7.6 %collective-permute-done.1.oth = bf16[528,256]{1,0:T(8,128)(2,1)S(1)} collective-permute-done((bf16[528,256]{1,0:T(8,128)(2,1)S(1)}, bf16[528,256]{1,0:T(8,128)(2,1)S(1)}, u32[]{:S(2)}, u32[]{:S(2)}) %collective-permute-start.1) | collective-permute-done | bytes 270368 | tf_op jit(solution)/shard_map/ppermute | solution.py:27
  53.6 0.3 shard_map.50
  53.9 1.5 %shard_map.51 = (f32[2,8,1024]{2,1,0:T(8,128)S(1)}, bf16[1024,256]{1,0:T(8,128)(2,1)S(1)}, f32[1024,1024]{1,0:T(8,128)S(1)}) custom-call(bf16[16,64,256]{2,1,0:T(8,128)(2,1)S(1)} %all-to-all-done.far, s32[1,1024]{1,0:T(1,128)S(1)} %get-tuple-element.13.ids, bf16[1024,256]{1,0:T(8,128)(2,1)S(1)} %get-tuple-element.14.nrow), custom_call_target="tpu_custom_call" | custom-call | flops 536870912 | bytes 1048576 | tf_op jit(solution)/shard_map/pallas_call | solution.py:216
  55.4 0.0 collective-permute-done.near
  55.4 0.0 copy-done
  55.4 1.4 %shard_map.52 = (f32[16,8,256]{2,1,0:T(8,128)S(1)}, bf16[1024,256]{1,0:T(8,128)(2,1)S(1)}, f32[1024,1024]{1,0:T(8,128)S(1)}) custom-call(bf16[16,64,256]{2,1,0:T(8,128)(2,1)S(1)} %collective-permute-done.near, s32[1,1024]{1,0:T(1,128)S(1)} %get-tuple-element.13.ids, f32[1,512]{1,0:T(1,128)S(1)} %bitcast.5, f32[2,8,1024]{2,1,0:T(8,128)S(1)} %get-tuple-element.15.sums, ...), custom_call_target="tpu_custom_call" | custom-call | flops 536870912 | bytes 1048576 | tf_op jit(solution)/shard_map/pallas_call | solution.py:216
  56.7 10.7 %all_to_all.25.got = f32[16,8,256]{2,1,0:T(8,128)S(1)} all-to-all(f32[16,8,256]{2,1,0:T(8,128)S(1)} %get-tuple-element.16), channel_id=1, replica_groups=mesh['zh'=4,'zl'=2,'yh'=4,'core'=2,'yl'=2,'x'=4] {'zl','yl','x'}, dimensions={0} | all-to-all | bytes 262144 | tf_op jit(solution)/shard_map/all_to_all | solution.py:31
  67.4 0.6 shard_map.53
  68.1 18.6 %all_to_all.26.cw = f32[32,1,128]{2,1,0:T(1,128)S(1)} all-to-all(f32[32,1,128]{2,1,0:T(1,128)S(1)} %get-tuple-element.23), channel_id=1, replica_groups=mesh['zh'=4,'zl'=2,'yh'=4,'core'=2,'yl'=2,'x'=4] {'core','yh','zh'}, dimensions={0} | all-to-all | bytes 32768 | tf_op jit(solution)/shard_map/all_to_all | solution.py:31
  86.6 3.4 %shard_map.54 = bf16[16,64,256]{2,1,0:T(8,128)(2,1)S(1)} custom-call(bf16[528,256]{1,0:T(8,128)(2,1)S(1)} %pad_maximum_fusion.own, bf16[528,256]{1,0:T(8,128)(2,1)S(1)} %collective-permute-done.1.oth, s32[1,1024]{1,0:T(1,128)S(1)} %get-tuple-element.13.ids, bf16[1024,256]{1,0:T(8,128)(2,1)S(1)} %get-tuple-element.18.ncol_far, ...), custom_call_target="tpu_custom_call" | custom-call | flops 1073741824 | bytes 1048576 | tf_op jit(solution)/shard_map/pallas_call | solution.py:216
  90.0 13.2 %all_to_all.27 = bf16[16,64,256]{2,1,0:T(8,128)(2,1)S(1)} all-to-all(bf16[16,64,256]{2,1,0:T(8,128)(2,1)S(1)} %shard_map.54), channel_id=1, replica_groups=mesh['zh'=4,'zl'=2,'yh'=4,'core'=2,'yl'=2,'x'=4] {'zl','yl','x'}, dimensions={0} | all-to-all | bytes 1048576 | tf_op jit(solution)/shard_map/all_to_all | solution.py:31
  103.2 0.1 reduce_sum.12
  103.4 8.5 %all_to_all.28 = bf16[8,64,256]{2,1,0:T(8,128)(2,1)S(1)} all-to-all(bf16[8,64,256]{2,1,0:T(8,128)(2,1)S(1)} %broadcast_in_dim.5), channel_id=1, replica_groups=mesh['zh'=4,'zl'=2,'yh'=4,'core'=2,'yl'=2,'x'=4] {'yl','x'}, dimensions={0} | all-to-all | bytes 524288 | tf_op jit(solution)/shard_map/all_to_all | solution.py:31
  111.9 0.8 bitcast_convert_fusion
  (4 shorter events, 0.1 us)
Async XLA Ops:
  0.6 54.7 %copy-start = (f32[512]{0:T(512)S(1)}, f32[512]{0:T(512)}, u32[]{:S(2)}) copy-start(f32[512]{0:T(512)} %param.5) | copy-start | bytes 6148
  2.3 36.7 %all-to-all-start = ((bf16[16,64,256]{2,1,0:T(8,128)(2,1)}), bf16[16,64,256]{2,1,0:T(8,128)(2,1)S(1)}, u32[]{:S(2)}, u32[]{:S(2)}) async-start(bf16[16,64,256]{2,1,0:T(8,128)(2,1)} %broadcast_in_dim.4), calls=%async_computation | async-start | bytes 1048576 | tf_op jit(solution)/shard_map/all_to_all | solution.py:31
  39.0 16.4 %collective-permute-start = (bf16[16,64,256]{2,1,0:T(8,128)(2,1)S(1)}, bf16[16,64,256]{2,1,0:T(8,128)(2,1)S(1)}, u32[]{:S(2)}, u32[]{:S(2)}) collective-permute-start(bf16[16,64,256]{2,1,0:T(8,128)(2,1)S(1)} %all-to-all-done.far), channel_id=1, source_target_pairs={{0,8},{8,0},{1,9},{9,1},{2,10},{10,2},{3,11},{11,3},{4,12},{12,4},... | collective-permute-start | bytes 1572872 | tf_op jit(solution)/shard_map/ppermute | solution.py:27
  43.6 9.9 %collective-permute-start.1 = (bf16[528,256]{1,0:T(8,128)(2,1)S(1)}, bf16[528,256]{1,0:T(8,128)(2,1)S(1)}, u32[]{:S(2)}, u32[]{:S(2)}) collective-permute-start(bf16[528,256]{1,0:T(8,128)(2,1)S(1)} %pad_maximum_fusion.own), channel_id=1, source_target_pairs={{0,64},{64,0},{1,65},{65,1},{2,66},{66,2},{3,67},{67,3},{4,68},{68... | collective-permute-start | bytes 811016 | tf_op jit(solution)/shard_map/ppermute | solution.py:27

commit v4 on v2

--- a/solution.py
+++ b/solution.py
@@ -61,6 +61,30 @@
         pair = (pair[0:2] * 256.0 + pair[2:4]).astype(jnp.int32)
         ids += [pair[n : n + 1] for n in range(pair.shape[0])]
     return jnp.concatenate(ids, axis=1)
+
+
+def pack_kernel(views, part, weight, own, spread, heft, mates, arrived):
+    rows = views.shape[0]
+    piece = spread.shape[1]
+    copy = pltpu.make_async_copy(views, own.at[pl.ds(0, rows)], arrived.at[0])
+    small = pltpu.make_async_copy(part, mates, arrived.at[1])
+    last = pltpu.make_async_copy(weight, heft, arrived.at[2])
+    small.start()
+    copy.start()
+    last.start()
+    small.wait()
+    ids = mates[...]
+    half_row = rows // 2
+    parts = [x[:, n * half_row : (n + 1) * half_row] for x in (ids >> 8, ids & 255) for n in (0, 1)]
+    blank = jnp.zeros((own.shape[0] - rows - 4, half_row), jnp.int32)
+    packed = jnp.concatenate(parts + [blank], axis=0).astype(jnp.float32)
+    own[pl.ds(rows, own.shape[0] - rows), :] = packed.astype(jnp.bfloat16)
+    slot = lax.axis_index(MP)
+    copy.wait()
+    last.wait()
+    mine = own[pl.ds(pl.multiple_of(slot * piece, piece), piece), :]
+    for n in range(spread.shape[0]):
+        spread[n] = mine
 
 
 def forward_half(sizes, at, near, source, ids, nrow, ncol, e_out, s_buf, total, positive):
@@ -231,19 +255,29 @@
     rows, width = views.shape
     members = sizes["mp"]
     piece = rows // members
-    slot = lax.axis_index(MP)
     f32, bf16 = jnp.float32, jnp.bfloat16
 
-    packed = jnp.concatenate([partner >> 8, partner & 255]).astype(bf16).reshape(-1, width)
-    packed = jnp.pad(packed, ((0, 16 - packed.shape[0]), (0, 0)))
-    own = lax.optimization_barrier(jnp.concatenate([views, packed], axis=0))
+    chunks = sizes["zh"] * sizes["yh"]
+    own, spread, heft = pl.pallas_call(
+        pack_kernel,
+        name="pack",
+        in_specs=[pl.BlockSpec(memory_space=pltpu.HBM)] * 3,
+        out_specs=[pl.BlockSpec(memory_space=pltpu.VMEM)] * 3,
+        out_shape=[
+            jax.ShapeDtypeStruct((rows + 16, width), bf16),
+            jax.ShapeDtypeStruct((chunks, piece, width), bf16),
+            jax.ShapeDtypeStruct((1, rows), f32),
+        ],
+        scratch_shapes=[pltpu.VMEM((1, rows), jnp.int32), pltpu.SemaphoreType.DMA((3,))],
+        compiler_params=pltpu.CompilerParams(vmem_limit_bytes=4 << 20),
+    )(*[
+        pltpu.with_memory_space_constraint(a, pltpu.HBM)
+        for a in (views, partner.reshape(1, rows), weight.reshape(1, rows))
+    ])
     oth = swap(own, "zl")
-    mine = lax.dynamic_slice_in_dim(own, slot * piece, piece, 0)
-    chunks = sizes["zh"] * sizes["yh"]
-    far = exchange(jnp.broadcast_to(mine[None], (chunks, piece, width)), FAR)
+    far = exchange(spread, FAR)
     near = swap(far, "core")
 
-    heft = weight.reshape(1, rows)
     half, both, team = chunks * piece, 2 * rows, 2 * members
     flops = 2 * half * both * width
     score = pltpu.VMEM((2, BLOCK, both), f32)

time: 112 us -> 111 us (level)
  other arithmetic: 2.59 us -> 0.92 us
where the time goes in v4:
time: 111 us
  blocking collectives  87.5 us (79%)
  Pallas kernels  8.21 us (7%)
  waiting for transfers between devices  7.56 us (7%)
  starting transfers between devices  6.02 us (5%)
    all_to_all x5, blocking collectives, exchange(): return lax.all_to_all(x, axes, 0, 0, tiled=True)  87.5 us
    ppermute x2, waiting for transfers between devices, swap(): return lax.ppermute(x, axis, [(0, 1), (1, 0)])  7.56 us
    pallas_call x4, Pallas kernels, call(): pl.pallas_call(kernel, in_specs=[vmem] * len(args), out_specs=[vmem] * le...  7.16 us
    ppermute x2, starting transfers between devices, swap(): return lax.ppermute(x, axis, [(0, 1), (1, 0)])  6.02 us
  transfers between devices with their start and end apart: 2, of which 1 were waited for; matrix products, arithmetic and copies ran while one was open for 0% of the time, Pallas kernels for 2%

profile of v4, /device:TPU:1, one launch (start us, length us, event | category | flops | bytes accessed | tf_op | source)
XLA Modules:
  0.0 110.9 jit_solution(1578379804190598037)
XLA Ops:
  0.6 1.0 pack.1
  1.7 36.5 %all_to_all.25.far = bf16[16,64,256]{2,1,0:T(8,128)(2,1)S(1)} all-to-all(bf16[16,64,256]{2,1,0:T(8,128)(2,1)S(1)} %get-tuple-element.16), channel_id=1, replica_groups=mesh['zh'=4,'zl'=2,'yh'=4,'core'=2,'yl'=2,'x'=4] {'yh','zh'}, dimensions={0} | all-to-all | bytes 1048576 | tf_op jit(solution)/shard_map/all_to_all | solution.py:31
  38.2 3.7 %collective-permute-start.1 = (bf16[16,64,256]{2,1,0:T(8,128)(2,1)S(1)}, bf16[16,64,256]{2,1,0:T(8,128)(2,1)S(1)}, u32[]{:S(2)}, u32[]{:S(2)}) collective-permute-start(bf16[16,64,256]{2,1,0:T(8,128)(2,1)S(1)} %all_to_all.25.far), channel_id=1, source_target_pairs={{0,8},{8,0},{1,9},{9,1},{2,10},{10,2},{3,11},{11,3},{4,12},{12,4},... | collective-permute-start | bytes 1572872 | tf_op jit(solution)/shard_map/ppermute | solution.py:27
  41.9 2.4 %collective-permute-start = (bf16[528,256]{1,0:T(8,128)(2,1)S(1)}, bf16[528,256]{1,0:T(8,128)(2,1)S(1)}, u32[]{:S(2)}, u32[]{:S(2)}) collective-permute-start(bf16[528,256]{1,0:T(8,128)(2,1)S(1)} %get-tuple-element.15.own), channel_id=1, source_target_pairs={{0,64},{64,0},{1,65},{65,1},{2,66},{66,2},{3,67},{67,3},{4,68},{68... | collective-permute-start | bytes 811016 | tf_op jit(solution)/shard_map/ppermute | solution.py:27
  44.2 7.6 %collective-permute-done.oth = bf16[528,256]{1,0:T(8,128)(2,1)S(1)} collective-permute-done((bf16[528,256]{1,0:T(8,128)(2,1)S(1)}, bf16[528,256]{1,0:T(8,128)(2,1)S(1)}, u32[]{:S(2)}, u32[]{:S(2)}) %collective-permute-start) | collective-permute-done | bytes 270368 | tf_op jit(solution)/shard_map/ppermute | solution.py:27
  51.8 1.8 %shard_map.50 = (f32[2,8,1024]{2,1,0:T(8,128)S(1)}, bf16[1024,256]{1,0:T(8,128)(2,1)S(1)}, bf16[1024,256]{1,0:T(8,128)(2,1)S(1)}, f32[1024,1024]{1,0:T(8,128)S(1)}) custom-call(bf16[528,256]{1,0:T(8,128)(2,1)S(1)} %get-tuple-element.15.own, bf16[528,256]{1,0:T(8,128)(2,1)S(1)} %collective-permute-done.oth, bf16[16,64,256]{2,1,0:T(8,128)(2,1)S(1)} %all_to_all.25.far), custom_call_target="tpu_custom_call" | custom-call | flops 536870912 | bytes 1048576 | tf_op jit(solution)/shard_map/pallas_call | solution.py:239
  53.6 0.0 collective-permute-done.1.near
  53.6 1.4 %shard_map.51 = (f32[16,8,256]{2,1,0:T(8,128)S(1)}, bf16[1024,256]{1,0:T(8,128)(2,1)S(1)}, f32[1024,1024]{1,0:T(8,128)S(1)}) custom-call(bf16[528,256]{1,0:T(8,128)(2,1)S(1)} %get-tuple-element.15.own, bf16[528,256]{1,0:T(8,128)(2,1)S(1)} %collective-permute-done.oth, bf16[16,64,256]{2,1,0:T(8,128)(2,1)S(1)} %collective-permute-done.1.near, ...), custom_call_target="tpu_custom_call" | custom-call | flops 536870912 | bytes 1048576 | tf_op jit(solution)/shard_map/pallas_call | solution.py:239
  55.0 10.7 %all_to_all.26.got = f32[16,8,256]{2,1,0:T(8,128)S(1)} all-to-all(f32[16,8,256]{2,1,0:T(8,128)S(1)} %get-tuple-element.20), channel_id=1, replica_groups=mesh['zh'=4,'zl'=2,'yh'=4,'core'=2,'yl'=2,'x'=4] {'zl','yl','x'}, dimensions={0} | all-to-all | bytes 262144 | tf_op jit(solution)/shard_map/all_to_all | solution.py:31
  65.6 0.6 shard_map.52
  66.3 18.6 %all_to_all.27.cw = f32[32,1,128]{2,1,0:T(1,128)S(1)} all-to-all(f32[32,1,128]{2,1,0:T(1,128)S(1)} %get-tuple-element.27), channel_id=1, replica_groups=mesh['zh'=4,'zl'=2,'yh'=4,'core'=2,'yl'=2,'x'=4] {'core','yh','zh'}, dimensions={0} | all-to-all | bytes 32768 | tf_op jit(solution)/shard_map/all_to_all | solution.py:31
  84.8 3.4 %shard_map.53 = bf16[16,64,256]{2,1,0:T(8,128)(2,1)S(1)} custom-call(bf16[528,256]{1,0:T(8,128)(2,1)S(1)} %get-tuple-element.15.own, bf16[528,256]{1,0:T(8,128)(2,1)S(1)} %collective-permute-done.oth, bf16[1024,256]{1,0:T(8,128)(2,1)S(1)} %get-tuple-element.22.ncol_far, bf16[1024,256]{1,0:T(8,128)(2,1)S(1)} %get-tuple-element.23.ncol_near, ...), custom_call_target="tpu_custom_call" | custom-call | flops 1073741824 | bytes 1048576 | tf_op jit(solution)/shard_map/pallas_call | solution.py:239
  88.2 13.2 %all_to_all.28 = bf16[16,64,256]{2,1,0:T(8,128)(2,1)S(1)} all-to-all(bf16[16,64,256]{2,1,0:T(8,128)(2,1)S(1)} %shard_map.53), channel_id=1, replica_groups=mesh['zh'=4,'zl'=2,'yh'=4,'core'=2,'yl'=2,'x'=4] {'zl','yl','x'}, dimensions={0} | all-to-all | bytes 1048576 | tf_op jit(solution)/shard_map/all_to_all | solution.py:31
  101.5 0.1 reduce_sum.12
  101.6 8.5 %all_to_all.29 = bf16[8,64,256]{2,1,0:T(8,128)(2,1)S(1)} all-to-all(bf16[8,64,256]{2,1,0:T(8,128)(2,1)S(1)} %broadcast_in_dim.2), channel_id=1, replica_groups=mesh['zh'=4,'zl'=2,'yh'=4,'core'=2,'yl'=2,'x'=4] {'yl','x'}, dimensions={0} | all-to-all | bytes 524288 | tf_op jit(solution)/shard_map/all_to_all | solution.py:31
  110.1 0.8 bitcast_convert_fusion
  (1 shorter events, 0.0 us)
Async XLA Ops:
  38.2 15.4 %collective-permute-start.1 = (bf16[16,64,256]{2,1,0:T(8,128)(2,1)S(1)}, bf16[16,64,256]{2,1,0:T(8,128)(2,1)S(1)}, u32[]{:S(2)}, u32[]{:S(2)}) collective-permute-start(bf16[16,64,256]{2,1,0:T(8,128)(2,1)S(1)} %all_to_all.25.far), channel_id=1, source_target_pairs={{0,8},{8,0},{1,9},{9,1},{2,10},{10,2},{3,11},{11,3},{4,12},{12,4},... | collective-permute-start | bytes 1572872 | tf_op jit(solution)/shard_map/ppermute | solution.py:27
  41.9 9.9 %collective-permute-start = (bf16[528,256]{1,0:T(8,128)(2,1)S(1)}, bf16[528,256]{1,0:T(8,128)(2,1)S(1)}, u32[]{:S(2)}, u32[]{:S(2)}) collective-permute-start(bf16[528,256]{1,0:T(8,128)(2,1)S(1)} %get-tuple-element.15.own), channel_id=1, source_target_pairs={{0,64},{64,0},{1,65},{65,1},{2,66},{66,2},{3,67},{67,3},{4,68},{68... | collective-permute-start | bytes 811016 | tf_op jit(solution)/shard_map/ppermute | solution.py:27

commit v5 on v4

--- a/solution.py
+++ b/solution.py
@@ -87,7 +87,9 @@
         spread[n] = mine
 
 
-def forward_half(sizes, at, near, source, ids, nrow, ncol, e_out, s_buf, total, positive):
+def forward_half(
+    sizes, at, near, source, ids, nrow, ncol, s_buf, lanes, total, positive
+):
     chunks, piece = source.shape[0], source.shape[1]
     both = nrow.shape[0]
     rows = both // 2
@@ -112,109 +114,137 @@
                 if mine is not None:
                     first = jnp.where(diag == mine + r, 0.0, e[:, :rows])
                     e = jnp.concatenate([first, e[:, rows:]], axis=1)
-                e_out[pl.ds(b * BLOCK + c * piece + r, step), :] = e
+                here = pl.ds(b * BLOCK + c * piece + r, step)
+                across = e[:, :128]
+                for n in range(128, both, 128):
+                    across = across + e[:, n : n + 128]
+                lanes[here, :] = across
                 total = total + e
                 positive = jnp.where(mates == base + r, s, positive)
-    return total, positive
-
-
-def far_kernel(sizes, own, oth, far, sums, ncol, nrow, e_out, s_buf):
+    column = [
+        jnp.sum(lanes[n : n + 128, :].T, axis=0, keepdims=True)
+        for n in range(0, chunks * piece, 128)
+    ]
+    return total, positive, jnp.concatenate(column, axis=0)
+
+
+def far_kernel(sizes, own, oth, far, sums, column, ncol, nrow, s_buf, lanes):
     rows = nrow.shape[0] // 2
     for at, source in ((0, own[0:rows, :]), (rows, oth[0:rows, :])):
         floats, _, inverse = scaled(source)
         nrow[pl.ds(at, rows), :] = (floats * inverse).astype(jnp.bfloat16)
     ids = partner_ids(own, oth, rows)
     zero = jnp.zeros((8, 2 * rows), jnp.float32)
-    total, positive = forward_half(
-        sizes, place(), False, far, ids, nrow, ncol, e_out, s_buf, zero, zero
+    total, positive, column[...] = forward_half(
+        sizes, place(), False, far, ids, nrow, ncol, s_buf, lanes, zero, zero
     )
     sums[0] = total
     sums[1] = positive
 
 
-def near_kernel(sizes, own, oth, near, weight, sums, nrow, msg, ncol, e_out, s_buf):
+def near_kernel(
+    sizes, own, oth, near, weight, sums, column, nrow, msg, cmsg, ncol, s_buf, lanes
+):
     rows = nrow.shape[0] // 2
     at = place()
     ids = partner_ids(own, oth, rows)
-    total, positive = forward_half(
-        sizes, at, True, near, ids, nrow, ncol, e_out, s_buf, sums[0], sums[1]
-    )
+    total, positive, last = forward_half(
+        sizes, at, True, near, ids, nrow, ncol, s_buf, lanes, sums[0], sums[1]
+    )
+    members = sizes["mp"]
+    piece = rows // members
+    _, zl, _, core, slot = at
+    mine = jnp.zeros((1, piece), jnp.float32)
+    for n in range(members):
+        mine = jnp.where(slot == n, weight[:, n * piece : (n + 1) * piece], mine)
+    coarse = mine.astype(jnp.bfloat16).astype(jnp.float32)
+    fine = jnp.concatenate([coarse, mine - coarse], axis=1)
+    first = jnp.where(core == 0, column[...], last)
+    second = jnp.where(core == 0, last, column[...])
+    blank = jnp.zeros((7, 2 * piece), jnp.float32)
+    packed = jnp.concatenate([first, second, fine, blank], axis=0).astype(jnp.bfloat16)
+    for n in range(cmsg.shape[0]):
+        cmsg[n] = packed
+
     total = jnp.sum(total, axis=0, keepdims=True)
     positive = jnp.sum(positive, axis=0, keepdims=True) * INV_TAU
-    zl = at[1]
-    same = [total[:, :rows], total[:, rows:], positive[:, :rows], weight[...]]
-    turned = [total[:, rows:], total[:, :rows], positive[:, rows:], weight[...]]
+    heft = jnp.where(slot == 0, weight[...], 0.0)
+    none = jnp.zeros_like(heft)
     half_row = rows // 2
-
-    def stacked(parts):
-        return jnp.concatenate(
+    for to, parts in (
+        (zl, [total[:, :rows], positive[:, :rows], heft, none]),
+        (1 - zl, [total[:, rows:], positive[:, rows:], none, none]),
+    ):
+        msg[to] = jnp.concatenate(
             [p[:, n * half_row : (n + 1) * half_row] for p in parts for n in range(2)], axis=0
         )
 
-    same, turned = stacked(same), stacked(turned)
-    members = sizes["mp"]
-    for n in range(members):
-        msg[zl * members + n] = same
-        msg[(1 - zl) * members + n] = turned
-
-
-def totals_kernel(sizes, got, weight, info, loss, cw):
-    _, zl, _, _, slot = place()
-    members = sizes["mp"]
-    summed = got[0]
-    for n in range(1, got.shape[0]):
-        summed = summed + got[n]
-    other_weight = got[(1 - zl) * members, 6:8, :]
-
-    def joined(pair):
-        return jnp.concatenate([pair[0:1], pair[1:2]], axis=1)
-
-    total, total_other = joined(summed[0:2]), joined(summed[2:4])
-    positive = joined(summed[4:6])
-    other_weight = joined(other_weight)
-    own_weight = weight[...]
-    share = own_weight / total
-    share_other = other_weight / total_other
-    loss[...] = jnp.log(total) - positive
-    info[...] = jnp.concatenate([share, share_other, own_weight, other_weight], axis=0)
-    piece = own_weight.shape[1] // members
-    out = jnp.zeros((1, 2 * piece), jnp.float32)
-    for n in range(members):
-        at = slice(n * piece, (n + 1) * piece)
-        out = jnp.where(slot == n, jnp.concatenate([share[:, at], own_weight[:, at]], axis=1), out)
-    for n in range(cw.shape[0]):
-        cw[n] = out
+
+def totals_kernel(got, info, loss):
+    zl = place()[1]
+
+    def joined(group, n):
+        return jnp.concatenate([group[n : n + 1], group[n + 1 : n + 2]], axis=1)
+
+    own, other = got[zl], got[1 - zl]
+    total, own_weight = joined(own, 0), joined(own, 4)
+    other_weight = joined(other, 4)
+    loss[...] = jnp.log(total) - joined(own, 2)
+    info[...] = jnp.concatenate(
+        [own_weight / total, other_weight / joined(other, 0), own_weight, other_weight], axis=0
+    )
 
 
 def backward_kernel(
-    sizes, own, oth, ncol_far, ncol_near, e_far, e_near, info, cw, msg, coef, acc
+    sizes, own, oth, nrow, ncol_far, ncol_near, info, cgot, msg, s_buf, coef, acc
 ):
     both, width = acc.shape[1], acc.shape[0]
     rows = both // 2
-    chunks = cw.shape[0] // 2
+    chunks = cgot.shape[0] // 2
     half = ncol_far.shape[0]
     piece = half // chunks
     step = 16
     at = place()
     ids = partner_ids(own, oth, rows)
-    mates = jnp.broadcast_to(ids, (step, both)) - lax.broadcasted_iota(jnp.int32, (step, both), 0)
+    sub = lax.broadcasted_iota(jnp.int32, (step, both), 0)
+    mates = jnp.broadcast_to(ids, (step, both)) - sub
+    diag = lax.broadcasted_iota(jnp.int32, (step, rows), 1) - sub[:, :rows]
+    right = nrow[...]
     row_share = jnp.concatenate([info[0:1, :], info[1:2, :]], axis=1)
     row_weight = jnp.concatenate([info[2:3, :], info[3:4, :]], axis=1)
     row_share = jnp.broadcast_to(row_share, (step, both))
     row_weight = jnp.broadcast_to(row_weight, (step, both))
+    column_total = cgot[0, 0:16, :].astype(jnp.float32)
+    for n in range(1, 2 * chunks):
+        column_total = column_total + cgot[n, 0:16, :].astype(jnp.float32)
+    inverse_total = 1.0 / column_total
     turn = 0
-    for near, ncol, e_ref in ((False, ncol_far, e_far), (True, ncol_near, e_near)):
+    for near, ncol in ((False, ncol_far), (True, ncol_near)):
         core = 1 - at[3] if near else at[3]
-        columns = cw[pl.ds(core * chunks, chunks)].reshape(chunks, 2 * piece).T
+        inverse = jnp.where(core == 0, inverse_total[0:8], inverse_total[8:16]).T
+        heft = []
+        for q in range(chunks):
+            row = cgot[core * chunks + q, 16:24, :].astype(jnp.float32)[0:1]
+            heft.append(row + jnp.concatenate([row[:, piece:], row[:, :piece]], axis=1))
+        heft = jnp.concatenate(heft, axis=0).T
         for b in range(half // BLOCK):
+            s_buf[turn % 2] = lax.dot_general(
+                ncol[pl.ds(b * BLOCK, BLOCK), :], right, NT, preferred_element_type=jnp.float32
+            )
             for c in range(BLOCK // piece):
                 q = b * (BLOCK // piece) + c
-                base, _ = chunk_scalars(at, q, near, piece, sizes)
-                column = columns[:, q : q + 1]
+                base, mine = chunk_scalars(at, q, near, piece, sizes)
+                odd = slice(q % 2 * piece, (q % 2 + 1) * piece)
+                pull_in = heft[odd, q : q + 1]
+                column = pull_in * inverse[odd, q // 2 : q // 2 + 1]
                 for r in range(0, piece, step):
-                    e = e_ref[pl.ds(b * BLOCK + c * piece + r, step), :]
+                    s = s_buf[turn % 2, pl.ds(c * piece + r, step), :]
+                    e = jnp.exp2(s * (INV_TAU * LOG2E))
+                    if mine is not None:
+                        first = jnp.where(diag == mine + r, 0.0, e[:, :rows])
+                        e = jnp.concatenate([first, e[:, rows:]], axis=1)
                     value = e * (row_share + column[r : r + step])
-                    pull = row_weight + column[piece + r : piece + r + step]
+                    pull = row_weight + pull_in[r : r + step]
                     value = jnp.where(mates == base + r, value - pull, value)
                     coef[turn % 2, pl.ds(c * piece + r, step), :] = value.astype(jnp.bfloat16)
             left = ncol[pl.ds(b * BLOCK, BLOCK), :].T
@@ -280,35 +310,43 @@
 
     half, both, team = chunks * piece, 2 * rows, 2 * members
     flops = 2 * half * both * width
-    score = pltpu.VMEM((2, BLOCK, both), f32)
-    sums, ncol_far, nrow, e_far = call(
+    scratch = [pltpu.VMEM((2, BLOCK, both), f32), pltpu.VMEM((half, 128), f32)]
+    sums, column, ncol_far, nrow = call(
         functools.partial(far_kernel, sizes),
-        [((2, 8, both), f32), ((half, width), bf16), ((both, width), bf16), ((half, both), f32)],
+        [
+            ((2, 8, both), f32),
+            ((half // 128, 128), f32),
+            ((half, width), bf16),
+            ((both, width), bf16),
+        ],
         (own, oth, far),
-        [score],
+        scratch,
         16,
         flops,
     )
-    msg, ncol_near, e_near = call(
+    msg, cmsg, ncol_near = call(
         functools.partial(near_kernel, sizes),
-        [((team, 8, rows // 2), f32), ((half, width), bf16), ((half, both), f32)],
-        (own, oth, near, heft, sums, nrow),
-        [score],
+        [
+            ((2, 8, rows // 2), f32),
+            ((2 * chunks, 24, 128), bf16),
+            ((half, width), bf16),
+        ],
+        (own, oth, near, heft, sums, column, nrow),
+        scratch,
         16,
         flops,
     )
-    got = exchange(msg, TEAM)
-    info, loss, cw = call(
-        functools.partial(totals_kernel, sizes),
-        [((4, rows), f32), ((1, rows), f32), ((2 * chunks, 1, 2 * piece), f32)],
-        (got, heft),
-    )
-    cw = exchange(cw, OWNERS)
+    got = msg + swap(msg, "zl")
+    cgot = exchange(cmsg, OWNERS)
+    got = got + swap(got, "yl")
+    for apart in (1, 2):
+        got = got + lax.ppermute(got, "x", [(n, n ^ apart) for n in range(sizes["x"])])
+    info, loss = call(totals_kernel, [((4, rows), f32), ((1, rows), f32)], (got,))
     (grads,) = call(
         functools.partial(backward_kernel, sizes),
         [((team, piece, width), bf16)],
-        (own, oth, ncol_far, ncol_near, e_far, e_near, info, cw),
-        [pltpu.VMEM((2, BLOCK, both), bf16), pltpu.VMEM((width, both), f32)],
+        (own, oth, nrow, ncol_far, ncol_near, info, cgot),
+        [pltpu.VMEM((2, BLOCK, both), f32), pltpu.VMEM((2, BLOCK, both), bf16), pltpu.VMEM((width, both), f32)],
         16,
         2 * flops,
     )

time: 111 us -> 116 us (1.045)
  the two profiles are of different devices: /device:TPU:1 before, /device:TPU:32 now
where the time goes in v5:
time: 116 us
  blocking collectives  56.1 us (48%)
  starting transfers between devices  27.6 us (24%)
  waiting for transfers between devices  19.3 us (17%)
  Pallas kernels  11.1 us (10%)
    all_to_all x3, blocking collectives, exchange(): return lax.all_to_all(x, axes, 0, 0, tiled=True)  56.1 us
    ppermute x4, waiting for transfers between devices, swap(): return lax.ppermute(x, axis, [(0, 1), (1, 0)])  14.9 us
    ppermute x4, starting transfers between devices, swap(): return lax.ppermute(x, axis, [(0, 1), (1, 0)])  10.6 us
    pallas_call x4, Pallas kernels, call(): pl.pallas_call(kernel, in_specs=[vmem] * len(args), out_specs=[vmem] * le...  10 us
    all_to_all x1, starting transfers between devices, exchange(): return lax.all_to_all(x, axes, 0, 0, tiled=True)  8.72 us
    ppermute x2, starting transfers between devices, body(): lax.ppermute(got, 'x', [(n, n ^ apart) for n in range(sizes['x'])])  8.3 us
    ppermute x2, waiting for transfers between devices, body(): lax.ppermute(got, 'x', [(n, n ^ apart) for n in range(sizes['x'])])  4.43 us
  transfers between devices with their start and end apart: 7, of which 5 were waited for; matrix products, arithmetic and copies ran while one was open for 0% of the time, Pallas kernels for 2%

profile of v5, /device:TPU:32, one launch (start us, length us, event | category | flops | bytes accessed | tf_op | source)
XLA Modules:
  0.0 115.8 jit_solution(131874972222143949)
XLA Ops:
  0.6 1.0 pack.1
  1.7 32.5 %all_to_all.20.far = bf16[16,64,256]{2,1,0:T(8,128)(2,1)S(1)} all-to-all(bf16[16,64,256]{2,1,0:T(8,128)(2,1)S(1)} %get-tuple-element.15), channel_id=1, replica_groups=mesh['zh'=4,'zl'=2,'yh'=4,'core'=2,'yl'=2,'x'=4] {'yh','zh'}, dimensions={0} | all-to-all | bytes 1048576 | tf_op jit(solution)/shard_map/all_to_all | solution.py:31
  34.2 1.9 %collective-permute-start.1 = (bf16[16,64,256]{2,1,0:T(8,128)(2,1)S(1)}, bf16[16,64,256]{2,1,0:T(8,128)(2,1)S(1)}, u32[]{:S(2)}, u32[]{:S(2)}) collective-permute-start(bf16[16,64,256]{2,1,0:T(8,128)(2,1)S(1)} %all_to_all.20.far), channel_id=1, source_target_pairs={{0,8},{8,0},{1,9},{9,1},{2,10},{10,2},{3,11},{11,3},{4,12},{12,4},... | collective-permute-start | bytes 1572872 | tf_op jit(solution)/shard_map/ppermute | solution.py:27
  36.1 3.9 %collective-permute-start = (bf16[528,256]{1,0:T(8,128)(2,1)S(1)}, bf16[528,256]{1,0:T(8,128)(2,1)S(1)}, u32[]{:S(2)}, u32[]{:S(2)}) collective-permute-start(bf16[528,256]{1,0:T(8,128)(2,1)S(1)} %get-tuple-element.14.own), channel_id=1, source_target_pairs={{0,64},{64,0},{1,65},{65,1},{2,66},{66,2},{3,67},{67,3},{4,68},{68... | collective-permute-start | bytes 811016 | tf_op jit(solution)/shard_map/ppermute | solution.py:27
  40.0 7.1 %collective-permute-done.oth = bf16[528,256]{1,0:T(8,128)(2,1)S(1)} collective-permute-done((bf16[528,256]{1,0:T(8,128)(2,1)S(1)}, bf16[528,256]{1,0:T(8,128)(2,1)S(1)}, u32[]{:S(2)}, u32[]{:S(2)}) %collective-permute-start) | collective-permute-done | bytes 270368 | tf_op jit(solution)/shard_map/ppermute | solution.py:27
  47.1 2.0 %shard_map.50 = (f32[2,8,1024]{2,1,0:T(8,128)S(1)}, f32[8,128]{1,0:T(8,128)S(1)}, bf16[1024,256]{1,0:T(8,128)(2,1)S(1)}, bf16[1024,256]{1,0:T(8,128)(2,1)S(1)}) custom-call(bf16[528,256]{1,0:T(8,128)(2,1)S(1)} %get-tuple-element.14.own, bf16[528,256]{1,0:T(8,128)(2,1)S(1)} %collective-permute-done.oth, bf16[16,64,256]{2,1,0:T(8,128)(2,1)S(1)} %all_to_all.20.far), custom_call_target="tpu_custom_call" | custom-call | flops 536870912 | bytes 1048576 | tf_op jit(solution)/shard_map/pallas_call | solution.py:269
  49.1 0.0 collective-permute-done.1.near
  49.2 2.1 %shard_map.51 = (f32[2,8,256]{2,1,0:T(8,128)S(1)}, bf16[32,24,128]{2,1,0:T(8,128)(2,1)}, bf16[1024,256]{1,0:T(8,128)(2,1)S(1)}) custom-call(bf16[528,256]{1,0:T(8,128)(2,1)S(1)} %get-tuple-element.14.own, bf16[528,256]{1,0:T(8,128)(2,1)S(1)} %collective-permute-done.oth, bf16[16,64,256]{2,1,0:T(8,128)(2,1)S(1)} %collective-permute-done.1.near, ...), custom_call_target="tpu_custom_call" | custom-call | flops 536870912 | bytes 1048576 | tf_op jit(solution)/shard_map/pallas_call | solution.py:269
  51.3 8.7 %all-to-all-start.1 = ((bf16[32,24,128]{2,1,0:T(8,128)(2,1)}), bf16[32,24,128]{2,1,0:T(8,128)(2,1)S(1)}, u32[]{:S(2)}, u32[]{:S(2)}) async-start(bf16[32,24,128]{2,1,0:T(8,128)(2,1)} %get-tuple-element.25), calls=%async_computation.1 | async-start | bytes 393216 | tf_op jit(solution)/shard_map/all_to_all | solution.py:31
  60.0 2.9 %collective-permute-start.2 = (f32[2,8,256]{2,1,0:T(8,128)S(1)}, f32[2,8,256]{2,1,0:T(8,128)S(1)}, u32[]{:S(2)}, u32[]{:S(2)}) collective-permute-start(f32[2,8,256]{2,1,0:T(8,128)S(1)} %get-tuple-element.20), channel_id=1, source_target_pairs={{0,64},{64,0},{1,65},{65,1},{2,66},{66,2},{3,67},{67,3},{4,68},{68... | collective-permute-start | bytes 49160 | tf_op jit(solution)/shard_map/ppermute | solution.py:27
  62.9 4.0 %collective-permute-done.2 = f32[2,8,256]{2,1,0:T(8,128)S(1)} collective-permute-done((f32[2,8,256]{2,1,0:T(8,128)S(1)}, f32[2,8,256]{2,1,0:T(8,128)S(1)}, u32[]{:S(2)}, u32[]{:S(2)}) %collective-permute-start.2) | collective-permute-done | bytes 16416 | tf_op jit(solution)/shard_map/ppermute | solution.py:27
  67.0 1.9 %collective-permute-start.3 = (f32[2,8,256]{2,1,0:T(8,128)S(1)}, f32[2,8,256]{2,1,0:T(8,128)S(1)}, u32[]{:S(2)}, u32[]{:S(2)}) collective-permute-start(f32[2,8,256]{2,1,0:T(8,128)S(1)} %add.12), channel_id=1, source_target_pairs={{0,4},{4,0},{1,5},{5,1},{2,6},{6,2},{3,7},{7,3},{8,12},{12,8},{9,1... | collective-permute-start | bytes 49160 | tf_op jit(solution)/shard_map/ppermute | solution.py:27
  68.9 3.7 %collective-permute-done.3 = f32[2,8,256]{2,1,0:T(8,128)S(1)} collective-permute-done((f32[2,8,256]{2,1,0:T(8,128)S(1)}, f32[2,8,256]{2,1,0:T(8,128)S(1)}, u32[]{:S(2)}, u32[]{:S(2)}) %collective-permute-start.3) | collective-permute-done | bytes 16416 | tf_op jit(solution)/shard_map/ppermute | solution.py:27
  72.6 3.4 %collective-permute-start.4 = (f32[2,8,256]{2,1,0:T(8,128)S(1)}, f32[2,8,256]{2,1,0:T(8,128)S(1)}, u32[]{:S(2)}, u32[]{:S(2)}) collective-permute-start(f32[2,8,256]{2,1,0:T(8,128)S(1)} %add.13), channel_id=1, source_target_pairs={{0,1},{1,0},{2,3},{3,2},{4,5},{5,4},{6,7},{7,6},{8,9},{9,8},{10,11... | collective-permute-start | bytes 49160 | tf_op jit(solution)/shard_map/ppermute | solution.py:343
  76.0 2.2 %collective-permute-done.4 = f32[2,8,256]{2,1,0:T(8,128)S(1)} collective-permute-done((f32[2,8,256]{2,1,0:T(8,128)S(1)}, f32[2,8,256]{2,1,0:T(8,128)S(1)}, u32[]{:S(2)}, u32[]{:S(2)}) %collective-permute-start.4) | collective-permute-done | bytes 16416 | tf_op jit(solution)/shard_map/ppermute | solution.py:343
  78.2 4.9 %collective-permute-start.5 = (f32[2,8,256]{2,1,0:T(8,128)S(1)}, f32[2,8,256]{2,1,0:T(8,128)S(1)}, u32[]{:S(2)}, u32[]{:S(2)}) collective-permute-start(f32[2,8,256]{2,1,0:T(8,128)S(1)} %add.14), channel_id=1, source_target_pairs={{0,2},{1,3},{2,0},{3,1},{4,6},{5,7},{6,4},{7,5},{8,10},{9,11},{10,... | collective-permute-start | bytes 49160 | tf_op jit(solution)/shard_map/ppermute | solution.py:343
  83.1 2.2 %collective-permute-done.5 = f32[2,8,256]{2,1,0:T(8,128)S(1)} collective-permute-done((f32[2,8,256]{2,1,0:T(8,128)S(1)}, f32[2,8,256]{2,1,0:T(8,128)S(1)}, u32[]{:S(2)}, u32[]{:S(2)}) %collective-permute-start.5) | collective-permute-done | bytes 16416 | tf_op jit(solution)/shard_map/ppermute | solution.py:343
  85.4 0.6 shard_map.52
  86.0 0.0 all-to-all-done.1.cgot
  86.0 5.3 %shard_map.53 = bf16[16,64,256]{2,1,0:T(8,128)(2,1)S(1)} custom-call(bf16[528,256]{1,0:T(8,128)(2,1)S(1)} %get-tuple-element.14.own, bf16[528,256]{1,0:T(8,128)(2,1)S(1)} %collective-permute-done.oth, bf16[1024,256]{1,0:T(8,128)(2,1)S(1)} %get-tuple-element.19.nrow, bf16[1024,256]{1,0:T(8,128)(2,1)S(1)} %get-tuple-element.22.ncol_far, ...), custom_call_target="tpu_custom_call" | custom-call | flops 1073741824 | bytes 1048576 | tf_op jit(solution)/shard_map/pallas_call | solution.py:269
  91.2 14.0 %all_to_all.21 = bf16[16,64,256]{2,1,0:T(8,128)(2,1)S(1)} all-to-all(bf16[16,64,256]{2,1,0:T(8,128)(2,1)S(1)} %shard_map.53), channel_id=1, replica_groups=mesh['zh'=4,'zl'=2,'yh'=4,'core'=2,'yl'=2,'x'=4] {'zl','yl','x'}, dimensions={0} | all-to-all | bytes 1048576 | tf_op jit(solution)/shard_map/all_to_all | solution.py:31
  105.2 0.1 reduce_sum.12
  105.3 9.6 %all_to_all.22 = bf16[8,64,256]{2,1,0:T(8,128)(2,1)S(1)} all-to-all(bf16[8,64,256]{2,1,0:T(8,128)(2,1)S(1)} %broadcast_in_dim.2), channel_id=1, replica_groups=mesh['zh'=4,'zl'=2,'yh'=4,'core'=2,'yl'=2,'x'=4] {'yl','x'}, dimensions={0} | all-to-all | bytes 524288 | tf_op jit(solution)/shard_map/all_to_all | solution.py:31
  114.9 0.8 bitcast_convert_fusion
  (5 shorter events, 0.0 us)
Async XLA Ops:
  34.2 14.9 %collective-permute-start.1 = (bf16[16,64,256]{2,1,0:T(8,128)(2,1)S(1)}, bf16[16,64,256]{2,1,0:T(8,128)(2,1)S(1)}, u32[]{:S(2)}, u32[]{:S(2)}) collective-permute-start(bf16[16,64,256]{2,1,0:T(8,128)(2,1)S(1)} %all_to_all.20.far), channel_id=1, source_target_pairs={{0,8},{8,0},{1,9},{9,1},{2,10},{10,2},{3,11},{11,3},{4,12},{12,4},... | collective-permute-start | bytes 1572872 | tf_op jit(solution)/shard_map/ppermute | solution.py:27
  36.1 11.0 %collective-permute-start = (bf16[528,256]{1,0:T(8,128)(2,1)S(1)}, bf16[528,256]{1,0:T(8,128)(2,1)S(1)}, u32[]{:S(2)}, u32[]{:S(2)}) collective-permute-start(bf16[528,256]{1,0:T(8,128)(2,1)S(1)} %get-tuple-element.14.own), channel_id=1, source_target_pairs={{0,64},{64,0},{1,65},{65,1},{2,66},{66,2},{3,67},{67,3},{4,68},{68... | collective-permute-start | bytes 811016 | tf_op jit(solution)/shard_map/ppermute | solution.py:27
  51.3 34.7 %all-to-all-start.1 = ((bf16[32,24,128]{2,1,0:T(8,128)(2,1)}), bf16[32,24,128]{2,1,0:T(8,128)(2,1)S(1)}, u32[]{:S(2)}, u32[]{:S(2)}) async-start(bf16[32,24,128]{2,1,0:T(8,128)(2,1)} %get-tuple-element.25), calls=%async_computation.1 | async-start | bytes 393216 | tf_op jit(solution)/shard_map/all_to_all | solution.py:31
  60.0 6.9 %collective-permute-start.2 = (f32[2,8,256]{2,1,0:T(8,128)S(1)}, f32[2,8,256]{2,1,0:T(8,128)S(1)}, u32[]{:S(2)}, u32[]{:S(2)}) collective-permute-start(f32[2,8,256]{2,1,0:T(8,128)S(1)} %get-tuple-element.20), channel_id=1, source_target_pairs={{0,64},{64,0},{1,65},{65,1},{2,66},{66,2},{3,67},{67,3},{4,68},{68... | collective-permute-start | bytes 49160 | tf_op jit(solution)/shard_map/ppermute | solution.py:27
  67.0 5.6 %collective-permute-start.3 = (f32[2,8,256]{2,1,0:T(8,128)S(1)}, f32[2,8,256]{2,1,0:T(8,128)S(1)}, u32[]{:S(2)}, u32[]{:S(2)}) collective-permute-start(f32[2,8,256]{2,1,0:T(8,128)S(1)} %add.12), channel_id=1, source_target_pairs={{0,4},{4,0},{1,5},{5,1},{2,6},{6,2},{3,7},{7,3},{8,12},{12,8},{9,1... | collective-permute-start | bytes 49160 | tf_op jit(solution)/shard_map/ppermute | solution.py:27
  72.6 5.6 %collective-permute-start.4 = (f32[2,8,256]{2,1,0:T(8,128)S(1)}, f32[2,8,256]{2,1,0:T(8,128)S(1)}, u32[]{:S(2)}, u32[]{:S(2)}) collective-permute-start(f32[2,8,256]{2,1,0:T(8,128)S(1)} %add.13), channel_id=1, source_target_pairs={{0,1},{1,0},{2,3},{3,2},{4,5},{5,4},{6,7},{7,6},{8,9},{9,8},{10,11... | collective-permute-start | bytes 49160 | tf_op jit(solution)/shard_map/ppermute | solution.py:343
  78.2 7.1 %collective-permute-start.5 = (f32[2,8,256]{2,1,0:T(8,128)S(1)}, f32[2,8,256]{2,1,0:T(8,128)S(1)}, u32[]{:S(2)}, u32[]{:S(2)}) collective-permute-start(f32[2,8,256]{2,1,0:T(8,128)S(1)} %add.14), channel_id=1, source_target_pairs={{0,2},{1,3},{2,0},{3,1},{4,6},{5,7},{6,4},{7,5},{8,10},{9,11},{10,... | collective-permute-start | bytes 49160 | tf_op jit(solution)/shard_map/ppermute | solution.py:343

commit v6 on v4

--- a/solution.py
+++ b/solution.py
@@ -14,9 +14,9 @@
 LOG2E = 1.4426950408889634
 
 DP = ("zh", "zl", "yh", "core")
-MP = ("yl", "x")
+MP = ("x", "yl")
 FAR = ("yh", "zh")
-TEAM = ("zl", "yl", "x")
+TEAM = ("zl", "x", "yl")
 OWNERS = ("core", "yh", "zh")
 
 BLOCK = 256
@@ -234,6 +234,18 @@
         msg[pl.ds(to * members, members)] = out.astype(jnp.bfloat16).reshape(members, -1, width)
 
 
+def finish_kernel(got, out, wide, stored):
+    piece = got.shape[1]
+    copies = []
+    for n in range(got.shape[0]):
+        at = pl.ds(n * piece, piece)
+        wide[at, :] = got[n].astype(jnp.float32)
+        copies.append(pltpu.make_async_copy(wide.at[at], out.at[at], stored.at[n]))
+        copies[-1].start()
+    for copy in copies:
+        copy.wait()
+
+
 def call(kernel, outs, args, scratch=(), mib=4, flops=0):
     vmem = pl.BlockSpec(memory_space=pltpu.VMEM)
     return pl.pallas_call(
@@ -314,8 +326,17 @@
     )
     shares = exchange(grads, TEAM)
     share = jnp.sum(shares.astype(f32), axis=0).astype(bf16)
-    grad = exchange(jnp.broadcast_to(share[None], (members, piece, width)), MP)
-    return loss.reshape(rows), grad.astype(f32).reshape(rows, width)
+    got = exchange(jnp.broadcast_to(share[None], (members, piece, width)), MP)
+    grad = pl.pallas_call(
+        finish_kernel,
+        name="finish",
+        in_specs=[pl.BlockSpec(memory_space=pltpu.VMEM)],
+        out_specs=pl.BlockSpec(memory_space=pltpu.HBM),
+        out_shape=jax.ShapeDtypeStruct((rows, width), f32),
+        scratch_shapes=[pltpu.VMEM((rows, width), f32), pltpu.SemaphoreType.DMA((members,))],
+        compiler_params=pltpu.CompilerParams(vmem_limit_bytes=4 << 20),
+    )(got)
+    return loss.reshape(rows), grad
 
 
 def solution(mesh):

time: 111 us -> 111 us (level); the launches traced: 111 us -> 109 us
  blocking collectives: 87.5 us -> 86.1 us
    all_to_all x5, blocking collectives: 87.5 us -> 86.1 us  [exchange(): return lax.all_to_all(x, axes, 0, 0, tiled=True)]
where the time goes in v6:
time: 111 us; the launch traced here: 109 us
  blocking collectives  86.1 us (78%)
  Pallas kernels  9.05 us (8%)
  waiting for transfers between devices  7.56 us (7%)
  starting transfers between devices  6.02 us (5%)
    all_to_all x5, blocking collectives, exchange(): return lax.all_to_all(x, axes, 0, 0, tiled=True)  86.1 us
    ppermute x2, waiting for transfers between devices, swap(): return lax.ppermute(x, axis, [(0, 1), (1, 0)])  7.56 us
    pallas_call x4, Pallas kernels, call(): pl.pallas_call(kernel, in_specs=[vmem] * len(args), out_specs=[vmem] * le...  7.15 us
    ppermute x2, starting transfers between devices, swap(): return lax.ppermute(x, axis, [(0, 1), (1, 0)])  6.02 us
  transfers between devices with their start and end apart: 2, of which 1 were waited for; matrix products, arithmetic and copies ran while one was open for 0% of the time, Pallas kernels for 2%

profile of v6, /device:TPU:1, one launch (start us, length us, event | category | flops | bytes accessed | tf_op | source)
XLA Modules:
  0.0 109.5 jit_solution(11997231068077858738)
XLA Ops:
  0.6 1.0 pack.1
  1.7 36.5 %all_to_all.25.far = bf16[16,64,256]{2,1,0:T(8,128)(2,1)S(1)} all-to-all(bf16[16,64,256]{2,1,0:T(8,128)(2,1)S(1)} %get-tuple-element.16), channel_id=1, replica_groups=mesh['zh'=4,'zl'=2,'yh'=4,'core'=2,'yl'=2,'x'=4] {'yh','zh'}, dimensions={0} | all-to-all | bytes 1048576 | tf_op jit(solution)/shard_map/all_to_all | solution.py:31
  38.2 3.7 %collective-permute-start.1 = (bf16[16,64,256]{2,1,0:T(8,128)(2,1)S(1)}, bf16[16,64,256]{2,1,0:T(8,128)(2,1)S(1)}, u32[]{:S(2)}, u32[]{:S(2)}) collective-permute-start(bf16[16,64,256]{2,1,0:T(8,128)(2,1)S(1)} %all_to_all.25.far), channel_id=1, source_target_pairs={{0,8},{8,0},{1,9},{9,1},{2,10},{10,2},{3,11},{11,3},{4,12},{12,4},... | collective-permute-start | bytes 1572872 | tf_op jit(solution)/shard_map/ppermute | solution.py:27
  41.9 2.4 %collective-permute-start = (bf16[528,256]{1,0:T(8,128)(2,1)S(1)}, bf16[528,256]{1,0:T(8,128)(2,1)S(1)}, u32[]{:S(2)}, u32[]{:S(2)}) collective-permute-start(bf16[528,256]{1,0:T(8,128)(2,1)S(1)} %get-tuple-element.15.own), channel_id=1, source_target_pairs={{0,64},{64,0},{1,65},{65,1},{2,66},{66,2},{3,67},{67,3},{4,68},{68... | collective-permute-start | bytes 811016 | tf_op jit(solution)/shard_map/ppermute | solution.py:27
  44.2 7.6 %collective-permute-done.oth = bf16[528,256]{1,0:T(8,128)(2,1)S(1)} collective-permute-done((bf16[528,256]{1,0:T(8,128)(2,1)S(1)}, bf16[528,256]{1,0:T(8,128)(2,1)S(1)}, u32[]{:S(2)}, u32[]{:S(2)}) %collective-permute-start) | collective-permute-done | bytes 270368 | tf_op jit(solution)/shard_map/ppermute | solution.py:27
  51.8 1.8 %shard_map.50 = (f32[2,8,1024]{2,1,0:T(8,128)S(1)}, bf16[1024,256]{1,0:T(8,128)(2,1)S(1)}, bf16[1024,256]{1,0:T(8,128)(2,1)S(1)}, f32[1024,1024]{1,0:T(8,128)S(1)}) custom-call(bf16[528,256]{1,0:T(8,128)(2,1)S(1)} %get-tuple-element.15.own, bf16[528,256]{1,0:T(8,128)(2,1)S(1)} %collective-permute-done.oth, bf16[16,64,256]{2,1,0:T(8,128)(2,1)S(1)} %all_to_all.25.far), custom_call_target="tpu_custom_call" | custom-call | flops 536870912 | bytes 1048576 | tf_op jit(solution)/shard_map/pallas_call | solution.py:251
  53.6 0.0 collective-permute-done.1.near
  53.6 1.4 %shard_map.51 = (f32[16,8,256]{2,1,0:T(8,128)S(1)}, bf16[1024,256]{1,0:T(8,128)(2,1)S(1)}, f32[1024,1024]{1,0:T(8,128)S(1)}) custom-call(bf16[528,256]{1,0:T(8,128)(2,1)S(1)} %get-tuple-element.15.own, bf16[528,256]{1,0:T(8,128)(2,1)S(1)} %collective-permute-done.oth, bf16[16,64,256]{2,1,0:T(8,128)(2,1)S(1)} %collective-permute-done.1.near, ...), custom_call_target="tpu_custom_call" | custom-call | flops 536870912 | bytes 1048576 | tf_op jit(solution)/shard_map/pallas_call | solution.py:251
  55.0 10.1 %all_to_all.26.got = f32[16,8,256]{2,1,0:T(8,128)S(1)} all-to-all(f32[16,8,256]{2,1,0:T(8,128)S(1)} %get-tuple-element.20), channel_id=1, replica_groups=mesh['zh'=4,'zl'=2,'yh'=4,'core'=2,'yl'=2,'x'=4] {'zl','x','yl'}, dimensions={0} | all-to-all | bytes 262144 | tf_op jit(solution)/shard_map/all_to_all | solution.py:31
  65.0 0.6 shard_map.52
  65.7 18.6 %all_to_all.27.cw = f32[32,1,128]{2,1,0:T(1,128)S(1)} all-to-all(f32[32,1,128]{2,1,0:T(1,128)S(1)} %get-tuple-element.27), channel_id=1, replica_groups=mesh['zh'=4,'zl'=2,'yh'=4,'core'=2,'yl'=2,'x'=4] {'core','yh','zh'}, dimensions={0} | all-to-all | bytes 32768 | tf_op jit(solution)/shard_map/all_to_all | solution.py:31
  84.3 3.4 %shard_map.53 = bf16[16,64,256]{2,1,0:T(8,128)(2,1)S(1)} custom-call(bf16[528,256]{1,0:T(8,128)(2,1)S(1)} %get-tuple-element.15.own, bf16[528,256]{1,0:T(8,128)(2,1)S(1)} %collective-permute-done.oth, bf16[1024,256]{1,0:T(8,128)(2,1)S(1)} %get-tuple-element.22.ncol_far, bf16[1024,256]{1,0:T(8,128)(2,1)S(1)} %get-tuple-element.23.ncol_near, ...), custom_call_target="tpu_custom_call" | custom-call | flops 1073741824 | bytes 1048576 | tf_op jit(solution)/shard_map/pallas_call | solution.py:251
  87.7 11.6 %all_to_all.28 = bf16[16,64,256]{2,1,0:T(8,128)(2,1)S(1)} all-to-all(bf16[16,64,256]{2,1,0:T(8,128)(2,1)S(1)} %shard_map.53), channel_id=1, replica_groups=mesh['zh'=4,'zl'=2,'yh'=4,'core'=2,'yl'=2,'x'=4] {'zl','x','yl'}, dimensions={0} | all-to-all | bytes 1048576 | tf_op jit(solution)/shard_map/all_to_all | solution.py:31
  99.3 0.1 reduce_sum.12
  99.4 9.2 %all_to_all.29.got = bf16[8,64,256]{2,1,0:T(8,128)(2,1)S(1)} all-to-all(bf16[8,64,256]{2,1,0:T(8,128)(2,1)S(1)} %broadcast_in_dim.2), channel_id=1, replica_groups=mesh['zh'=4,'zl'=2,'yh'=4,'core'=2,'yl'=2,'x'=4] {'x','yl'}, dimensions={0} | all-to-all | bytes 524288 | tf_op jit(solution)/shard_map/all_to_all | solution.py:31
  108.6 0.9 finish.1
  (1 shorter events, 0.0 us)
Async XLA Ops:
  38.2 15.4 %collective-permute-start.1 = (bf16[16,64,256]{2,1,0:T(8,128)(2,1)S(1)}, bf16[16,64,256]{2,1,0:T(8,128)(2,1)S(1)}, u32[]{:S(2)}, u32[]{:S(2)}) collective-permute-start(bf16[16,64,256]{2,1,0:T(8,128)(2,1)S(1)} %all_to_all.25.far), channel_id=1, source_target_pairs={{0,8},{8,0},{1,9},{9,1},{2,10},{10,2},{3,11},{11,3},{4,12},{12,4},... | collective-permute-start | bytes 1572872 | tf_op jit(solution)/shard_map/ppermute | solution.py:27
  41.9 9.9 %collective-permute-start = (bf16[528,256]{1,0:T(8,128)(2,1)S(1)}, bf16[528,256]{1,0:T(8,128)(2,1)S(1)}, u32[]{:S(2)}, u32[]{:S(2)}) collective-permute-start(bf16[528,256]{1,0:T(8,128)(2,1)S(1)} %get-tuple-element.15.own), channel_id=1, source_target_pairs={{0,64},{64,0},{1,65},{65,1},{2,66},{66,2},{3,67},{67,3},{4,68},{68... | collective-permute-start | bytes 811016 | tf_op jit(solution)/shard_map/ppermute | solution.py:27

commit v7 on v5

--- a/solution.py
+++ b/solution.py
@@ -14,9 +14,9 @@
 LOG2E = 1.4426950408889634
 
 DP = ("zh", "zl", "yh", "core")
-MP = ("yl", "x")
+MP = ("x", "yl")
 FAR = ("yh", "zh")
-TEAM = ("zl", "yl", "x")
+TEAM = ("zl", "x", "yl")
 OWNERS = ("core", "yh", "zh")
 
 BLOCK = 256
@@ -52,6 +52,29 @@
         return base, None
     mine = jnp.logical_and(yh == its_yh, zh == its_zh)
     return base, jnp.where(mine, slot * piece, -(1 << 20))
+
+
+def triple(x):
+    high = x.astype(jnp.bfloat16).astype(jnp.float32)
+    rest = x - high
+    middle = rest.astype(jnp.bfloat16).astype(jnp.float32)
+    return high, middle, rest - middle
+
+
+def row_weights(refs, rows):
+    parts = []
+    for ref in refs:
+        tail = ref[pl.ds(rows, 16), :].astype(jnp.float32)
+        pair = tail[4:6] + tail[6:8] + tail[8:10]
+        parts += [pair[n : n + 1] for n in range(pair.shape[0])]
+    return jnp.concatenate(parts, axis=1)
+
+
+def chosen(row, slot, piece):
+    mine = row[:, :piece]
+    for n in range(1, row.shape[1] // piece):
+        mine = jnp.where(slot == n, row[:, n * piece : (n + 1) * piece], mine)
+    return mine
 
 
 def partner_ids(own_ref, oth_ref, rows):
@@ -76,19 +99,22 @@
     ids = mates[...]
     half_row = rows // 2
     parts = [x[:, n * half_row : (n + 1) * half_row] for x in (ids >> 8, ids & 255) for n in (0, 1)]
-    blank = jnp.zeros((own.shape[0] - rows - 4, half_row), jnp.int32)
-    packed = jnp.concatenate(parts + [blank], axis=0).astype(jnp.float32)
+    parts = [x.astype(jnp.float32) for x in parts]
+    last.wait()
+    for x in triple(heft[...]):
+        parts += [x[:, n * half_row : (n + 1) * half_row] for n in (0, 1)]
+    parts.append(jnp.zeros((own.shape[0] - rows - len(parts), half_row), jnp.float32))
+    packed = jnp.concatenate(parts, axis=0)
     own[pl.ds(rows, own.shape[0] - rows), :] = packed.astype(jnp.bfloat16)
     slot = lax.axis_index(MP)
     copy.wait()
-    last.wait()
     mine = own[pl.ds(pl.multiple_of(slot * piece, piece), piece), :]
     for n in range(spread.shape[0]):
         spread[n] = mine
 
 
 def forward_half(
-    sizes, at, near, source, ids, nrow, ncol, s_buf, lanes, total, positive
+    sizes, at, near, source, ids, nrow, ncol, e_out, s_buf, lanes, total, positive
 ):
     chunks, piece = source.shape[0], source.shape[1]
     both = nrow.shape[0]
@@ -115,6 +141,7 @@
                     first = jnp.where(diag == mine + r, 0.0, e[:, :rows])
                     e = jnp.concatenate([first, e[:, rows:]], axis=1)
                 here = pl.ds(b * BLOCK + c * piece + r, step)
+                e_out[here, :] = e
                 across = e[:, :128]
                 for n in range(128, both, 128):
                     across = across + e[:, n : n + 128]
@@ -128,7 +155,7 @@
     return total, positive, jnp.concatenate(column, axis=0)
 
 
-def far_kernel(sizes, own, oth, far, sums, column, ncol, nrow, s_buf, lanes):
+def far_kernel(sizes, own, oth, far, sums, column, ncol, nrow, e_out, s_buf, lanes):
     rows = nrow.shape[0] // 2
     for at, source in ((0, own[0:rows, :]), (rows, oth[0:rows, :])):
         floats, _, inverse = scaled(source)
@@ -136,27 +163,27 @@
     ids = partner_ids(own, oth, rows)
     zero = jnp.zeros((8, 2 * rows), jnp.float32)
     total, positive, column[...] = forward_half(
-        sizes, place(), False, far, ids, nrow, ncol, s_buf, lanes, zero, zero
+        sizes, place(), False, far, ids, nrow, ncol, e_out, s_buf, lanes, zero, zero
     )
     sums[0] = total
     sums[1] = positive
 
 
 def near_kernel(
-    sizes, own, oth, near, weight, sums, column, nrow, msg, cmsg, ncol, s_buf, lanes
+    sizes, own, oth, near, weight, sums, column, nrow, scores, cmsg, ncol, e_out, s_buf, lanes
 ):
     rows = nrow.shape[0] // 2
     at = place()
     ids = partner_ids(own, oth, rows)
     total, positive, last = forward_half(
-        sizes, at, True, near, ids, nrow, ncol, s_buf, lanes, sums[0], sums[1]
-    )
-    members = sizes["mp"]
-    piece = rows // members
-    _, zl, _, core, slot = at
-    mine = jnp.zeros((1, piece), jnp.float32)
-    for n in range(members):
-        mine = jnp.where(slot == n, weight[:, n * piece : (n + 1) * piece], mine)
+        sizes, at, True, near, ids, nrow, ncol, e_out, s_buf, lanes, sums[0], sums[1]
+    )
+    total = jnp.sum(total, axis=0, keepdims=True)
+    positive = jnp.sum(positive, axis=0, keepdims=True) * INV_TAU
+    scores[...] = jnp.concatenate([total, positive], axis=0)
+    piece = rows // sizes["mp"]
+    core, slot = at[3], at[4]
+    mine = chosen(weight[...], slot, piece)
     coarse = mine.astype(jnp.bfloat16).astype(jnp.float32)
     fine = jnp.concatenate([coarse, mine - coarse], axis=1)
     first = jnp.where(core == 0, column[...], last)
@@ -166,39 +193,11 @@
     for n in range(cmsg.shape[0]):
         cmsg[n] = packed
 
-    total = jnp.sum(total, axis=0, keepdims=True)
-    positive = jnp.sum(positive, axis=0, keepdims=True) * INV_TAU
-    heft = jnp.where(slot == 0, weight[...], 0.0)
-    none = jnp.zeros_like(heft)
-    half_row = rows // 2
-    for to, parts in (
-        (zl, [total[:, :rows], positive[:, :rows], heft, none]),
-        (1 - zl, [total[:, rows:], positive[:, rows:], none, none]),
-    ):
-        msg[to] = jnp.concatenate(
-            [p[:, n * half_row : (n + 1) * half_row] for p in parts for n in range(2)], axis=0
-        )
-
-
-def totals_kernel(got, info, loss):
-    zl = place()[1]
-
-    def joined(group, n):
-        return jnp.concatenate([group[n : n + 1], group[n + 1 : n + 2]], axis=1)
-
-    own, other = got[zl], got[1 - zl]
-    total, own_weight = joined(own, 0), joined(own, 4)
-    other_weight = joined(other, 4)
-    loss[...] = jnp.log(total) - joined(own, 2)
-    info[...] = jnp.concatenate(
-        [own_weight / total, other_weight / joined(other, 0), own_weight, other_weight], axis=0
-    )
-
 
 def backward_kernel(
-    sizes, own, oth, nrow, ncol_far, ncol_near, info, cgot, msg, s_buf, coef, acc
+    sizes, own, oth, ncol_far, ncol_near, e_far, e_near, scores, cgot, msg, near_coef, coef, acc
 ):
-    both, width = acc.shape[1], acc.shape[0]
+    both, width = acc.shape[2], acc.shape[1]
     rows = both // 2
     chunks = cgot.shape[0] // 2
     half = ncol_far.shape[0]
@@ -206,20 +205,14 @@
     step = 16
     at = place()
     ids = partner_ids(own, oth, rows)
-    sub = lax.broadcasted_iota(jnp.int32, (step, both), 0)
-    mates = jnp.broadcast_to(ids, (step, both)) - sub
-    diag = lax.broadcasted_iota(jnp.int32, (step, rows), 1) - sub[:, :rows]
-    right = nrow[...]
-    row_share = jnp.concatenate([info[0:1, :], info[1:2, :]], axis=1)
-    row_weight = jnp.concatenate([info[2:3, :], info[3:4, :]], axis=1)
-    row_share = jnp.broadcast_to(row_share, (step, both))
-    row_weight = jnp.broadcast_to(row_weight, (step, both))
+    mates = jnp.broadcast_to(ids, (step, both)) - lax.broadcasted_iota(jnp.int32, (step, both), 0)
+    row_weight = jnp.broadcast_to(row_weights((own, oth), rows), (step, both))
     column_total = cgot[0, 0:16, :].astype(jnp.float32)
     for n in range(1, 2 * chunks):
         column_total = column_total + cgot[n, 0:16, :].astype(jnp.float32)
     inverse_total = 1.0 / column_total
     turn = 0
-    for near, ncol in ((False, ncol_far), (True, ncol_near)):
+    for near, ncol, e_ref in ((False, ncol_far, e_far), (True, ncol_near, e_near)):
         core = 1 - at[3] if near else at[3]
         inverse = jnp.where(core == 0, inverse_total[0:8], inverse_total[8:16]).T
         heft = []
@@ -228,40 +221,92 @@
             heft.append(row + jnp.concatenate([row[:, piece:], row[:, :piece]], axis=1))
         heft = jnp.concatenate(heft, axis=0).T
         for b in range(half // BLOCK):
-            s_buf[turn % 2] = lax.dot_general(
-                ncol[pl.ds(b * BLOCK, BLOCK), :], right, NT, preferred_element_type=jnp.float32
-            )
             for c in range(BLOCK // piece):
                 q = b * (BLOCK // piece) + c
-                base, mine = chunk_scalars(at, q, near, piece, sizes)
+                base, _ = chunk_scalars(at, q, near, piece, sizes)
                 odd = slice(q % 2 * piece, (q % 2 + 1) * piece)
                 pull_in = heft[odd, q : q + 1]
                 column = pull_in * inverse[odd, q // 2 : q // 2 + 1]
                 for r in range(0, piece, step):
-                    s = s_buf[turn % 2, pl.ds(c * piece + r, step), :]
-                    e = jnp.exp2(s * (INV_TAU * LOG2E))
-                    if mine is not None:
-                        first = jnp.where(diag == mine + r, 0.0, e[:, :rows])
-                        e = jnp.concatenate([first, e[:, rows:]], axis=1)
-                    value = e * (row_share + column[r : r + step])
+                    here = pl.ds(c * piece + r, step)
+                    e = e_ref[pl.ds(b * BLOCK + c * piece + r, step), :]
+                    near_coef[turn % 2, here, :] = e.astype(jnp.bfloat16)
+                    value = e * column[r : r + step]
                     pull = row_weight + pull_in[r : r + step]
                     value = jnp.where(mates == base + r, value - pull, value)
-                    coef[turn % 2, pl.ds(c * piece + r, step), :] = value.astype(jnp.bfloat16)
+                    coef[turn % 2, here, :] = value.astype(jnp.bfloat16)
             left = ncol[pl.ds(b * BLOCK, BLOCK), :].T
-            product = jnp.dot(left, coef[turn % 2], preferred_element_type=jnp.float32)
-            if turn == 0:
-                acc[...] = product
-            else:
-                acc[...] += product
+            for which, right in enumerate((near_coef, coef)):
+                product = jnp.dot(left, right[turn % 2], preferred_element_type=jnp.float32)
+                if turn == 0:
+                    acc[which] = product
+                else:
+                    acc[which] += product
             turn += 1
     zl = at[1]
     members = sizes["mp"]
+    own_rows = rows // members
+    none = jnp.zeros((1, width - 3 * own_rows), jnp.float32)
+    blank = jnp.zeros((6, width), jnp.float32)
     for to, first, source in ((zl, 0, own[0:rows, :]), (1 - zl, rows, oth[0:rows, :])):
         floats, _, inverse = scaled(source)
-        g = acc[:, first : first + rows].T * INV_TAU
         unit = floats * inverse
-        out = (g - unit * jnp.sum(unit * g, axis=1, keepdims=True)) * inverse
-        msg[pl.ds(to * members, members)] = out.astype(jnp.bfloat16).reshape(members, -1, width)
+        lot = pl.ds(to * members, members)
+        for which in range(2):
+            g = acc[which, :, first : first + rows].T * INV_TAU
+            out = (g - unit * jnp.sum(unit * g, axis=1, keepdims=True)) * inverse
+            out = out.astype(jnp.bfloat16).reshape(members, own_rows, width)
+            msg[lot, which * own_rows : (which + 1) * own_rows, :] = out
+        pieces = [triple(scores[n : n + 1, first : first + rows]) for n in range(2)]
+        for n in range(members):
+            cut = slice(n * own_rows, (n + 1) * own_rows)
+            lines = [jnp.concatenate([p[:, cut] for p in x] + [none], axis=1) for x in pieces]
+            extra = jnp.concatenate(lines + [blank], axis=0).astype(jnp.bfloat16)
+            msg[to * members + n, 2 * own_rows : 2 * own_rows + 8, :] = extra
+
+
+def owner_kernel(sizes, own, got, out):
+    piece = (got.shape[1] - 8) // 2
+    width = got.shape[2]
+    rows = piece * sizes["mp"]
+    slot = place()[4]
+    first, second, extra = (
+        got[0, lo:hi, :].astype(jnp.float32)
+        for lo, hi in ((0, piece), (piece, 2 * piece), (2 * piece, 2 * piece + 8))
+    )
+    for n in range(1, got.shape[0]):
+        first = first + got[n, 0:piece, :].astype(jnp.float32)
+        second = second + got[n, piece : 2 * piece, :].astype(jnp.float32)
+        extra = extra + got[n, 2 * piece : 2 * piece + 8, :].astype(jnp.float32)
+    extra = extra[:, :piece] + extra[:, piece : 2 * piece] + extra[:, 2 * piece : 3 * piece]
+    total, positive = extra[0:1], extra[1:2]
+    share = chosen(row_weights((own,), rows), slot, piece) / total
+    share = jnp.concatenate([share, share], axis=1)
+    share = jnp.broadcast_to(share, (8, 2 * piece)).T[0:piece, 0:1]
+    grad = (first * share + second).astype(jnp.bfloat16)
+    loss = jnp.log(total) - positive
+    none = jnp.zeros((1, width - 3 * piece), jnp.float32)
+    line = jnp.concatenate([*triple(loss), none], axis=1)
+    line = jnp.concatenate([line, jnp.zeros((7, width), jnp.float32)], axis=0)
+    line = line.astype(jnp.bfloat16)
+    for n in range(out.shape[0]):
+        out[n, 0:piece, :] = grad
+        out[n, piece : piece + 8, :] = line
+
+
+def finish_kernel(got, out, loss, wide, stored):
+    piece = got.shape[1] - 8
+    copies, losses = [], []
+    for n in range(got.shape[0]):
+        at = pl.ds(n * piece, piece)
+        wide[at, :] = got[n, 0:piece, :].astype(jnp.float32)
+        copies.append(pltpu.make_async_copy(wide.at[at], out.at[at], stored.at[n]))
+        copies[-1].start()
+        line = got[n, piece : piece + 8, :].astype(jnp.float32)[0:1]
+        losses.append(line[:, :piece] + line[:, piece : 2 * piece] + line[:, 2 * piece : 3 * piece])
+    loss[...] = jnp.concatenate(losses, axis=1)
+    for copy in copies:
+        copy.wait()
 
 
 def call(kernel, outs, args, scratch=(), mib=4, flops=0):
@@ -311,49 +356,60 @@
     half, both, team = chunks * piece, 2 * rows, 2 * members
     flops = 2 * half * both * width
     scratch = [pltpu.VMEM((2, BLOCK, both), f32), pltpu.VMEM((half, 128), f32)]
-    sums, column, ncol_far, nrow = call(
+    sums, column, ncol_far, nrow, e_far = call(
         functools.partial(far_kernel, sizes),
         [
             ((2, 8, both), f32),
             ((half // 128, 128), f32),
             ((half, width), bf16),
             ((both, width), bf16),
+            ((half, both), f32),
         ],
         (own, oth, far),
         scratch,
         16,
         flops,
     )
-    msg, cmsg, ncol_near = call(
+    scores, cmsg, ncol_near, e_near = call(
         functools.partial(near_kernel, sizes),
         [
-            ((2, 8, rows // 2), f32),
+            ((2, both), f32),
             ((2 * chunks, 24, 128), bf16),
             ((half, width), bf16),
+            ((half, both), f32),
         ],
         (own, oth, near, heft, sums, column, nrow),
         scratch,
         16,
         flops,
     )
-    got = msg + swap(msg, "zl")
     cgot = exchange(cmsg, OWNERS)
-    got = got + swap(got, "yl")
-    for apart in (1, 2):
-        got = got + lax.ppermute(got, "x", [(n, n ^ apart) for n in range(sizes["x"])])
-    info, loss = call(totals_kernel, [((4, rows), f32), ((1, rows), f32)], (got,))
-    (grads,) = call(
+    (msg,) = call(
         functools.partial(backward_kernel, sizes),
-        [((team, piece, width), bf16)],
-        (own, oth, nrow, ncol_far, ncol_near, info, cgot),
-        [pltpu.VMEM((2, BLOCK, both), f32), pltpu.VMEM((2, BLOCK, both), bf16), pltpu.VMEM((width, both), f32)],
+        [((team, 2 * piece + 8, width), bf16)],
+        (own, oth, ncol_far, ncol_near, e_far, e_near, scores, cgot),
+        [pltpu.VMEM((2, BLOCK, both), bf16)] * 2 + [pltpu.VMEM((2, width, both), f32)],
         16,
-        2 * flops,
-    )
-    shares = exchange(grads, TEAM)
-    share = jnp.sum(shares.astype(f32), axis=0).astype(bf16)
-    grad = exchange(jnp.broadcast_to(share[None], (members, piece, width)), MP)
-    return loss.reshape(rows), grad.astype(f32).reshape(rows, width)
+        4 * flops,
+    )
+    got = exchange(msg, TEAM)
+    (share,) = call(
+        functools.partial(owner_kernel, sizes), [((members, piece + 8, width), bf16)], (own, got)
+    )
+    got = exchange(share, MP)
+    grad, loss = pl.pallas_call(
+        finish_kernel,
+        name="finish",
+        in_specs=[pl.BlockSpec(memory_space=pltpu.VMEM)],
+        out_specs=[pl.BlockSpec(memory_space=pltpu.HBM), pl.BlockSpec(memory_space=pltpu.VMEM)],
+        out_shape=[
+            jax.ShapeDtypeStruct((rows, width), f32),
+            jax.ShapeDtypeStruct((1, rows), f32),
+        ],
+        scratch_shapes=[pltpu.VMEM((rows, width), f32), pltpu.SemaphoreType.DMA((members,))],
+        compiler_params=pltpu.CompilerParams(vmem_limit_bytes=4 << 20),
+    )(got)
+    return loss.reshape(rows), grad
 
 
 def solution(mesh):

time: 116 us -> 113 us (0.974)
  the two profiles are of different devices: /device:TPU:32 before, /device:TPU:1 now
where the time goes in v7:
time: 113 us; the launch traced here: 112 us
  blocking collectives  84.9 us (75%)
  Pallas kernels  13.3 us (12%)
  waiting for transfers between devices  7.56 us (7%)
  starting transfers between devices  6.02 us (5%)
    all_to_all x4, blocking collectives, exchange(): return lax.all_to_all(x, axes, 0, 0, tiled=True)  84.9 us
    pallas_call x4, Pallas kernels, call(): pl.pallas_call(kernel, in_specs=[vmem] * len(args), out_specs=[vmem] * le...  10.8 us
    ppermute x2, waiting for transfers between devices, swap(): return lax.ppermute(x, axis, [(0, 1), (1, 0)])  7.56 us
    ppermute x2, starting transfers between devices, swap(): return lax.ppermute(x, axis, [(0, 1), (1, 0)])  6.02 us
  transfers between devices with their start and end apart: 2, of which 1 were waited for; matrix products, arithmetic and copies ran while one was open for 0% of the time, Pallas kernels for 2%

profile of v7, /device:TPU:1, one launch (start us, length us, event | category | flops | bytes accessed | tf_op | source)
XLA Modules:
  0.0 112.4 jit_solution(11666152527825119292)
XLA Ops:
  0.6 1.0 pack.1
  1.7 36.5 %all_to_all.20.far = bf16[16,64,256]{2,1,0:T(8,128)(2,1)S(1)} all-to-all(bf16[16,64,256]{2,1,0:T(8,128)(2,1)S(1)} %get-tuple-element.17), channel_id=1, replica_groups=mesh['zh'=4,'zl'=2,'yh'=4,'core'=2,'yl'=2,'x'=4] {'yh','zh'}, dimensions={0} | all-to-all | bytes 1048576 | tf_op jit(solution)/shard_map/all_to_all | solution.py:31
  38.2 3.7 %collective-permute-start.1 = (bf16[16,64,256]{2,1,0:T(8,128)(2,1)S(1)}, bf16[16,64,256]{2,1,0:T(8,128)(2,1)S(1)}, u32[]{:S(2)}, u32[]{:S(2)}) collective-permute-start(bf16[16,64,256]{2,1,0:T(8,128)(2,1)S(1)} %all_to_all.20.far), channel_id=1, source_target_pairs={{0,8},{8,0},{1,9},{9,1},{2,10},{10,2},{3,11},{11,3},{4,12},{12,4},... | collective-permute-start | bytes 1572872 | tf_op jit(solution)/shard_map/ppermute | solution.py:27
  41.9 2.4 %collective-permute-start = (bf16[528,256]{1,0:T(8,128)(2,1)S(1)}, bf16[528,256]{1,0:T(8,128)(2,1)S(1)}, u32[]{:S(2)}, u32[]{:S(2)}) collective-permute-start(bf16[528,256]{1,0:T(8,128)(2,1)S(1)} %get-tuple-element.16.own), channel_id=1, source_target_pairs={{0,64},{64,0},{1,65},{65,1},{2,66},{66,2},{3,67},{67,3},{4,68},{68... | collective-permute-start | bytes 811016 | tf_op jit(solution)/shard_map/ppermute | solution.py:27
  44.2 7.6 %collective-permute-done.oth = bf16[528,256]{1,0:T(8,128)(2,1)S(1)} collective-permute-done((bf16[528,256]{1,0:T(8,128)(2,1)S(1)}, bf16[528,256]{1,0:T(8,128)(2,1)S(1)}, u32[]{:S(2)}, u32[]{:S(2)}) %collective-permute-start) | collective-permute-done | bytes 270368 | tf_op jit(solution)/shard_map/ppermute | solution.py:27
  51.8 2.1 %shard_map.50 = (f32[2,8,1024]{2,1,0:T(8,128)S(1)}, f32[8,128]{1,0:T(8,128)S(1)}, bf16[1024,256]{1,0:T(8,128)(2,1)S(1)}, bf16[1024,256]{1,0:T(8,128)(2,1)S(1)}, f32[1024,1024]{1,0:T(8,128)S(1)}) custom-call(bf16[528,256]{1,0:T(8,128)(2,1)S(1)} %get-tuple-element.16.own, bf16[528,256]{1,0:T(8,128)(2,1)S(1)} %collective-permute-done.oth, ...), custom_call_target="tpu_custom_call" | custom-call | flops 536870912 | bytes 1048576 | tf_op jit(solution)/shard_map/pallas_call | solution.py:314
  53.8 0.0 collective-permute-done.1.near
  53.9 1.6 %shard_map.51 = (f32[2,1024]{1,0:T(2,128)S(1)}, bf16[32,24,128]{2,1,0:T(8,128)(2,1)S(1)}, bf16[1024,256]{1,0:T(8,128)(2,1)S(1)}, f32[1024,1024]{1,0:T(8,128)S(1)}) custom-call(bf16[528,256]{1,0:T(8,128)(2,1)S(1)} %get-tuple-element.16.own, bf16[528,256]{1,0:T(8,128)(2,1)S(1)} %collective-permute-done.oth, ...), custom_call_target="tpu_custom_call" | custom-call | flops 536870912 | bytes 1048576 | tf_op jit(solution)/shard_map/pallas_call | solution.py:314
  55.5 17.8 %all_to_all.21.cgot = bf16[32,24,128]{2,1,0:T(8,128)(2,1)S(1)} all-to-all(bf16[32,24,128]{2,1,0:T(8,128)(2,1)S(1)} %get-tuple-element.27), channel_id=1, replica_groups=mesh['zh'=4,'zl'=2,'yh'=4,'core'=2,'yl'=2,'x'=4] {'core','yh','zh'}, dimensions={0} | all-to-all | bytes 393216 | tf_op jit(solution)/shard_map/all_to_all | solution.py:31
  73.2 6.4 %shard_map.52 = bf16[16,136,256]{2,1,0:T(8,128)(2,1)S(1)} custom-call(bf16[528,256]{1,0:T(8,128)(2,1)S(1)} %get-tuple-element.16.own, bf16[528,256]{1,0:T(8,128)(2,1)S(1)} %collective-permute-done.oth, bf16[1024,256]{1,0:T(8,128)(2,1)S(1)} %get-tuple-element.18.ncol_far, bf16[1024,256]{1,0:T(8,128)(2,1)S(1)} %get-tuple-element.23.ncol_near, ...), custom_call_target="tpu_custom_call" | custom-call | flops 2147483648 | bytes 1048576 | tf_op jit(solution)/shard_map/pallas_call | solution.py:314
  79.6 20.8 %all_to_all.22.got = bf16[16,136,256]{2,1,0:T(8,128)(2,1)S(1)} all-to-all(bf16[16,136,256]{2,1,0:T(8,128)(2,1)S(1)} %shard_map.52), channel_id=1, replica_groups=mesh['zh'=4,'zl'=2,'yh'=4,'core'=2,'yl'=2,'x'=4] {'zl','x','yl'}, dimensions={0} | all-to-all | bytes 2228224 | tf_op jit(solution)/shard_map/all_to_all | solution.py:31
  100.4 0.7 shard_map.53
  101.1 9.8 %all_to_all.23.got = bf16[8,72,256]{2,1,0:T(8,128)(2,1)S(1)} all-to-all(bf16[8,72,256]{2,1,0:T(8,128)(2,1)S(1)} %shard_map.53), channel_id=1, replica_groups=mesh['zh'=4,'zl'=2,'yh'=4,'core'=2,'yl'=2,'x'=4] {'x','yl'}, dimensions={0} | all-to-all | bytes 589824 | tf_op jit(solution)/shard_map/all_to_all | solution.py:31
  111.0 1.5 %finish.1 = (f32[512,256]{1,0:T(8,128)}, f32[1,512]{1,0:T(1,128)}) custom-call(bf16[8,72,256]{2,1,0:T(8,128)(2,1)S(1)} %all_to_all.23.got), custom_call_target="tpu_custom_call" | custom-call | tf_op jit(solution)/shard_map/finish/pallas_call | solution.py:400
Async XLA Ops:
  38.2 15.7 %collective-permute-start.1 = (bf16[16,64,256]{2,1,0:T(8,128)(2,1)S(1)}, bf16[16,64,256]{2,1,0:T(8,128)(2,1)S(1)}, u32[]{:S(2)}, u32[]{:S(2)}) collective-permute-start(bf16[16,64,256]{2,1,0:T(8,128)(2,1)S(1)} %all_to_all.20.far), channel_id=1, source_target_pairs={{0,8},{8,0},{1,9},{9,1},{2,10},{10,2},{3,11},{11,3},{4,12},{12,4},... | collective-permute-start | bytes 1572872 | tf_op jit(solution)/shard_map/ppermute | solution.py:27
  41.9 9.9 %collective-permute-start = (bf16[528,256]{1,0:T(8,128)(2,1)S(1)}, bf16[528,256]{1,0:T(8,128)(2,1)S(1)}, u32[]{:S(2)}, u32[]{:S(2)}) collective-permute-start(bf16[528,256]{1,0:T(8,128)(2,1)S(1)} %get-tuple-element.16.own), channel_id=1, source_target_pairs={{0,64},{64,0},{1,65},{65,1},{2,66},{66,2},{3,67},{67,3},{4,68},{68... | collective-permute-start | bytes 811016 | tf_op jit(solution)/shard_map/ppermute | solution.py:27

commit v8 on v6

--- a/solution.py
+++ b/solution.py
@@ -216,14 +216,13 @@
                     value = e * (row_share + column[r : r + step])
                     pull = row_weight + column[piece + r : piece + r + step]
                     value = jnp.where(mates == base + r, value - pull, value)
-                    coef[turn % 2, pl.ds(c * piece + r, step), :] = value.astype(jnp.bfloat16)
-            left = ncol[pl.ds(b * BLOCK, BLOCK), :].T
-            product = jnp.dot(left, coef[turn % 2], preferred_element_type=jnp.float32)
-            if turn == 0:
-                acc[...] = product
-            else:
-                acc[...] += product
-            turn += 1
+                    coef[turn, pl.ds(b * BLOCK + c * piece + r, step), :] = value.astype(jnp.bfloat16)
+        product = jnp.dot(ncol[...].T, coef[turn], preferred_element_type=jnp.float32)
+        if turn == 0:
+            acc[...] = product
+        else:
+            acc[...] += product
+        turn += 1
     zl = at[1]
     members = sizes["mp"]
     for to, first, source in ((zl, 0, own[0:rows, :]), (1 - zl, rows, oth[0:rows, :])):
@@ -234,9 +233,10 @@
         msg[pl.ds(to * members, members)] = out.astype(jnp.bfloat16).reshape(members, -1, width)
 
 
-def finish_kernel(got, out, wide, stored):
+def finish_kernel(got, loss, out, loss_out, wide, stored):
     piece = got.shape[1]
-    copies = []
+    copies = [pltpu.make_async_copy(loss, loss_out, stored.at[got.shape[0]])]
+    copies[0].start()
     for n in range(got.shape[0]):
         at = pl.ds(n * piece, piece)
         wide[at, :] = got[n].astype(jnp.float32)
@@ -320,22 +320,25 @@
         functools.partial(backward_kernel, sizes),
         [((team, piece, width), bf16)],
         (own, oth, ncol_far, ncol_near, e_far, e_near, info, cw),
-        [pltpu.VMEM((2, BLOCK, both), bf16), pltpu.VMEM((width, both), f32)],
+        [pltpu.VMEM((2, half, both), bf16), pltpu.VMEM((width, both), f32)],
         16,
         2 * flops,
     )
     shares = exchange(grads, TEAM)
     share = jnp.sum(shares.astype(f32), axis=0).astype(bf16)
     got = exchange(jnp.broadcast_to(share[None], (members, piece, width)), MP)
-    grad = pl.pallas_call(
+    grad, loss = pl.pallas_call(
         finish_kernel,
         name="finish",
-        in_specs=[pl.BlockSpec(memory_space=pltpu.VMEM)],
-        out_specs=pl.BlockSpec(memory_space=pltpu.HBM),
-        out_shape=jax.ShapeDtypeStruct((rows, width), f32),
-        scratch_shapes=[pltpu.VMEM((rows, width), f32), pltpu.SemaphoreType.DMA((members,))],
+        in_specs=[pl.BlockSpec(memory_space=pltpu.VMEM)] * 2,
+        out_specs=[pl.BlockSpec(memory_space=pltpu.HBM)] * 2,
+        out_shape=[
+            jax.ShapeDtypeStruct((rows, width), f32),
+            jax.ShapeDtypeStruct((1, rows), f32),
+        ],
+        scratch_shapes=[pltpu.VMEM((rows, width), f32), pltpu.SemaphoreType.DMA((members + 1,))],
         compiler_params=pltpu.CompilerParams(vmem_limit_bytes=4 << 20),
-    )(got)
+    )(got, loss)
     return loss.reshape(rows), grad
 
 

time: 111 us -> 110 us (level)
  no operation moved by 1% of the time
where the time goes in v8:
time: 110 us; the launch traced here: 109 us
  blocking collectives  86.1 us (78%)
  Pallas kernels  8.4 us (8%)
  waiting for transfers between devices  7.56 us (7%)
  starting transfers between devices  6.02 us (5%)
    all_to_all x5, blocking collectives, exchange(): return lax.all_to_all(x, axes, 0, 0, tiled=True)  86.1 us
    ppermute x2, waiting for transfers between devices, swap(): return lax.ppermute(x, axis, [(0, 1), (1, 0)])  7.56 us
    pallas_call x4, Pallas kernels, call(): pl.pallas_call(kernel, in_specs=[vmem] * len(args), out_specs=[vmem] * le...  6.49 us
    ppermute x2, starting transfers between devices, swap(): return lax.ppermute(x, axis, [(0, 1), (1, 0)])  6.02 us
  transfers between devices with their start and end apart: 2, of which 1 were waited for; matrix products, arithmetic and copies ran while one was open for 0% of the time, Pallas kernels for 2%

profile of v8, /device:TPU:1, one launch (start us, length us, event | category | flops | bytes accessed | tf_op | source)
XLA Modules:
  0.0 108.9 jit_solution(17517420643682029078)
XLA Ops:
  0.6 1.0 pack.1
  1.7 36.5 %all_to_all.25.far = bf16[16,64,256]{2,1,0:T(8,128)(2,1)S(1)} all-to-all(bf16[16,64,256]{2,1,0:T(8,128)(2,1)S(1)} %get-tuple-element.18), channel_id=1, replica_groups=mesh['zh'=4,'zl'=2,'yh'=4,'core'=2,'yl'=2,'x'=4] {'yh','zh'}, dimensions={0} | all-to-all | bytes 1048576 | tf_op jit(solution)/shard_map/all_to_all | solution.py:31
  38.2 3.7 %collective-permute-start.1 = (bf16[16,64,256]{2,1,0:T(8,128)(2,1)S(1)}, bf16[16,64,256]{2,1,0:T(8,128)(2,1)S(1)}, u32[]{:S(2)}, u32[]{:S(2)}) collective-permute-start(bf16[16,64,256]{2,1,0:T(8,128)(2,1)S(1)} %all_to_all.25.far), channel_id=1, source_target_pairs={{0,8},{8,0},{1,9},{9,1},{2,10},{10,2},{3,11},{11,3},{4,12},{12,4},... | collective-permute-start | bytes 1572872 | tf_op jit(solution)/shard_map/ppermute | solution.py:27
  41.9 2.4 %collective-permute-start = (bf16[528,256]{1,0:T(8,128)(2,1)S(1)}, bf16[528,256]{1,0:T(8,128)(2,1)S(1)}, u32[]{:S(2)}, u32[]{:S(2)}) collective-permute-start(bf16[528,256]{1,0:T(8,128)(2,1)S(1)} %get-tuple-element.17.own), channel_id=1, source_target_pairs={{0,64},{64,0},{1,65},{65,1},{2,66},{66,2},{3,67},{67,3},{4,68},{68... | collective-permute-start | bytes 811016 | tf_op jit(solution)/shard_map/ppermute | solution.py:27
  44.2 7.6 %collective-permute-done.oth = bf16[528,256]{1,0:T(8,128)(2,1)S(1)} collective-permute-done((bf16[528,256]{1,0:T(8,128)(2,1)S(1)}, bf16[528,256]{1,0:T(8,128)(2,1)S(1)}, u32[]{:S(2)}, u32[]{:S(2)}) %collective-permute-start) | collective-permute-done | bytes 270368 | tf_op jit(solution)/shard_map/ppermute | solution.py:27
  51.8 1.8 %shard_map.50 = (f32[2,8,1024]{2,1,0:T(8,128)S(1)}, bf16[1024,256]{1,0:T(8,128)(2,1)S(1)}, bf16[1024,256]{1,0:T(8,128)(2,1)S(1)}, f32[1024,1024]{1,0:T(8,128)S(1)}) custom-call(bf16[528,256]{1,0:T(8,128)(2,1)S(1)} %get-tuple-element.17.own, bf16[528,256]{1,0:T(8,128)(2,1)S(1)} %collective-permute-done.oth, bf16[16,64,256]{2,1,0:T(8,128)(2,1)S(1)} %all_to_all.25.far), custom_call_target="tpu_custom_call" | custom-call | flops 536870912 | bytes 1048576 | tf_op jit(solution)/shard_map/pallas_call | solution.py:251
  53.6 0.0 collective-permute-done.1.near
  53.6 1.4 %shard_map.51 = (f32[16,8,256]{2,1,0:T(8,128)S(1)}, bf16[1024,256]{1,0:T(8,128)(2,1)S(1)}, f32[1024,1024]{1,0:T(8,128)S(1)}) custom-call(bf16[528,256]{1,0:T(8,128)(2,1)S(1)} %get-tuple-element.17.own, bf16[528,256]{1,0:T(8,128)(2,1)S(1)} %collective-permute-done.oth, bf16[16,64,256]{2,1,0:T(8,128)(2,1)S(1)} %collective-permute-done.1.near, ...), custom_call_target="tpu_custom_call" | custom-call | flops 536870912 | bytes 1048576 | tf_op jit(solution)/shard_map/pallas_call | solution.py:251
  55.0 10.1 %all_to_all.26.got = f32[16,8,256]{2,1,0:T(8,128)S(1)} all-to-all(f32[16,8,256]{2,1,0:T(8,128)S(1)} %get-tuple-element.26), channel_id=1, replica_groups=mesh['zh'=4,'zl'=2,'yh'=4,'core'=2,'yl'=2,'x'=4] {'zl','x','yl'}, dimensions={0} | all-to-all | bytes 262144 | tf_op jit(solution)/shard_map/all_to_all | solution.py:31
  65.0 0.1 shard_map.52
  65.2 18.6 %all_to_all.27.cw = f32[32,1,128]{2,1,0:T(1,128)S(1)} all-to-all(f32[32,1,128]{2,1,0:T(1,128)S(1)} %get-tuple-element.28), channel_id=1, replica_groups=mesh['zh'=4,'zl'=2,'yh'=4,'core'=2,'yl'=2,'x'=4] {'core','yh','zh'}, dimensions={0} | all-to-all | bytes 32768 | tf_op jit(solution)/shard_map/all_to_all | solution.py:31
  83.8 3.2 %shard_map.53 = bf16[16,64,256]{2,1,0:T(8,128)(2,1)S(1)} custom-call(bf16[528,256]{1,0:T(8,128)(2,1)S(1)} %get-tuple-element.17.own, bf16[528,256]{1,0:T(8,128)(2,1)S(1)} %collective-permute-done.oth, bf16[1024,256]{1,0:T(8,128)(2,1)S(1)} %get-tuple-element.19.ncol_far, bf16[1024,256]{1,0:T(8,128)(2,1)S(1)} %get-tuple-element.23.ncol_near, ...), custom_call_target="tpu_custom_call" | custom-call | flops 1073741824 | bytes 1048576 | tf_op jit(solution)/shard_map/pallas_call | solution.py:251
  87.1 11.6 %all_to_all.28 = bf16[16,64,256]{2,1,0:T(8,128)(2,1)S(1)} all-to-all(bf16[16,64,256]{2,1,0:T(8,128)(2,1)S(1)} %shard_map.53), channel_id=1, replica_groups=mesh['zh'=4,'zl'=2,'yh'=4,'core'=2,'yl'=2,'x'=4] {'zl','x','yl'}, dimensions={0} | all-to-all | bytes 1048576 | tf_op jit(solution)/shard_map/all_to_all | solution.py:31
  98.7 0.1 reduce_sum.12
  98.8 9.2 %all_to_all.29.got = bf16[8,64,256]{2,1,0:T(8,128)(2,1)S(1)} all-to-all(bf16[8,64,256]{2,1,0:T(8,128)(2,1)S(1)} %broadcast_in_dim.2), channel_id=1, replica_groups=mesh['zh'=4,'zl'=2,'yh'=4,'core'=2,'yl'=2,'x'=4] {'x','yl'}, dimensions={0} | all-to-all | bytes 524288 | tf_op jit(solution)/shard_map/all_to_all | solution.py:31
  108.0 0.9 finish.1
  (1 shorter events, 0.0 us)
Async XLA Ops:
  38.2 15.4 %collective-permute-start.1 = (bf16[16,64,256]{2,1,0:T(8,128)(2,1)S(1)}, bf16[16,64,256]{2,1,0:T(8,128)(2,1)S(1)}, u32[]{:S(2)}, u32[]{:S(2)}) collective-permute-start(bf16[16,64,256]{2,1,0:T(8,128)(2,1)S(1)} %all_to_all.25.far), channel_id=1, source_target_pairs={{0,8},{8,0},{1,9},{9,1},{2,10},{10,2},{3,11},{11,3},{4,12},{12,4},... | collective-permute-start | bytes 1572872 | tf_op jit(solution)/shard_map/ppermute | solution.py:27
  41.9 9.9 %collective-permute-start = (bf16[528,256]{1,0:T(8,128)(2,1)S(1)}, bf16[528,256]{1,0:T(8,128)(2,1)S(1)}, u32[]{:S(2)}, u32[]{:S(2)}) collective-permute-start(bf16[528,256]{1,0:T(8,128)(2,1)S(1)} %get-tuple-element.17.own), channel_id=1, source_target_pairs={{0,64},{64,0},{1,65},{65,1},{2,66},{66,2},{3,67},{67,3},{4,68},{68... | collective-permute-start | bytes 811016 | tf_op jit(solution)/shard_map/ppermute | solution.py:27

commit v9 on v8

--- a/solution.py
+++ b/solution.py
@@ -118,26 +118,28 @@
     return total, positive
 
 
-def far_kernel(sizes, own, oth, far, sums, ncol, nrow, e_out, s_buf):
+def rows_kernel(own, oth, nrow, ids):
     rows = nrow.shape[0] // 2
     for at, source in ((0, own[0:rows, :]), (rows, oth[0:rows, :])):
         floats, _, inverse = scaled(source)
         nrow[pl.ds(at, rows), :] = (floats * inverse).astype(jnp.bfloat16)
-    ids = partner_ids(own, oth, rows)
-    zero = jnp.zeros((8, 2 * rows), jnp.float32)
+    ids[...] = partner_ids(own, oth, rows)
+
+
+def far_kernel(sizes, far, ids, nrow, sums, ncol, e_out, s_buf):
+    zero = jnp.zeros((8, nrow.shape[0]), jnp.float32)
     total, positive = forward_half(
-        sizes, place(), False, far, ids, nrow, ncol, e_out, s_buf, zero, zero
+        sizes, place(), False, far, ids[...], nrow, ncol, e_out, s_buf, zero, zero
     )
     sums[0] = total
     sums[1] = positive
 
 
-def near_kernel(sizes, own, oth, near, weight, sums, nrow, msg, ncol, e_out, s_buf):
+def near_kernel(sizes, near, ids, weight, sums, nrow, msg, ncol, e_out, s_buf):
     rows = nrow.shape[0] // 2
     at = place()
-    ids = partner_ids(own, oth, rows)
     total, positive = forward_half(
-        sizes, at, True, near, ids, nrow, ncol, e_out, s_buf, sums[0], sums[1]
+        sizes, at, True, near, ids[...], nrow, ncol, e_out, s_buf, sums[0], sums[1]
     )
     total = jnp.sum(total, axis=0, keepdims=True)
     positive = jnp.sum(positive, axis=0, keepdims=True) * INV_TAU
@@ -187,7 +189,7 @@
 
 
 def backward_kernel(
-    sizes, own, oth, ncol_far, ncol_near, e_far, e_near, info, cw, msg, coef, acc
+    sizes, own, oth, ids, ncol_far, ncol_near, e_far, e_near, info, cw, msg, coef, acc
 ):
     both, width = acc.shape[1], acc.shape[0]
     rows = both // 2
@@ -196,8 +198,7 @@
     piece = half // chunks
     step = 16
     at = place()
-    ids = partner_ids(own, oth, rows)
-    mates = jnp.broadcast_to(ids, (step, both)) - lax.broadcasted_iota(jnp.int32, (step, both), 0)
+    mates = jnp.broadcast_to(ids[...], (step, both)) - lax.broadcasted_iota(jnp.int32, (step, both), 0)
     row_share = jnp.concatenate([info[0:1, :], info[1:2, :]], axis=1)
     row_weight = jnp.concatenate([info[2:3, :], info[3:4, :]], axis=1)
     row_share = jnp.broadcast_to(row_share, (step, both))
@@ -288,15 +289,17 @@
     ])
     oth = swap(own, "zl")
     far = exchange(spread, FAR)
+    both = 2 * rows
+    nrow, ids = call(rows_kernel, [((both, width), bf16), ((1, both), jnp.int32)], (own, oth))
     near = swap(far, "core")
 
-    half, both, team = chunks * piece, 2 * rows, 2 * members
+    half, team = chunks * piece, 2 * members
     flops = 2 * half * both * width
     score = pltpu.VMEM((2, BLOCK, both), f32)
-    sums, ncol_far, nrow, e_far = call(
+    sums, ncol_far, e_far = call(
         functools.partial(far_kernel, sizes),
-        [((2, 8, both), f32), ((half, width), bf16), ((both, width), bf16), ((half, both), f32)],
-        (own, oth, far),
+        [((2, 8, both), f32), ((half, width), bf16), ((half, both), f32)],
+        (far, ids, nrow),
         [score],
         16,
         flops,
@@ -304,7 +307,7 @@
     msg, ncol_near, e_near = call(
         functools.partial(near_kernel, sizes),
         [((team, 8, rows // 2), f32), ((half, width), bf16), ((half, both), f32)],
-        (own, oth, near, heft, sums, nrow),
+        (near, ids, heft, sums, nrow),
         [score],
         16,
         flops,
@@ -319,7 +322,7 @@
     (grads,) = call(
         functools.partial(backward_kernel, sizes),
         [((team, piece, width), bf16)],
-        (own, oth, ncol_far, ncol_near, e_far, e_near, info, cw),
+        (own, oth, ids, ncol_far, ncol_near, e_far, e_near, info, cw),
         [pltpu.VMEM((2, half, both), bf16), pltpu.VMEM((width, both), f32)],
         16,
         2 * flops,

time: 110 us -> 111 us (level)
    pallas_call x4 -> x5, Pallas kernels: 6.49 us -> 6.59 us  [call(): pl.pallas_call(kernel, in_specs=[vmem] * len(args), out_specs=[vmem] * le...]
where the time goes in v9:
time: 111 us; the launch traced here: 109 us
  blocking collectives  86.1 us (78%)
  Pallas kernels  8.5 us (8%)
  waiting for transfers between devices  7.56 us (7%)
  starting transfers between devices  6.02 us (5%)
    all_to_all x5, blocking collectives, exchange(): return lax.all_to_all(x, axes, 0, 0, tiled=True)  86.1 us
    ppermute x2, waiting for transfers between devices, swap(): return lax.ppermute(x, axis, [(0, 1), (1, 0)])  7.56 us
    pallas_call x5, Pallas kernels, call(): pl.pallas_call(kernel, in_specs=[vmem] * len(args), out_specs=[vmem] * le...  6.59 us
    ppermute x2, starting transfers between devices, swap(): return lax.ppermute(x, axis, [(0, 1), (1, 0)])  6.02 us
  transfers between devices with their start and end apart: 2, of which 1 were waited for; matrix products, arithmetic and copies ran while one was open for 0% of the time, Pallas kernels for 2%

profile of v9, /device:TPU:1, one launch (start us, length us, event | category | flops | bytes accessed | tf_op | source)
XLA Modules:
  0.0 109.0 jit_solution(12134156838203927271)
XLA Ops:
  0.6 1.0 pack.1
  1.7 36.5 %all_to_all.25.far = bf16[16,64,256]{2,1,0:T(8,128)(2,1)S(1)} all-to-all(bf16[16,64,256]{2,1,0:T(8,128)(2,1)S(1)} %get-tuple-element.20), channel_id=1, replica_groups=mesh['zh'=4,'zl'=2,'yh'=4,'core'=2,'yl'=2,'x'=4] {'yh','zh'}, dimensions={0} | all-to-all | bytes 1048576 | tf_op jit(solution)/shard_map/all_to_all | solution.py:31
  38.2 3.7 %collective-permute-start.1 = (bf16[16,64,256]{2,1,0:T(8,128)(2,1)S(1)}, bf16[16,64,256]{2,1,0:T(8,128)(2,1)S(1)}, u32[]{:S(2)}, u32[]{:S(2)}) collective-permute-start(bf16[16,64,256]{2,1,0:T(8,128)(2,1)S(1)} %all_to_all.25.far), channel_id=1, source_target_pairs={{0,8},{8,0},{1,9},{9,1},{2,10},{10,2},{3,11},{11,3},{4,12},{12,4},... | collective-permute-start | bytes 1572872 | tf_op jit(solution)/shard_map/ppermute | solution.py:27
  41.9 2.4 %collective-permute-start = (bf16[528,256]{1,0:T(8,128)(2,1)S(1)}, bf16[528,256]{1,0:T(8,128)(2,1)S(1)}, u32[]{:S(2)}, u32[]{:S(2)}) collective-permute-start(bf16[528,256]{1,0:T(8,128)(2,1)S(1)} %get-tuple-element.18.own), channel_id=1, source_target_pairs={{0,64},{64,0},{1,65},{65,1},{2,66},{66,2},{3,67},{67,3},{4,68},{68... | collective-permute-start | bytes 811016 | tf_op jit(solution)/shard_map/ppermute | solution.py:27
  44.2 7.6 %collective-permute-done.oth = bf16[528,256]{1,0:T(8,128)(2,1)S(1)} collective-permute-done((bf16[528,256]{1,0:T(8,128)(2,1)S(1)}, bf16[528,256]{1,0:T(8,128)(2,1)S(1)}, u32[]{:S(2)}, u32[]{:S(2)}) %collective-permute-start) | collective-permute-done | bytes 270368 | tf_op jit(solution)/shard_map/ppermute | solution.py:27
  51.8 0.3 shard_map.50
  52.1 1.5 %shard_map.51 = (f32[2,8,1024]{2,1,0:T(8,128)S(1)}, bf16[1024,256]{1,0:T(8,128)(2,1)S(1)}, f32[1024,1024]{1,0:T(8,128)S(1)}) custom-call(bf16[16,64,256]{2,1,0:T(8,128)(2,1)S(1)} %all_to_all.25.far, s32[1,1024]{1,0:T(1,128)S(1)} %get-tuple-element.19.ids, bf16[1024,256]{1,0:T(8,128)(2,1)S(1)} %get-tuple-element.21.nrow), custom_call_target="tpu_custom_call" | custom-call | flops 536870912 | bytes 1048576 | tf_op jit(solution)/shard_map/pallas_call | solution.py:252
  53.6 0.0 collective-permute-done.1.near
  53.6 1.4 %shard_map.52 = (f32[16,8,256]{2,1,0:T(8,128)S(1)}, bf16[1024,256]{1,0:T(8,128)(2,1)S(1)}, f32[1024,1024]{1,0:T(8,128)S(1)}) custom-call(bf16[16,64,256]{2,1,0:T(8,128)(2,1)S(1)} %collective-permute-done.1.near, s32[1,1024]{1,0:T(1,128)S(1)} %get-tuple-element.19.ids, f32[1,512]{1,0:T(1,128)S(1)} %get-tuple-element.23.weight, ...), custom_call_target="tpu_custom_call" | custom-call | flops 536870912 | bytes 1048576 | tf_op jit(solution)/shard_map/pallas_call | solution.py:252
  55.0 10.1 %all_to_all.26.got = f32[16,8,256]{2,1,0:T(8,128)S(1)} all-to-all(f32[16,8,256]{2,1,0:T(8,128)S(1)} %get-tuple-element.28), channel_id=1, replica_groups=mesh['zh'=4,'zl'=2,'yh'=4,'core'=2,'yl'=2,'x'=4] {'zl','x','yl'}, dimensions={0} | all-to-all | bytes 262144 | tf_op jit(solution)/shard_map/all_to_all | solution.py:31
  65.1 0.1 shard_map.53
  65.2 18.7 %all_to_all.27.cw = f32[32,1,128]{2,1,0:T(1,128)S(1)} all-to-all(f32[32,1,128]{2,1,0:T(1,128)S(1)} %get-tuple-element.30), channel_id=1, replica_groups=mesh['zh'=4,'zl'=2,'yh'=4,'core'=2,'yl'=2,'x'=4] {'core','yh','zh'}, dimensions={0} | all-to-all | bytes 32768 | tf_op jit(solution)/shard_map/all_to_all | solution.py:31
  83.8 3.3 %shard_map.54 = bf16[16,64,256]{2,1,0:T(8,128)(2,1)S(1)} custom-call(bf16[528,256]{1,0:T(8,128)(2,1)S(1)} %get-tuple-element.18.own, bf16[528,256]{1,0:T(8,128)(2,1)S(1)} %collective-permute-done.oth, s32[1,1024]{1,0:T(1,128)S(1)} %get-tuple-element.19.ids, bf16[1024,256]{1,0:T(8,128)(2,1)S(1)} %get-tuple-element.22.ncol_far, ...), custom_call_target="tpu_custom_call" | custom-call | flops 1073741824 | bytes 1048576 | tf_op jit(solution)/shard_map/pallas_call | solution.py:252
  87.2 11.6 %all_to_all.28 = bf16[16,64,256]{2,1,0:T(8,128)(2,1)S(1)} all-to-all(bf16[16,64,256]{2,1,0:T(8,128)(2,1)S(1)} %shard_map.54), channel_id=1, replica_groups=mesh['zh'=4,'zl'=2,'yh'=4,'core'=2,'yl'=2,'x'=4] {'zl','x','yl'}, dimensions={0} | all-to-all | bytes 1048576 | tf_op jit(solution)/shard_map/all_to_all | solution.py:31
  98.8 0.1 reduce_sum.12
  98.9 9.2 %all_to_all.29.got = bf16[8,64,256]{2,1,0:T(8,128)(2,1)S(1)} all-to-all(bf16[8,64,256]{2,1,0:T(8,128)(2,1)S(1)} %broadcast_in_dim.2), channel_id=1, replica_groups=mesh['zh'=4,'zl'=2,'yh'=4,'core'=2,'yl'=2,'x'=4] {'x','yl'}, dimensions={0} | all-to-all | bytes 524288 | tf_op jit(solution)/shard_map/all_to_all | solution.py:31
  108.1 0.9 finish.1
  (1 shorter events, 0.0 us)
Async XLA Ops:
  38.2 15.4 %collective-permute-start.1 = (bf16[16,64,256]{2,1,0:T(8,128)(2,1)S(1)}, bf16[16,64,256]{2,1,0:T(8,128)(2,1)S(1)}, u32[]{:S(2)}, u32[]{:S(2)}) collective-permute-start(bf16[16,64,256]{2,1,0:T(8,128)(2,1)S(1)} %all_to_all.25.far), channel_id=1, source_target_pairs={{0,8},{8,0},{1,9},{9,1},{2,10},{10,2},{3,11},{11,3},{4,12},{12,4},... | collective-permute-start | bytes 1572872 | tf_op jit(solution)/shard_map/ppermute | solution.py:27
  41.9 9.9 %collective-permute-start = (bf16[528,256]{1,0:T(8,128)(2,1)S(1)}, bf16[528,256]{1,0:T(8,128)(2,1)S(1)}, u32[]{:S(2)}, u32[]{:S(2)}) collective-permute-start(bf16[528,256]{1,0:T(8,128)(2,1)S(1)} %get-tuple-element.18.own), channel_id=1, source_target_pairs={{0,64},{64,0},{1,65},{65,1},{2,66},{66,2},{3,67},{67,3},{4,68},{68... | collective-permute-start | bytes 811016 | tf_op jit(solution)/shard_map/ppermute | solution.py:27

commit v10 on v8

--- a/solution.py
+++ b/solution.py
@@ -52,6 +52,22 @@
         return base, None
     mine = jnp.logical_and(yh == its_yh, zh == its_zh)
     return base, jnp.where(mine, slot * piece, -(1 << 20))
+
+
+def triple(x):
+    high = x.astype(jnp.bfloat16).astype(jnp.float32)
+    rest = x - high
+    middle = rest.astype(jnp.bfloat16).astype(jnp.float32)
+    return high, middle, rest - middle
+
+
+def row_weights(refs, rows):
+    parts = []
+    for ref in refs:
+        tail = ref[pl.ds(rows, 16), :].astype(jnp.float32)
+        pair = tail[4:6] + tail[6:8] + tail[8:10]
+        parts += [pair[n : n + 1] for n in range(pair.shape[0])]
+    return jnp.concatenate(parts, axis=1)
 
 
 def partner_ids(own_ref, oth_ref, rows):
@@ -76,12 +92,15 @@
     ids = mates[...]
     half_row = rows // 2
     parts = [x[:, n * half_row : (n + 1) * half_row] for x in (ids >> 8, ids & 255) for n in (0, 1)]
-    blank = jnp.zeros((own.shape[0] - rows - 4, half_row), jnp.int32)
-    packed = jnp.concatenate(parts + [blank], axis=0).astype(jnp.float32)
+    parts = [x.astype(jnp.float32) for x in parts]
+    last.wait()
+    for x in triple(heft[...]):
+        parts += [x[:, n * half_row : (n + 1) * half_row] for n in (0, 1)]
+    parts.append(jnp.zeros((own.shape[0] - rows - len(parts), half_row), jnp.float32))
+    packed = jnp.concatenate(parts, axis=0)
     own[pl.ds(rows, own.shape[0] - rows), :] = packed.astype(jnp.bfloat16)
     slot = lax.axis_index(MP)
     copy.wait()
-    last.wait()
     mine = own[pl.ds(pl.multiple_of(slot * piece, piece), piece), :]
     for n in range(spread.shape[0]):
         spread[n] = mine
@@ -132,7 +151,7 @@
     sums[1] = positive
 
 
-def near_kernel(sizes, own, oth, near, weight, sums, nrow, msg, ncol, e_out, s_buf):
+def near_kernel(sizes, own, oth, near, sums, nrow, msg, ncol, e_out, s_buf):
     rows = nrow.shape[0] // 2
     at = place()
     ids = partner_ids(own, oth, rows)
@@ -142,37 +161,24 @@
     total = jnp.sum(total, axis=0, keepdims=True)
     positive = jnp.sum(positive, axis=0, keepdims=True) * INV_TAU
     zl = at[1]
-    same = [total[:, :rows], total[:, rows:], positive[:, :rows], weight[...]]
-    turned = [total[:, rows:], total[:, :rows], positive[:, rows:], weight[...]]
-    half_row = rows // 2
-
-    def stacked(parts):
-        return jnp.concatenate(
-            [p[:, n * half_row : (n + 1) * half_row] for p in parts for n in range(2)], axis=0
-        )
-
-    same, turned = stacked(same), stacked(turned)
+    same = jnp.concatenate([total[:, :rows], total[:, rows:], positive[:, :rows]], axis=1)
+    turned = jnp.concatenate([total[:, rows:], total[:, :rows], positive[:, rows:]], axis=1)
     members = sizes["mp"]
     for n in range(members):
         msg[zl * members + n] = same
         msg[(1 - zl) * members + n] = turned
 
 
-def totals_kernel(sizes, got, weight, info, loss, cw):
-    _, zl, _, _, slot = place()
+def totals_kernel(sizes, oth, got, weight, info, loss, cw):
+    slot = place()[4]
     members = sizes["mp"]
     summed = got[0]
     for n in range(1, got.shape[0]):
         summed = summed + got[n]
-    other_weight = got[(1 - zl) * members, 6:8, :]
-
-    def joined(pair):
-        return jnp.concatenate([pair[0:1], pair[1:2]], axis=1)
-
-    total, total_other = joined(summed[0:2]), joined(summed[2:4])
-    positive = joined(summed[4:6])
-    other_weight = joined(other_weight)
-    own_weight = weight[...]
+    rows = weight.shape[1]
+    total, total_other = summed[:, :rows], summed[:, rows : 2 * rows]
+    positive = summed[:, 2 * rows :]
+    own_weight, other_weight = weight[...], row_weights((oth,), rows)
     share = own_weight / total
     share_other = other_weight / total_other
     loss[...] = jnp.log(total) - positive
@@ -303,8 +309,8 @@
     )
     msg, ncol_near, e_near = call(
         functools.partial(near_kernel, sizes),
-        [((team, 8, rows // 2), f32), ((half, width), bf16), ((half, both), f32)],
-        (own, oth, near, heft, sums, nrow),
+        [((team, 1, 3 * rows), f32), ((half, width), bf16), ((half, both), f32)],
+        (own, oth, near, sums, nrow),
         [score],
         16,
         flops,
@@ -313,7 +319,7 @@
     info, loss, cw = call(
         functools.partial(totals_kernel, sizes),
         [((4, rows), f32), ((1, rows), f32), ((2 * chunks, 1, 2 * piece), f32)],
-        (got, heft),
+        (oth, got, heft),
     )
     cw = exchange(cw, OWNERS)
     (grads,) = call(

time: 110 us -> 110 us (level)
  no operation moved by 1% of the time
where the time goes in v10:
time: 110 us; the launch traced here: 109 us
  blocking collectives  86 us (78%)
  Pallas kernels  8.39 us (8%)
  waiting for transfers between devices  7.56 us (7%)
  starting transfers between devices  6.02 us (5%)
    all_to_all x5, blocking collectives, exchange(): return lax.all_to_all(x, axes, 0, 0, tiled=True)  86 us
    ppermute x2, waiting for transfers between devices, swap(): return lax.ppermute(x, axis, [(0, 1), (1, 0)])  7.56 us
    pallas_call x4, Pallas kernels, call(): pl.pallas_call(kernel, in_specs=[vmem] * len(args), out_specs=[vmem] * le...  6.48 us
    ppermute x2, starting transfers between devices, swap(): return lax.ppermute(x, axis, [(0, 1), (1, 0)])  6.02 us
  transfers between devices with their start and end apart: 2, of which 1 were waited for; matrix products, arithmetic and copies ran while one was open for 0% of the time, Pallas kernels for 2%

profile of v10, /device:TPU:1, one launch (start us, length us, event | category | flops | bytes accessed | tf_op | source)
XLA Modules:
  0.0 108.8 jit_solution(9048115869738687450)
XLA Ops:
  0.6 1.0 pack.1
  1.7 36.5 %all_to_all.25.far = bf16[16,64,256]{2,1,0:T(8,128)(2,1)S(1)} all-to-all(bf16[16,64,256]{2,1,0:T(8,128)(2,1)S(1)} %get-tuple-element.18), channel_id=1, replica_groups=mesh['zh'=4,'zl'=2,'yh'=4,'core'=2,'yl'=2,'x'=4] {'yh','zh'}, dimensions={0} | all-to-all | bytes 1048576 | tf_op jit(solution)/shard_map/all_to_all | solution.py:31
  38.2 3.7 %collective-permute-start.1 = (bf16[16,64,256]{2,1,0:T(8,128)(2,1)S(1)}, bf16[16,64,256]{2,1,0:T(8,128)(2,1)S(1)}, u32[]{:S(2)}, u32[]{:S(2)}) collective-permute-start(bf16[16,64,256]{2,1,0:T(8,128)(2,1)S(1)} %all_to_all.25.far), channel_id=1, source_target_pairs={{0,8},{8,0},{1,9},{9,1},{2,10},{10,2},{3,11},{11,3},{4,12},{12,4},... | collective-permute-start | bytes 1572872 | tf_op jit(solution)/shard_map/ppermute | solution.py:27
  41.9 2.4 %collective-permute-start = (bf16[528,256]{1,0:T(8,128)(2,1)S(1)}, bf16[528,256]{1,0:T(8,128)(2,1)S(1)}, u32[]{:S(2)}, u32[]{:S(2)}) collective-permute-start(bf16[528,256]{1,0:T(8,128)(2,1)S(1)} %get-tuple-element.17.own), channel_id=1, source_target_pairs={{0,64},{64,0},{1,65},{65,1},{2,66},{66,2},{3,67},{67,3},{4,68},{68... | collective-permute-start | bytes 811016 | tf_op jit(solution)/shard_map/ppermute | solution.py:27
  44.2 7.6 %collective-permute-done.oth = bf16[528,256]{1,0:T(8,128)(2,1)S(1)} collective-permute-done((bf16[528,256]{1,0:T(8,128)(2,1)S(1)}, bf16[528,256]{1,0:T(8,128)(2,1)S(1)}, u32[]{:S(2)}, u32[]{:S(2)}) %collective-permute-start) | collective-permute-done | bytes 270368 | tf_op jit(solution)/shard_map/ppermute | solution.py:27
  51.8 1.8 %shard_map.50 = (f32[2,8,1024]{2,1,0:T(8,128)S(1)}, bf16[1024,256]{1,0:T(8,128)(2,1)S(1)}, bf16[1024,256]{1,0:T(8,128)(2,1)S(1)}, f32[1024,1024]{1,0:T(8,128)S(1)}) custom-call(bf16[528,256]{1,0:T(8,128)(2,1)S(1)} %get-tuple-element.17.own, bf16[528,256]{1,0:T(8,128)(2,1)S(1)} %collective-permute-done.oth, bf16[16,64,256]{2,1,0:T(8,128)(2,1)S(1)} %all_to_all.25.far), custom_call_target="tpu_custom_call" | custom-call | flops 536870912 | bytes 1048576 | tf_op jit(solution)/shard_map/pallas_call | solution.py:257
  53.6 0.0 collective-permute-done.1.near
  53.6 1.4 %shard_map.51 = (f32[16,1,1536]{2,1,0:T(1,128)S(1)}, bf16[1024,256]{1,0:T(8,128)(2,1)S(1)}, f32[1024,1024]{1,0:T(8,128)S(1)}) custom-call(bf16[528,256]{1,0:T(8,128)(2,1)S(1)} %get-tuple-element.17.own, bf16[528,256]{1,0:T(8,128)(2,1)S(1)} %collective-permute-done.oth, bf16[16,64,256]{2,1,0:T(8,128)(2,1)S(1)} %collective-permute-done.1.near, ...), custom_call_target="tpu_custom_call" | custom-call | flops 536870912 | bytes 1048576 | tf_op jit(solution)/shard_map/pallas_call | solution.py:257
  55.0 10.0 %all_to_all.26.got = f32[16,1,1536]{2,1,0:T(1,128)S(1)} all-to-all(f32[16,1,1536]{2,1,0:T(1,128)S(1)} %get-tuple-element.25), channel_id=1, replica_groups=mesh['zh'=4,'zl'=2,'yh'=4,'core'=2,'yl'=2,'x'=4] {'zl','x','yl'}, dimensions={0} | all-to-all | bytes 196608 | tf_op jit(solution)/shard_map/all_to_all | solution.py:31
  65.0 0.1 shard_map.52
  65.1 18.6 %all_to_all.27.cw = f32[32,1,128]{2,1,0:T(1,128)S(1)} all-to-all(f32[32,1,128]{2,1,0:T(1,128)S(1)} %get-tuple-element.28), channel_id=1, replica_groups=mesh['zh'=4,'zl'=2,'yh'=4,'core'=2,'yl'=2,'x'=4] {'core','yh','zh'}, dimensions={0} | all-to-all | bytes 32768 | tf_op jit(solution)/shard_map/all_to_all | solution.py:31
  83.8 3.2 %shard_map.53 = bf16[16,64,256]{2,1,0:T(8,128)(2,1)S(1)} custom-call(bf16[528,256]{1,0:T(8,128)(2,1)S(1)} %get-tuple-element.17.own, bf16[528,256]{1,0:T(8,128)(2,1)S(1)} %collective-permute-done.oth, bf16[1024,256]{1,0:T(8,128)(2,1)S(1)} %get-tuple-element.19.ncol_far, bf16[1024,256]{1,0:T(8,128)(2,1)S(1)} %get-tuple-element.22.ncol_near, ...), custom_call_target="tpu_custom_call" | custom-call | flops 1073741824 | bytes 1048576 | tf_op jit(solution)/shard_map/pallas_call | solution.py:257
  87.0 11.7 %all_to_all.28 = bf16[16,64,256]{2,1,0:T(8,128)(2,1)S(1)} all-to-all(bf16[16,64,256]{2,1,0:T(8,128)(2,1)S(1)} %shard_map.53), channel_id=1, replica_groups=mesh['zh'=4,'zl'=2,'yh'=4,'core'=2,'yl'=2,'x'=4] {'zl','x','yl'}, dimensions={0} | all-to-all | bytes 1048576 | tf_op jit(solution)/shard_map/all_to_all | solution.py:31
  98.7 0.1 reduce_sum.12
  98.8 9.1 %all_to_all.29.got = bf16[8,64,256]{2,1,0:T(8,128)(2,1)S(1)} all-to-all(bf16[8,64,256]{2,1,0:T(8,128)(2,1)S(1)} %broadcast_in_dim.2), channel_id=1, replica_groups=mesh['zh'=4,'zl'=2,'yh'=4,'core'=2,'yl'=2,'x'=4] {'x','yl'}, dimensions={0} | all-to-all | bytes 524288 | tf_op jit(solution)/shard_map/all_to_all | solution.py:31
  107.9 0.9 finish.1
  (1 shorter events, 0.0 us)
Async XLA Ops:
  38.2 15.4 %collective-permute-start.1 = (bf16[16,64,256]{2,1,0:T(8,128)(2,1)S(1)}, bf16[16,64,256]{2,1,0:T(8,128)(2,1)S(1)}, u32[]{:S(2)}, u32[]{:S(2)}) collective-permute-start(bf16[16,64,256]{2,1,0:T(8,128)(2,1)S(1)} %all_to_all.25.far), channel_id=1, source_target_pairs={{0,8},{8,0},{1,9},{9,1},{2,10},{10,2},{3,11},{11,3},{4,12},{12,4},... | collective-permute-start | bytes 1572872 | tf_op jit(solution)/shard_map/ppermute | solution.py:27
  41.9 9.9 %collective-permute-start = (bf16[528,256]{1,0:T(8,128)(2,1)S(1)}, bf16[528,256]{1,0:T(8,128)(2,1)S(1)}, u32[]{:S(2)}, u32[]{:S(2)}) collective-permute-start(bf16[528,256]{1,0:T(8,128)(2,1)S(1)} %get-tuple-element.17.own), channel_id=1, source_target_pairs={{0,64},{64,0},{1,65},{65,1},{2,66},{66,2},{3,67},{67,3},{4,68},{68... | collective-permute-start | bytes 811016 | tf_op jit(solution)/shard_map/ppermute | solution.py:27

commit v11 on v10

--- a/solution.py
+++ b/solution.py
@@ -239,6 +239,15 @@
         msg[pl.ds(to * members, members)] = out.astype(jnp.bfloat16).reshape(members, -1, width)
 
 
+def owner_kernel(got, out):
+    total = got[0].astype(jnp.float32)
+    for n in range(1, got.shape[0]):
+        total = total + got[n].astype(jnp.float32)
+    total = total.astype(jnp.bfloat16)
+    for n in range(out.shape[0]):
+        out[n] = total
+
+
 def finish_kernel(got, loss, out, loss_out, wide, stored):
     piece = got.shape[1]
     copies = [pltpu.make_async_copy(loss, loss_out, stored.at[got.shape[0]])]
@@ -331,8 +340,8 @@
         2 * flops,
     )
     shares = exchange(grads, TEAM)
-    share = jnp.sum(shares.astype(f32), axis=0).astype(bf16)
-    got = exchange(jnp.broadcast_to(share[None], (members, piece, width)), MP)
+    (share,) = call(owner_kernel, [((members, piece, width), bf16)], (shares,))
+    got = exchange(share, MP)
     grad, loss = pl.pallas_call(
         finish_kernel,
         name="finish",

time: 110 us -> 110 us (level)
    pallas_call x4 -> x5, Pallas kernels: 6.48 us -> 6.56 us  [call(): pl.pallas_call(kernel, in_specs=[vmem] * len(args), out_specs=[vmem] * le...]
where the time goes in v11:
time: 110 us; the launch traced here: 109 us
  blocking collectives  86 us (78%)
  Pallas kernels  8.46 us (8%)
  waiting for transfers between devices  7.56 us (7%)
  starting transfers between devices  6.02 us (5%)
    all_to_all x5, blocking collectives, exchange(): return lax.all_to_all(x, axes, 0, 0, tiled=True)  86 us
    ppermute x2, waiting for transfers between devices, swap(): return lax.ppermute(x, axis, [(0, 1), (1, 0)])  7.56 us
    pallas_call x5, Pallas kernels, call(): pl.pallas_call(kernel, in_specs=[vmem] * len(args), out_specs=[vmem] * le...  6.56 us
    ppermute x2, starting transfers between devices, swap(): return lax.ppermute(x, axis, [(0, 1), (1, 0)])  6.02 us
  transfers between devices with their start and end apart: 2, of which 1 were waited for; matrix products, arithmetic and copies ran while one was open for 0% of the time, Pallas kernels for 2%

profile of v11, /device:TPU:1, one launch (start us, length us, event | category | flops | bytes accessed | tf_op | source)
XLA Modules:
  0.0 108.8 jit_solution(12228820281315368582)
XLA Ops:
  0.6 1.0 pack.1
  1.7 36.5 %all_to_all.25.far = bf16[16,64,256]{2,1,0:T(8,128)(2,1)S(1)} all-to-all(bf16[16,64,256]{2,1,0:T(8,128)(2,1)S(1)} %get-tuple-element.18), channel_id=1, replica_groups=mesh['zh'=4,'zl'=2,'yh'=4,'core'=2,'yl'=2,'x'=4] {'yh','zh'}, dimensions={0} | all-to-all | bytes 1048576 | tf_op jit(solution)/shard_map/all_to_all | solution.py:31
  38.2 3.7 %collective-permute-start.1 = (bf16[16,64,256]{2,1,0:T(8,128)(2,1)S(1)}, bf16[16,64,256]{2,1,0:T(8,128)(2,1)S(1)}, u32[]{:S(2)}, u32[]{:S(2)}) collective-permute-start(bf16[16,64,256]{2,1,0:T(8,128)(2,1)S(1)} %all_to_all.25.far), channel_id=1, source_target_pairs={{0,8},{8,0},{1,9},{9,1},{2,10},{10,2},{3,11},{11,3},{4,12},{12,4},... | collective-permute-start | bytes 1572872 | tf_op jit(solution)/shard_map/ppermute | solution.py:27
  41.9 2.4 %collective-permute-start = (bf16[528,256]{1,0:T(8,128)(2,1)S(1)}, bf16[528,256]{1,0:T(8,128)(2,1)S(1)}, u32[]{:S(2)}, u32[]{:S(2)}) collective-permute-start(bf16[528,256]{1,0:T(8,128)(2,1)S(1)} %get-tuple-element.17.own), channel_id=1, source_target_pairs={{0,64},{64,0},{1,65},{65,1},{2,66},{66,2},{3,67},{67,3},{4,68},{68... | collective-permute-start | bytes 811016 | tf_op jit(solution)/shard_map/ppermute | solution.py:27
  44.2 7.6 %collective-permute-done.oth = bf16[528,256]{1,0:T(8,128)(2,1)S(1)} collective-permute-done((bf16[528,256]{1,0:T(8,128)(2,1)S(1)}, bf16[528,256]{1,0:T(8,128)(2,1)S(1)}, u32[]{:S(2)}, u32[]{:S(2)}) %collective-permute-start) | collective-permute-done | bytes 270368 | tf_op jit(solution)/shard_map/ppermute | solution.py:27
  51.8 1.8 %shard_map.50 = (f32[2,8,1024]{2,1,0:T(8,128)S(1)}, bf16[1024,256]{1,0:T(8,128)(2,1)S(1)}, bf16[1024,256]{1,0:T(8,128)(2,1)S(1)}, f32[1024,1024]{1,0:T(8,128)S(1)}) custom-call(bf16[528,256]{1,0:T(8,128)(2,1)S(1)} %get-tuple-element.17.own, bf16[528,256]{1,0:T(8,128)(2,1)S(1)} %collective-permute-done.oth, bf16[16,64,256]{2,1,0:T(8,128)(2,1)S(1)} %all_to_all.25.far), custom_call_target="tpu_custom_call" | custom-call | flops 536870912 | bytes 1048576 | tf_op jit(solution)/shard_map/pallas_call | solution.py:266
  53.6 0.0 collective-permute-done.1.near
  53.6 1.4 %shard_map.51 = (f32[16,1,1536]{2,1,0:T(1,128)S(1)}, bf16[1024,256]{1,0:T(8,128)(2,1)S(1)}, f32[1024,1024]{1,0:T(8,128)S(1)}) custom-call(bf16[528,256]{1,0:T(8,128)(2,1)S(1)} %get-tuple-element.17.own, bf16[528,256]{1,0:T(8,128)(2,1)S(1)} %collective-permute-done.oth, bf16[16,64,256]{2,1,0:T(8,128)(2,1)S(1)} %collective-permute-done.1.near, ...), custom_call_target="tpu_custom_call" | custom-call | flops 536870912 | bytes 1048576 | tf_op jit(solution)/shard_map/pallas_call | solution.py:266
  55.0 10.0 %all_to_all.26.got = f32[16,1,1536]{2,1,0:T(1,128)S(1)} all-to-all(f32[16,1,1536]{2,1,0:T(1,128)S(1)} %get-tuple-element.25), channel_id=1, replica_groups=mesh['zh'=4,'zl'=2,'yh'=4,'core'=2,'yl'=2,'x'=4] {'zl','x','yl'}, dimensions={0} | all-to-all | bytes 196608 | tf_op jit(solution)/shard_map/all_to_all | solution.py:31
  65.0 0.1 shard_map.52
  65.1 18.6 %all_to_all.27.cw = f32[32,1,128]{2,1,0:T(1,128)S(1)} all-to-all(f32[32,1,128]{2,1,0:T(1,128)S(1)} %get-tuple-element.28), channel_id=1, replica_groups=mesh['zh'=4,'zl'=2,'yh'=4,'core'=2,'yl'=2,'x'=4] {'core','yh','zh'}, dimensions={0} | all-to-all | bytes 32768 | tf_op jit(solution)/shard_map/all_to_all | solution.py:31
  83.8 3.2 %shard_map.53 = bf16[16,64,256]{2,1,0:T(8,128)(2,1)S(1)} custom-call(bf16[528,256]{1,0:T(8,128)(2,1)S(1)} %get-tuple-element.17.own, bf16[528,256]{1,0:T(8,128)(2,1)S(1)} %collective-permute-done.oth, bf16[1024,256]{1,0:T(8,128)(2,1)S(1)} %get-tuple-element.19.ncol_far, bf16[1024,256]{1,0:T(8,128)(2,1)S(1)} %get-tuple-element.22.ncol_near, ...), custom_call_target="tpu_custom_call" | custom-call | flops 1073741824 | bytes 1048576 | tf_op jit(solution)/shard_map/pallas_call | solution.py:266
  87.0 11.7 %all_to_all.28.got = bf16[16,64,256]{2,1,0:T(8,128)(2,1)S(1)} all-to-all(bf16[16,64,256]{2,1,0:T(8,128)(2,1)S(1)} %shard_map.53), channel_id=1, replica_groups=mesh['zh'=4,'zl'=2,'yh'=4,'core'=2,'yl'=2,'x'=4] {'zl','x','yl'}, dimensions={0} | all-to-all | bytes 1048576 | tf_op jit(solution)/shard_map/all_to_all | solution.py:31
  98.7 0.1 shard_map.54
  98.8 9.1 %all_to_all.29.got = bf16[8,64,256]{2,1,0:T(8,128)(2,1)S(1)} all-to-all(bf16[8,64,256]{2,1,0:T(8,128)(2,1)S(1)} %shard_map.54), channel_id=1, replica_groups=mesh['zh'=4,'zl'=2,'yh'=4,'core'=2,'yl'=2,'x'=4] {'x','yl'}, dimensions={0} | all-to-all | bytes 524288 | tf_op jit(solution)/shard_map/all_to_all | solution.py:31
  107.9 0.9 finish.1
Async XLA Ops:
  38.2 15.4 %collective-permute-start.1 = (bf16[16,64,256]{2,1,0:T(8,128)(2,1)S(1)}, bf16[16,64,256]{2,1,0:T(8,128)(2,1)S(1)}, u32[]{:S(2)}, u32[]{:S(2)}) collective-permute-start(bf16[16,64,256]{2,1,0:T(8,128)(2,1)S(1)} %all_to_all.25.far), channel_id=1, source_target_pairs={{0,8},{8,0},{1,9},{9,1},{2,10},{10,2},{3,11},{11,3},{4,12},{12,4},... | collective-permute-start | bytes 1572872 | tf_op jit(solution)/shard_map/ppermute | solution.py:27
  41.9 9.9 %collective-permute-start = (bf16[528,256]{1,0:T(8,128)(2,1)S(1)}, bf16[528,256]{1,0:T(8,128)(2,1)S(1)}, u32[]{:S(2)}, u32[]{:S(2)}) collective-permute-start(bf16[528,256]{1,0:T(8,128)(2,1)S(1)} %get-tuple-element.17.own), channel_id=1, source_target_pairs={{0,64},{64,0},{1,65},{65,1},{2,66},{66,2},{3,67},{67,3},{4,68},{68... | collective-permute-start | bytes 811016 | tf_op jit(solution)/shard_map/ppermute | solution.py:27
